TPU v7x, 32 devices: a whole 2x2x4 slice. The times are simulated.
32 devices in a mesh: dp: 8 (over y, x, core), vocab: 4 (over z).
Axes of the slice: x: 2, y: 2, z: 4, core: 2. Of those that a mesh axis runs over, the one named last changes fastest.
Arguments:
- student_hidden: bfloat16 [1024, 1536], P('dp'), may hold values from -16 to 16
- head_weight: bfloat16 [1536, 16384], P('dp', 'vocab'), may hold values from -1 to 1
- teacher_logprobs: float32 [1024, 20480], P('dp', 'vocab'), may hold values from -45 to 0, as said below
- align_index: int32 [128, 2], replicated, may hold values from 0 to 159, as said below
- align_tiles: bfloat16 [128, 2, 128, 128], P('vocab'), may hold values from 0 to 6.1
- grad_scale: float32 [1024], P('dp'), may hold values from 30 to 300
Outputs:
- hidden_grad: bfloat16 [1024, 1536], P('dp', 'vocab')
- head_grad: bfloat16 [1536, 16384], P('dp', 'vocab')
Inputs may be any that keep to these rules, and one draw needn't show every extreme that they name: `teacher_logprobs`: each row's exponentials sum to 1 over the 20480 teacher entries. `align_index`: teacher block j is held by vocab index j // 40. Of the 64 entries of the student blocks held by one vocab index, at most 32 name teacher blocks held by any one vocab index, and for every vocab index some vocab index holds exactly 32 of them.
All inputs are finite; a program needn't handle non-finite values.
Results may differ from a plain program's by a relative error of at most 0.015.
Values may be sent and summed in bfloat16 or wider, within the bound.
No kernel may reach another device: no remote copies, remote signals or barrier semaphores. Data moves between devices by JAX's collectives and lax.ppermute only.
A program may use at most 128 MiB of HBM per device.

v0:
```python
import functools

import jax
import jax.numpy as jnp
from jax import lax
from jax.experimental import pallas as pl
from jax.experimental.pallas import tpu as pltpu
from jax.sharding import PartitionSpec as P


BLOCK = 128
K = 2
CHUNKS = 2

ANY = pl.BlockSpec(memory_space=pl.ANY)
VMEM = pl.BlockSpec(memory_space=pltpu.VMEM)
F32 = jnp.float32
BF16 = jnp.bfloat16


def swap(x, axis, bits):
    return lax.ppermute(x, axis, [(i, i ^ bits) for i in range(lax.axis_size(axis))])


def probs_kernel(x_ref, *out_refs):
    rows = out_refs[0].shape[1]
    for j in range(out_refs[0].shape[0]):
        block = jnp.exp(x_ref[:, j * BLOCK : (j + 1) * BLOCK]).astype(BF16)
        for c, out in enumerate(out_refs):
            out[j] = block[c * rows : (c + 1) * rows]


def teacher_blocks(logprobs):
    tokens, cols = logprobs.shape
    count = cols // BLOCK
    step = next(s for s in (8, 5, 4, 2, 1) if count % s == 0)
    rows = tokens // CHUNKS
    return pl.pallas_call(
        probs_kernel,
        grid=(count // step,),
        in_specs=[pl.BlockSpec((tokens, step * BLOCK), lambda i: (0, i))],
        out_specs=[pl.BlockSpec((step, rows, BLOCK), lambda i: (i, 0, 0))] * CHUNKS,
        out_shape=[jax.ShapeDtypeStruct((count, rows, BLOCK), BF16)] * CHUNKS,
        name="probs",
    )(logprobs)


def pack_kernel(first, vocab, tab_ref, *refs):
    sources, out_ref, sems = refs[:-2], refs[-2], refs[-1]
    v = tab_ref[8, 0]
    capacity = out_ref.shape[0]
    row = jnp.where(v == 1, 0, 1)

    def visit(p, started):
        slot = tab_ref[2 + row, p] - first

        @pl.when((slot >= 0) & (slot < capacity))
        def _():
            if started:
                pltpu.make_async_copy(sources[0].at[0], out_ref.at[0], sems.at[p]).wait()
            else:
                for d, source in enumerate(sources):

                    @pl.when(tab_ref[4 + row, p] == d + 1)
                    def _(source=source):
                        pltpu.make_async_copy(
                            source.at[tab_ref[6 + row, p]], out_ref.at[slot], sems.at[p]
                        ).start()

    @pl.when((v == 1) | (v == vocab - 2))
    def _():
        for started in (False, True):
            lax.fori_loop(0, tab_ref.shape[1], lambda p, c: (visit(p, started), c)[1], 0)


def pack(tab, first, capacity, sources, vocab):
    return pl.pallas_call(
        functools.partial(pack_kernel, first, vocab),
        grid_spec=pltpu.PrefetchScalarGridSpec(
            num_scalar_prefetch=1,
            grid=(),
            in_specs=[ANY] * len(sources),
            out_specs=VMEM,
            scratch_shapes=[pltpu.SemaphoreType.DMA((tab.shape[1],))],
        ),
        out_shape=jax.ShapeDtypeStruct((capacity,) + sources[0].shape[1:], BF16),
        name="pack",
    )(tab, *sources)


def mapped_kernel(chips, tab_ref, *refs):
    sources, tiles_ref, outs, buf, sems = refs[: -chips - 3], refs[-chips - 3], refs[-chips - 2 : -2], refs[-2], refs[-1]
    me = tab_ref[8, 1]
    pairs = tab_ref.shape[1]
    per = outs[0].shape[1] // BLOCK

    def start(p, carry):
        for i, source in enumerate(sources):

            @pl.when(tab_ref[0, p] == i)
            def _(source=source):
                pltpu.make_async_copy(source.at[tab_ref[1, p]], buf.at[p], sems.at[p]).start()

        return carry

    def finish(p, carry):
        pltpu.make_async_copy(sources[0].at[0], buf.at[p], sems.at[p]).wait()
        return carry

    lax.fori_loop(0, pairs, start, 0)
    lax.fori_loop(0, pairs, finish, 0)
    for s, out in enumerate(outs):
        dest = lax.bitwise_xor(me, s)
        for j in range(per):
            b = dest * per + j
            total = jnp.dot(buf[K * b], tiles_ref[b, 0], preferred_element_type=F32)
            for k in range(1, K):
                total += jnp.dot(buf[K * b + k], tiles_ref[b, k], preferred_element_type=F32)
            out[:, j * BLOCK : (j + 1) * BLOCK] = total.astype(BF16)


def mapped_parts(tab, sources, tiles, chips):
    rows = sources[0].shape[1]
    cols = tiles.shape[0] * BLOCK // chips
    pairs = tab.shape[1]
    return pl.pallas_call(
        functools.partial(mapped_kernel, chips),
        grid_spec=pltpu.PrefetchScalarGridSpec(
            num_scalar_prefetch=1,
            grid=(),
            in_specs=[ANY] * len(sources) + [VMEM],
            out_specs=[VMEM] * chips,
            scratch_shapes=[pltpu.VMEM((pairs, rows, BLOCK), BF16), pltpu.SemaphoreType.DMA((pairs,))],
        ),
        out_shape=[jax.ShapeDtypeStruct((rows, cols), BF16)] * chips,
        name="mapped",
    )(tab, *sources, tiles)


def logits_kernel(core_ref, x_ref, own_ref, other_ref, e_ref, m_ref, s_ref):
    c = core_ref[0]
    logits = jnp.dot(x_ref[c], own_ref[...], preferred_element_type=F32)
    logits += jnp.dot(x_ref[1 - c], other_ref[...], preferred_element_type=F32)
    top = jnp.max(logits, axis=1, keepdims=True)
    e = jnp.exp(logits - top)
    e_ref[...] = e
    m_ref[...] = top
    s_ref[...] = jnp.sum(e, axis=1, keepdims=True)


def logits_parts(core, hidden, own, other, tokens):
    rows = hidden.shape[1]
    features, cols = own.shape
    spec = lambda n: pl.BlockSpec((tokens, n), lambda i, core: (i, 0))
    shape = lambda n: jax.ShapeDtypeStruct((rows, n), F32)
    fixed = pl.BlockSpec((features, cols), lambda i, core: (0, 0))
    return pl.pallas_call(
        logits_kernel,
        grid_spec=pltpu.PrefetchScalarGridSpec(
            num_scalar_prefetch=1,
            grid=(rows // tokens,),
            in_specs=[pl.BlockSpec((2, tokens, features), lambda i, core: (0, i, 0)), fixed, fixed],
            out_specs=[spec(cols), spec(1), spec(1)],
        ),
        out_shape=[shape(cols), shape(1), shape(1)],
        name="logits",
    )(core, hidden, own, other)


def stats_kernel(top_ref, *refs):
    shares, out_ref = refs[:-1], refs[-1]
    chips = len(shares)
    for k in range(chips):
        rows = [k ^ r for r in range(chips)]
        tops = [shares[r][j : j + 1] for r, j in enumerate(rows)]
        top = functools.reduce(jnp.maximum, tops)
        total = sum(shares[r][chips + j : chips + j + 1] * jnp.exp(tops[r] - top) for r, j in enumerate(rows))
        mass = shares[k][2 * chips : 2 * chips + 1]
        scale = shares[k][2 * chips + 1 : 2 * chips + 2]
        out_ref[0, k : k + 1] = scale * mass * (jnp.exp(top_ref[k : k + 1] - top) / total)
        out_ref[1, k : k + 1] = scale


def grads_kernel(chips, core_ref, e_ref, a_ref, b_ref, own_ref, other_ref, *refs):
    mapped, dl_ref, outs = refs[:chips], refs[-chips - 1], refs[-chips:]
    c = core_ref[0]
    for k in range(chips):
        dl = (a_ref[k] * e_ref[k] - b_ref[k] * mapped[k][...].astype(F32)).astype(BF16)
        dl_ref[k] = dl
        for half, weight in ((c, own_ref), (1 - c, other_ref)):
            terms = lax.dot_general(dl, weight[...], (((1,), (1,)), ((), ())), preferred_element_type=F32)
            outs[k][half] = terms.astype(BF16)


def grads(chunk, core, e, a, b, own, other, mapped, dl):
    chips, rows = len(mapped), mapped[0].shape[0]
    features, cols = own.shape
    part = lambda n: pl.BlockSpec((chips, rows, n), lambda i, core: (0, chunk, 0))
    whole = lambda *shape: pl.BlockSpec(shape, lambda i, core: (0,) * len(shape))
    return pl.pallas_call(
        functools.partial(grads_kernel, chips),
        grid_spec=pltpu.PrefetchScalarGridSpec(
            num_scalar_prefetch=1,
            grid=(1,),
            in_specs=[part(cols), part(1), part(1), whole(features, cols), whole(features, cols)]
            + [whole(rows, cols)] * chips
            + ([] if dl is None else [ANY]),
            out_specs=[part(cols)] + [whole(2, rows, features)] * chips,
        ),
        out_shape=[jax.ShapeDtypeStruct(e.shape, BF16)]
        + [jax.ShapeDtypeStruct((2, rows, features), BF16)] * chips,
        input_output_aliases={} if dl is None else {6 + chips: 0},
        name="grads",
    )(core, e, a, b, own, other, *mapped, *([] if dl is None else [dl]))


def body(student_hidden, head_weight, teacher_logprobs, align_index, align_tiles, grad_scale):
    vocab = lax.axis_size("vocab")
    dp = lax.axis_size("dp")
    v = lax.axis_index("vocab")
    d = lax.axis_index("dp")
    chips, chip, c = dp // 2, d // 2, d % 2
    core = c.astype(jnp.int32)[None]
    tokens, features = student_hidden.shape
    count = teacher_logprobs.shape[1] // BLOCK
    pairs = align_tiles.shape[0] * K
    capacity = (2 * pairs + vocab - 1) // vocab
    packs = (pairs + capacity - 1) // capacity
    if vocab < 4 or vocab & (vocab - 1) or dp & (dp - 1):
        raise ValueError("mesh sizes")
    groups = [[2 * i + j for i in range(chips)] for j in range(2)]

    blocks = teacher_blocks(teacher_logprobs)

    hops = [(r, i) for r in range(1, vocab - 1) for i in range(r - 1, vocab - 2)]
    number_of = [[0] * vocab for _ in range(vocab)]
    for i in range(1, vocab - 1):
        for o in range(vocab):
            if o != i:
                link = i - 1 if o < i else vocab - 2 - i
                number_of[i][o] = 1 + hops.index((abs(o - i), link))

    rows = align_index.reshape(vocab, pairs)
    ends = jnp.stack([rows[0], rows[vocab - 1]])
    end_owner, end_local = lax.div(ends, jnp.int32(count)), lax.rem(ends, jnp.int32(count))
    end_far = jnp.abs(end_owner - jnp.array([[0], [vocab - 1]]))
    number = jnp.arange(pairs)
    later = (end_far[:, None, :] > end_far[:, :, None]) | (
        (end_far[:, None, :] == end_far[:, :, None]) & (number[None, None, :] >= number[None, :, None])
    )
    end_slot = packs * capacity - jnp.sum((later & (end_far[:, None, :] > 0)).astype(jnp.int32), axis=2)
    end_slot = jnp.where(end_far > 0, end_slot, -1)
    own = lax.dynamic_index_in_dim(rows, v, 0, keepdims=False)
    own_owner, own_local = lax.div(own, jnp.int32(count)), lax.rem(own, jnp.int32(count))
    own_slot = jnp.where(v == 0, end_slot[0], end_slot[1])
    at_end = ((v == 0) | (v == vocab - 1)) & (own_owner != v)
    numbers = lax.dynamic_index_in_dim(jnp.array(number_of, jnp.int32), v, 0, keepdims=False)
    source = jnp.sum(
        jnp.where(own_owner[None, :] == jnp.arange(vocab)[:, None], numbers[:, None], 0), axis=0
    )
    source = jnp.where(at_end, 1 + len(hops) + lax.div(own_slot, jnp.int32(capacity)), source)
    place = jnp.where(at_end, lax.rem(own_slot, jnp.int32(capacity)), own_local)
    me = jnp.where(number == 0, v, chip)
    tab = jnp.concatenate(
        [source[None], place[None], end_slot, end_far, end_local, me[None]], axis=0
    ).astype(jnp.int32)

    def exchange(own_blocks):
        moved = {(0, i): own_blocks for i in range(-1, vocab)}
        for r, i in hops:
            moved[r, i] = lax.ppermute(
                moved[r - 1, i - 1], "vocab", [(i, i + 1), (vocab - 1 - i, vocab - 2 - i)]
            )
        near = [own_blocks] + [moved[r, vocab - 3] for r in range(1, vocab - 1)]
        packed = []
        for q in range(packs):
            part = pack(tab, q * capacity, capacity, near[: q - packs + vocab], vocab)
            packed.append(lax.ppermute(part, "vocab", [(vocab - 2, vocab - 1), (1, 0)]))
        return [own_blocks] + [moved[hop] for hop in hops] + packed

    sources = [exchange(part) for part in blocks]

    weight_own = lax.all_to_all(head_weight, "dp", split_axis=1, concat_axis=0, axis_index_groups=groups, tiled=True)
    weight_other = swap(weight_own, "dp", 1)

    hidden = student_hidden.reshape(tokens, chips, 2, features // dp).transpose(2, 0, 1, 3)
    hidden = hidden.reshape(2, tokens, features // 2)
    others = [swap(hidden, "dp", 2 * j) for j in range(1, chips)]
    hidden = jnp.concatenate([hidden] + others, axis=1)
    e, top, total = logits_parts(core, hidden, weight_own, weight_other, tokens)
    top, total = top.reshape(chips, tokens), total.reshape(chips, tokens)

    row_sums = jnp.sum(align_tiles.astype(F32), axis=3).reshape(pairs, BLOCK)
    all_sums = [row_sums] + [swap(row_sums, "vocab", t) for t in range(1, vocab)]
    all_rows = [own] + [lax.dynamic_index_in_dim(rows, v ^ t, 0, keepdims=False) for t in range(1, vocab)]
    hits = (jnp.concatenate(all_rows)[None, :] == (v * count + jnp.arange(count))[:, None]).astype(F32)
    entry_weight = jnp.dot(hits, jnp.concatenate(all_sums), precision=lax.Precision.HIGHEST)
    mass = jnp.concatenate(
        [jnp.sum(part.astype(F32) * entry_weight[:, None, :], axis=(0, 2)) for part in blocks]
    )

    share = jnp.concatenate([top, total, mass[None]])
    shares = [share] + [swap(share, "vocab", t) for t in range(1, vocab)]
    plane_top = functools.reduce(jnp.maximum, [s[:chips] for s in shares])
    plane_total = sum(s[chips : 2 * chips] * jnp.exp(s[:chips] - plane_top) for s in shares)
    plane_mass = sum(s[2 * chips] for s in shares)
    share = jnp.concatenate([plane_top, plane_total, plane_mass[None], grad_scale[None]])
    shares = [share] + [swap(share, "dp", 2 * j) for j in range(1, chips)]
    coefs = pl.pallas_call(
        stats_kernel,
        in_specs=[VMEM] * (chips + 1),
        out_specs=VMEM,
        out_shape=jax.ShapeDtypeStruct((2, chips, tokens), F32),
        name="stats",
    )(top, *shares)
    a, b = coefs[0][..., None], coefs[1][..., None]
    e = e.reshape(chips, tokens, -1)

    dl, hidden_parts = None, []
    for n in range(CHUNKS):
        parts = mapped_parts(tab, sources[n], align_tiles, chips)
        parts = [parts[0]] + [swap(parts[j], "dp", 2 * j) for j in range(1, chips)]
        dl, *terms = grads(n, core, e, a, b, weight_own, weight_other, parts, dl)
        others = [swap(terms[j], "dp", 2 * j) for j in range(1, chips)]
        rows_sum = sum([x.astype(F32) for x in others], terms[0].astype(F32))
        rows_sum = rows_sum.astype(BF16).reshape(2, -1, chips, features // dp).transpose(1, 2, 0, 3)
        pieces = rows_sum.reshape(-1, vocab, features // vocab).transpose(1, 0, 2)
        piece = lambda t: lax.dynamic_index_in_dim(pieces, v ^ t, 0, keepdims=False)
        part = piece(0).astype(F32)
        for t in range(1, vocab):
            part += swap(piece(t), "vocab", t).astype(F32)
        hidden_parts.append(part.astype(BF16))
    hidden_grad = jnp.concatenate(hidden_parts)
    dl = dl.reshape(chips * tokens, -1)

    def head_half(half):
        x = lax.dynamic_index_in_dim(hidden, half, 0, keepdims=False)
        return lax.dot_general(x, dl, (((0,), (0,)), ((), ())), preferred_element_type=F32).astype(BF16)

    half = head_half(1 - c)
    got = swap(half, "dp", 1)
    head_terms = (head_half(c).astype(F32) + got.astype(F32)).astype(BF16)
    head_grad = lax.all_to_all(
        head_terms, "dp", split_axis=0, concat_axis=1, axis_index_groups=groups, tiled=True
    )
    return (hidden_grad, head_grad)


def solution(mesh):
    placed = (
        P("dp", None),
        P("dp", "vocab"),
        P("dp", "vocab"),
        P(),
        P("vocab", None, None, None),
        P("dp"),
    )
    return jax.shard_map(
        body,
        mesh=mesh,
        in_specs=placed,
        out_specs=(P("dp", "vocab"), P("dp", "vocab")),
        check_vma=False,
    )
```

profile of v0, /device:TPU:0, one launch (start us, length us, event | category | flops | bytes accessed | tf_op | source)
XLA Modules:
  0.0 212.2 jit_solution(9081513879136753822)
XLA Ops:
  0.6 2.7 %copy.56 = bf16[24,4,8,1024]{3,2,0,1:T(8,128)(2,1)} copy(bf16[24,4,8,1024]{3,2,1,0:T(8,128)(2,1)} %bitcast.86) | data formatting | bytes 3145728 | tf_op jit(solution)/shard_map/all_to_all | solution.py:283
  3.3 5.2 %all-to-all-start = ((bf16[192,4,1024]{2,0,1:T(8,128)(2,1)}), bf16[192,4,1024]{2,0,1:T(8,128)(2,1)S(1)}, u32[]{:S(2)}, u32[]{:S(2)}) async-start(bf16[192,4,1024]{2,0,1:T(8,128)(2,1)} %bitcast.78), calls=%async_computation | async-start | bytes 3145728 | tf_op jit(solution)/shard_map/all_to_all | solution.py:283
  8.5 2.8 %convert_reduce_fusion = f32[32,2,128]{2,1,0:T(2,128)} fusion(bf16[32,2,128,128]{3,2,1,0:T(8,128)(2,1)} %refs_6_.3), kind=kLoop, calls=%fused_computation | loop fusion | flops 2088960 | bytes 2129920 | tf_op jit(solution)/shard_map/reduce_sum | solution.py:293
  11.4 3.6 %collective-permute-start.6 = (f32[64,128]{1,0:T(8,128)}, f32[64,128]{1,0:T(8,128)S(1)}, u32[]{:S(2)}, u32[]{:S(2)}) collective-permute-start(f32[64,128]{1,0:T(8,128)} %bitcast.12), channel_id=1, source_target_pairs={{0,3},{1,2},{2,1},{3,0},{4,7},{5,6},{6,5},{7,4},{8,11},{9,10},{10,... | collective-permute-start | bytes 98312 | tf_op jit(solution)/shard_map/ppermute | solution.py:22
  15.0 4.4 %probs.1 = (bf16[40,64,128]{2,1,0:T(8,128)(2,1)}, bf16[40,64,128]{2,1,0:T(8,128)(2,1)}) custom-call(f32[128,5120]{1,0:T(8,128)} %x_ref.1), custom_call_target="tpu_custom_call" | custom-call | tf_op jit(solution)/shard_map/probs/pallas_call | solution.py:38
  19.4 1.6 collective-permute-start.14
  21.0 6.6 %collective-permute-start.13 = (bf16[40,64,128]{2,1,0:T(8,128)(2,1)}, bf16[40,64,128]{2,1,0:T(8,128)(2,1)}, u32[]{:S(2)}, u32[]{:S(2)}) collective-permute-start(bf16[40,64,128]{2,1,0:T(8,128)(2,1)} %get-tuple-element.28.refs_0_), channel_id=1, source_target_pairs={{0,1},{3,2},{4,5},{7,6},{8,9},{11,10},{12,13},{15,14},{16,17},{19,... | collective-permute-start | bytes 1966088 | tf_op jit(solution)/shard_map/ppermute | solution.py:271
  30.2 1.2 copy.36
  32.2 1.2 copy.41
  33.4 2.9 %collective-permute-start.2 = (bf16[2,128,768]{2,1,0:T(8,128)(2,1)S(1)}, bf16[2,128,768]{2,1,0:T(8,128)(2,1)}, u32[]{:S(2)}, u32[]{:S(2)}) collective-permute-start(bf16[2,128,768]{2,1,0:T(8,128)(2,1)S(1)} %copy.41), channel_id=1, source_target_pairs={{0,24},{4,28},{8,16},{12,20},{16,8},{20,12},{24,0},{28,4},{1,25},{... | collective-permute-start | bytes 1179656 | tf_op jit(solution)/shard_map/ppermute | solution.py:22
  36.3 4.4 %collective-permute-done.4 = f32[64,128]{1,0:T(8,128)} collective-permute-done((f32[64,128]{1,0:T(8,128)}, f32[64,128]{1,0:T(8,128)}, u32[]{:S(2)}, u32[]{:S(2)}) %collective-permute-start.4) | collective-permute-done | bytes 32800 | tf_op jit(solution)/shard_map/ppermute | solution.py:22
  40.7 5.2 %collective-permute-start.27 = (bf16[40,64,128]{2,1,0:T(8,128)(2,1)}, bf16[40,64,128]{2,1,0:T(8,128)(2,1)}, u32[]{:S(2)}, u32[]{:S(2)}) collective-permute-start(bf16[40,64,128]{2,1,0:T(8,128)(2,1)} %get-tuple-element.29.refs_0_), channel_id=1, source_target_pairs={{0,1},{3,2},{4,5},{7,6},{8,9},{11,10},{12,13},{15,14},{16,17},{19,... | collective-permute-start | bytes 1966088 | tf_op jit(solution)/shard_map/ppermute | solution.py:271
  45.9 1.5 collective-permute-start.15
  47.5 1.2 fusion.30
  49.4 1.1 compare_select_fusion
  50.5 1.7 collective-permute-start.1
  52.2 1.5 collective-permute-start
  54.2 2.4 %concatenate.51.tab_ref = s32[9,64]{1,0:T(8,128)} concatenate(s32[1,64]{1,0:T(1,128)} %get-tuple-element.71, s32[1,64]{1,0:T(1,128)S(1)} %get-tuple-element.50, s32[2,64]{1,0:T(2,128)S(1)} %subtract_select_fusion, s32[2,64]{1,0:T(2,128)S(1)} %get-tuple-element.53, s32[2,64]{1,0:T(2,128)S(1)} %broadcast_remainder_fusion, s32[1,64]{1,0:T(1,128)} %get-tuple-element.70), dimensions={0} | concatenate | bytes 4608 | tf_op jit(solution)/shard_map/concatenate | solution.py:264
  57.5 1.5 collective-permute-start.28
  59.0 1.5 collective-permute-start.29
  60.6 1.6 fusion.4
  62.2 2.2 %pack.4 = bf16[32,64,128]{2,1,0:T(8,128)(2,1)} custom-call(s32[9,64]{1,0:T(8,128)} %concatenate.51.tab_ref, bf16[40,64,128]{2,1,0:T(8,128)(2,1)} %get-tuple-element.28.refs_0_, bf16[40,64,128]{2,1,0:T(8,128)(2,1)} %collective-permute-done.14.refs_1_.refs_2_), custom_call_target="tpu_custom_call" | custom-call | tf_op jit(solution)/shard_map/pack/pallas_call | solution.py:77
  64.4 2.2 %pack.5 = bf16[32,64,128]{2,1,0:T(8,128)(2,1)} custom-call(s32[9,64]{1,0:T(8,128)} %concatenate.51.tab_ref, bf16[40,64,128]{2,1,0:T(8,128)(2,1)} %get-tuple-element.28.refs_0_, bf16[40,64,128]{2,1,0:T(8,128)(2,1)} %collective-permute-done.14.refs_1_.refs_2_, bf16[40,64,128]{2,1,0:T(8,128)(2,1)} %collective-permute-done.15.refs_2_.refs_3_), custom_call_target="tpu_custom_call" | custom-call | tf_op jit(solution)/shard_map/pack/pallas_call | solution.py:77
  66.6 1.3 collective-permute-start.16
  68.0 1.3 collective-permute-start.17
  69.2 1.7 multiply_reduce_fusion.1
  71.0 2.5 %pad_maximum_fusion.x_ref = bf16[2,512,768]{2,1,0:T(8,128)(2,1)} fusion(bf16[2,128,768]{2,1,0:T(8,128)(2,1)} %collective-permute-done.2, bf16[2,128,768]{2,1,0:T(8,128)(2,1)} %collective-permute-done.1, bf16[2,128,768]{2,1,0:T(8,128)(2,1)} %collective-permute-done, bf16[2,128,768]{2,1,0:T(8,128)(2,1)S(1)} %copy.41), kind=kLoop, calls=%fused_computation.5 | loop fusion | flops 6291456 | bytes 3145728 | tf_op jit(solution)/shard_map/concatenate | solution.py:289
  73.5 1.2 copy-done.1
  74.7 6.4 %logits.1 = (f32[512,1024]{1,0:T(8,128)}, f32[512,1]{1,0:T(8,128)}, f32[512,1]{1,0:T(8,128)}) custom-call(s32[1]{0:T(128)} %bitcast.core_ref, bf16[2,512,768]{2,1,0:T(8,128)(2,1)} %pad_maximum_fusion.x_ref, bf16[768,1024]{1,0:T(8,128)(2,1)} %bitcast.80, bf16[768,1024]{1,0:T(8,128)(2,1)} %copy-done.1), custom_call_target="tpu_custom_call" | custom-call | tf_op jit(solution)/shard_map/logits/pallas_call | solution.py:157
  83.2 1.5 collective-permute-start.9
  84.8 11.5 %collective-permute-start.8 = (f32[9,128]{1,0:T(8,128)S(1)}, f32[9,128]{1,0:T(8,128)S(1)}, u32[]{:S(2)}, u32[]{:S(2)}) collective-permute-start(f32[9,128]{1,0:T(8,128)S(1)} %pad_maximum_fusion.2), channel_id=1, source_target_pairs={{0,2},{1,3},{2,0},{3,1},{4,6},{5,7},{6,4},{7,5},{8,10},{9,11},{10,... | collective-permute-start | bytes 13832 | tf_op jit(solution)/shard_map/ppermute | solution.py:22
  96.3 2.2 %pack.6 = bf16[32,64,128]{2,1,0:T(8,128)(2,1)} custom-call(s32[9,64]{1,0:T(8,128)} %concatenate.51.tab_ref, bf16[40,64,128]{2,1,0:T(8,128)(2,1)} %get-tuple-element.29.refs_0_, bf16[40,64,128]{2,1,0:T(8,128)(2,1)} %collective-permute-done.28.refs_1_.refs_2_), custom_call_target="tpu_custom_call" | custom-call | tf_op jit(solution)/shard_map/pack/pallas_call | solution.py:77
  98.5 2.3 %pack.7 = bf16[32,64,128]{2,1,0:T(8,128)(2,1)} custom-call(s32[9,64]{1,0:T(8,128)} %concatenate.51.tab_ref, bf16[40,64,128]{2,1,0:T(8,128)(2,1)} %get-tuple-element.29.refs_0_, bf16[40,64,128]{2,1,0:T(8,128)(2,1)} %collective-permute-done.28.refs_1_.refs_2_, bf16[40,64,128]{2,1,0:T(8,128)(2,1)} %collective-permute-done.29.refs_2_.refs_3_), custom_call_target="tpu_custom_call" | custom-call | tf_op jit(solution)/shard_map/pack/pallas_call | solution.py:77
  100.8 1.3 collective-permute-start.30
  102.1 1.5 collective-permute-start.31
  103.6 6.1 %mapped.2 = (bf16[64,1024]{1,0:T(8,128)(2,1)}, bf16[64,1024]{1,0:T(8,128)(2,1)}, bf16[64,1024]{1,0:T(8,128)(2,1)}, bf16[64,1024]{1,0:T(8,128)(2,1)}) custom-call(s32[9,64]{1,0:T(8,128)} %concatenate.51.tab_ref, bf16[40,64,128]{2,1,0:T(8,128)(2,1)} %get-tuple-element.28.refs_0_, bf16[40,64,128]{2,1,0:T(8,128)(2,1)} %collective-permute-done.13.refs_1_, ...), custom_call_target="tpu_custom_call" | custom-call | tf_op jit(solution)/shard_map/mapped/pallas_call | solution.py:126
  109.7 1.4 collective-permute-start.18
  111.3 1.5 collective-permute-start.12
  113.5 8.1 %collective-permute-done.30.refs_4_ = bf16[32,64,128]{2,1,0:T(8,128)(2,1)S(1)} collective-permute-done((bf16[32,64,128]{2,1,0:T(8,128)(2,1)S(1)}, bf16[32,64,128]{2,1,0:T(8,128)(2,1)S(1)}, u32[]{:S(2)}, u32[]{:S(2)}) %collective-permute-start.30) | collective-permute-done | bytes 524320 | tf_op jit(solution)/shard_map/ppermute | solution.py:278
  121.5 1.4 collective-permute-start.10
  122.9 4.9 %collective-permute-done.31.refs_5_ = bf16[32,64,128]{2,1,0:T(8,128)(2,1)S(1)} collective-permute-done((bf16[32,64,128]{2,1,0:T(8,128)(2,1)}, bf16[32,64,128]{2,1,0:T(8,128)(2,1)S(1)}, u32[]{:S(2)}, u32[]{:S(2)}) %collective-permute-start.31) | collective-permute-done | bytes 524320 | tf_op jit(solution)/shard_map/ppermute | solution.py:278
  128.9 6.1 %mapped.3 = (bf16[64,1024]{1,0:T(8,128)(2,1)}, bf16[64,1024]{1,0:T(8,128)(2,1)}, bf16[64,1024]{1,0:T(8,128)(2,1)}, bf16[64,1024]{1,0:T(8,128)(2,1)}) custom-call(s32[9,64]{1,0:T(8,128)} %concatenate.51.tab_ref, bf16[40,64,128]{2,1,0:T(8,128)(2,1)} %get-tuple-element.29.refs_0_, bf16[40,64,128]{2,1,0:T(8,128)(2,1)} %collective-permute-done.27.refs_1_, ...), custom_call_target="tpu_custom_call" | custom-call | tf_op jit(solution)/shard_map/mapped/pallas_call | solution.py:126
  135.0 1.8 collective-permute-start.20
  138.6 1.4 stats.1
  140.0 1.7 collective-permute-start.34
  144.8 7.5 %grads.2 = (bf16[4,128,1024]{2,1,0:T(8,128)(2,1)}, bf16[2,64,768]{2,1,0:T(8,128)(2,1)}, bf16[2,64,768]{2,1,0:T(8,128)(2,1)}, bf16[2,64,768]{2,1,0:T(8,128)(2,1)}, bf16[2,64,768]{2,1,0:T(8,128)(2,1)}) custom-call(s32[1]{0:T(128)} %bitcast.core_ref, f32[4,128,1024]{2,1,0:T(8,128)} %bitcast.83, f32[4,128,1]{2,1,0:T(8,128)} %copy.46.a_ref, ...), custom_call_target="tpu_custom_call" | custom-call | tf_op jit(solution)/shard_map/grads/pallas_call | solution.py:200
  153.1 7.7 %grads.3 = (bf16[4,128,1024]{2,1,0:T(8,128)(2,1)}, bf16[2,64,768]{2,1,0:T(8,128)(2,1)}, bf16[2,64,768]{2,1,0:T(8,128)(2,1)}, bf16[2,64,768]{2,1,0:T(8,128)(2,1)}, bf16[2,64,768]{2,1,0:T(8,128)(2,1)}) custom-call(s32[1]{0:T(128)} %bitcast.core_ref, f32[4,128,1024]{2,1,0:T(8,128)} %bitcast.84, ...), custom_call_target="tpu_custom_call", output_to_operand_aliasing={{0}: (10, {})} | custom-call | tf_op jit(solution)/shard_map/grads/pallas_call | solution.py:200
  160.8 3.4 %convolution_convert_fusion = bf16[768,1024]{1,0:T(8,128)(2,1)} fusion(bf16[512,1024]{1,0:T(8,128)(2,1)} %bitcast.92, bf16[2,512,768]{2,1,0:T(8,128)(2,1)S(1)} %copy-done.2, s32[]{:T(128)S(6)} %select_n.97), kind=kOutput, calls=%fused_computation.2 | convolution fusion | flops 806092800 | bytes 3407876 | tf_op jit(solution)/shard_map/dot_general | solution.py:338
  165.9 1.7 collective-permute-start.23
  168.3 2.2 %convolution_convert_fusion.1 = bf16[768,1024]{1,0:T(8,128)(2,1)S(1)} fusion(bf16[512,1024]{1,0:T(8,128)(2,1)} %bitcast.93, bf16[2,512,768]{2,1,0:T(8,128)(2,1)S(1)} %copy-done.2, s32[]{:T(128)S(6)} %select_n.96), kind=kOutput, calls=%fused_computation.3 | convolution fusion | flops 806092800 | bytes 3407876 | tf_op jit(solution)/shard_map/dot_general | solution.py:338
  170.6 1.1 collective-permute-start.36
  171.7 1.8 add_convert_fusion
  173.5 3.9 %all-to-all-start.1 = ((bf16[4,192,1024]{2,1,0:T(8,128)(2,1)}), bf16[4,192,1024]{2,1,0:T(8,128)(2,1)S(1)}, u32[]{:S(2)}, u32[]{:S(2)}) async-start(bf16[4,192,1024]{2,1,0:T(8,128)(2,1)} %bitcast.35), calls=%async_computation.1 | async-start | bytes 3145728 | tf_op jit(solution)/shard_map/all_to_all | solution.py:343
  177.5 2.7 %collective-permute-start.37 = (bf16[2,64,768]{2,1,0:T(8,128)(2,1)}, bf16[2,64,768]{2,1,0:T(8,128)(2,1)S(1)}, u32[]{:S(2)}, u32[]{:S(2)}) collective-permute-start(bf16[2,64,768]{2,1,0:T(8,128)(2,1)} %get-tuple-element.46), channel_id=1, source_target_pairs={{0,24},{4,28},{8,16},{12,20},{16,8},{20,12},{24,0},{28,4},{1,25},{... | collective-permute-start | bytes 589832 | tf_op jit(solution)/shard_map/ppermute | solution.py:22
  180.1 1.2 add_convert_fusion.2
  182.2 1.8 collective-permute-start.26
  184.0 1.7 collective-permute-start.25
  185.6 16.2 %collective-permute-done.37 = bf16[2,64,768]{2,1,0:T(8,128)(2,1)S(1)} collective-permute-done((bf16[2,64,768]{2,1,0:T(8,128)(2,1)}, bf16[2,64,768]{2,1,0:T(8,128)(2,1)S(1)}, u32[]{:S(2)}, u32[]{:S(2)}) %collective-permute-start.37) | collective-permute-done | bytes 196640 | tf_op jit(solution)/shard_map/ppermute | solution.py:22
  202.8 1.8 collective-permute-start.40
  204.6 1.7 collective-permute-start.39
  206.3 1.2 collective-permute-done.38
  207.5 1.4 collective-permute-done.40
  208.9 1.4 collective-permute-done.39
  210.9 1.3 copy.54
  (136 shorter events, 20.0 us)
Async XLA Ops:
  3.3 25.3 %all-to-all-start = ((bf16[192,4,1024]{2,0,1:T(8,128)(2,1)}), bf16[192,4,1024]{2,0,1:T(8,128)(2,1)S(1)}, u32[]{:S(2)}, u32[]{:S(2)}) async-start(bf16[192,4,1024]{2,0,1:T(8,128)(2,1)} %bitcast.78), calls=%async_computation | async-start | bytes 3145728 | tf_op jit(solution)/shard_map/all_to_all | solution.py:283
  11.4 16.2 %copy-start.16 = (s32[128,2]{0,1:T(2,128)S(1)}, s32[128,2]{0,1:T(2,128)}, u32[]{:S(2)}) copy-start(s32[128,2]{0,1:T(2,128)} %param.11) | copy-start | bytes 3076
  11.4 18.1 %collective-permute-start.6 = (f32[64,128]{1,0:T(8,128)}, f32[64,128]{1,0:T(8,128)S(1)}, u32[]{:S(2)}, u32[]{:S(2)}) collective-permute-start(f32[64,128]{1,0:T(8,128)} %bitcast.12), channel_id=1, source_target_pairs={{0,3},{1,2},{2,1},{3,0},{4,7},{5,6},{6,5},{7,4},{8,11},{9,10},{10,... | collective-permute-start | bytes 98312 | tf_op jit(solution)/shard_map/ppermute | solution.py:22
  15.0 18.4 %collective-permute-start.5 = (f32[64,128]{1,0:T(8,128)}, f32[64,128]{1,0:T(8,128)}, u32[]{:S(2)}, u32[]{:S(2)}) collective-permute-start(f32[64,128]{1,0:T(8,128)} %bitcast.12), channel_id=1, source_target_pairs={{0,2},{1,3},{2,0},{3,1},{4,6},{5,7},{6,4},{7,5},{8,10},{9,11},{10,... | collective-permute-start | bytes 98312 | tf_op jit(solution)/shard_map/ppermute | solution.py:22
  19.4 32.9 %collective-permute-start.14 = (bf16[40,64,128]{2,1,0:T(8,128)(2,1)}, bf16[40,64,128]{2,1,0:T(8,128)(2,1)}, u32[]{:S(2)}, u32[]{:S(2)}) collective-permute-start(bf16[40,64,128]{2,1,0:T(8,128)(2,1)} %get-tuple-element.28.refs_0_), channel_id=1, source_target_pairs={{1,2},{2,1},{5,6},{6,5},{9,10},{10,9},{13,14},{14,13},{17,18},{18,... | collective-permute-start | bytes 1966088 | tf_op jit(solution)/shard_map/ppermute | solution.py:271
  21.0 25.0 %collective-permute-start.13 = (bf16[40,64,128]{2,1,0:T(8,128)(2,1)}, bf16[40,64,128]{2,1,0:T(8,128)(2,1)}, u32[]{:S(2)}, u32[]{:S(2)}) collective-permute-start(bf16[40,64,128]{2,1,0:T(8,128)(2,1)} %get-tuple-element.28.refs_0_), channel_id=1, source_target_pairs={{0,1},{3,2},{4,5},{7,6},{8,9},{11,10},{12,13},{15,14},{16,17},{19,... | collective-permute-start | bytes 1966088 | tf_op jit(solution)/shard_map/ppermute | solution.py:271
  28.6 35.8 %copy-start = (bf16[192,4,1024]{2,0,1:T(8,128)(2,1)}, bf16[192,4,1024]{2,0,1:T(8,128)(2,1)S(1)}, u32[]{:S(2)}) copy-start(bf16[192,4,1024]{2,0,1:T(8,128)(2,1)S(1)} %all-to-all-done) | copy-start | bytes 4718596
  28.6 44.9 %collective-permute-start.3 = (bf16[768,1024]{1,0:T(8,128)(2,1)S(1)}, bf16[768,1024]{1,0:T(8,128)(2,1)S(1)}, u32[]{:S(2)}, u32[]{:S(2)}) collective-permute-start(bf16[768,1024]{1,0:T(8,128)(2,1)S(1)} %bitcast.79), channel_id=1, source_target_pairs={{0,4},{4,0},{8,12},{12,8},{16,20},{20,16},{24,28},{28,24},{1,5},{5... | collective-permute-start | bytes 4718600 | tf_op jit(solution)/shard_map/ppermute | solution.py:22
  29.5 0.7 copy-start.22
  29.5 11.2 %collective-permute-start.4 = (f32[64,128]{1,0:T(8,128)}, f32[64,128]{1,0:T(8,128)}, u32[]{:S(2)}, u32[]{:S(2)}) collective-permute-start(f32[64,128]{1,0:T(8,128)} %bitcast.12), channel_id=1, source_target_pairs={{0,1},{1,0},{2,3},{3,2},{4,5},{5,4},{6,7},{7,6},{8,9},{9,8},{10,11... | collective-permute-start | bytes 98312 | tf_op jit(solution)/shard_map/ppermute | solution.py:22
  33.4 17.2 %collective-permute-start.2 = (bf16[2,128,768]{2,1,0:T(8,128)(2,1)S(1)}, bf16[2,128,768]{2,1,0:T(8,128)(2,1)}, u32[]{:S(2)}, u32[]{:S(2)}) collective-permute-start(bf16[2,128,768]{2,1,0:T(8,128)(2,1)S(1)} %copy.41), channel_id=1, source_target_pairs={{0,24},{4,28},{8,16},{12,20},{16,8},{20,12},{24,0},{28,4},{1,25},{... | collective-permute-start | bytes 1179656 | tf_op jit(solution)/shard_map/ppermute | solution.py:22
  40.7 16.8 %collective-permute-start.27 = (bf16[40,64,128]{2,1,0:T(8,128)(2,1)}, bf16[40,64,128]{2,1,0:T(8,128)(2,1)}, u32[]{:S(2)}, u32[]{:S(2)}) collective-permute-start(bf16[40,64,128]{2,1,0:T(8,128)(2,1)} %get-tuple-element.29.refs_0_), channel_id=1, source_target_pairs={{0,1},{3,2},{4,5},{7,6},{8,9},{11,10},{12,13},{15,14},{16,17},{19,... | collective-permute-start | bytes 1966088 | tf_op jit(solution)/shard_map/ppermute | solution.py:271
  45.9 13.1 %collective-permute-start.15 = (bf16[40,64,128]{2,1,0:T(8,128)(2,1)}, bf16[40,64,128]{2,1,0:T(8,128)(2,1)}, u32[]{:S(2)}, u32[]{:S(2)}) collective-permute-start(bf16[40,64,128]{2,1,0:T(8,128)(2,1)} %collective-permute-done.13.refs_1_), channel_id=1, source_target_pairs={{1,2},{2,1},{5,6},{6,5},{9,10},{10,9},{13,14},{14,13},{17,18},{18,... | collective-permute-start | bytes 1966088 | tf_op jit(solution)/shard_map/ppermute | solution.py:271
  50.5 16.1 %collective-permute-start.1 = (bf16[2,128,768]{2,1,0:T(8,128)(2,1)S(1)}, bf16[2,128,768]{2,1,0:T(8,128)(2,1)}, u32[]{:S(2)}, u32[]{:S(2)}) collective-permute-start(bf16[2,128,768]{2,1,0:T(8,128)(2,1)S(1)} %copy.41), channel_id=1, source_target_pairs={{0,16},{4,20},{8,24},{12,28},{16,0},{20,4},{24,8},{28,12},{1,17},{... | collective-permute-start | bytes 1179656 | tf_op jit(solution)/shard_map/ppermute | solution.py:22
  52.2 15.7 %collective-permute-start = (bf16[2,128,768]{2,1,0:T(8,128)(2,1)S(1)}, bf16[2,128,768]{2,1,0:T(8,128)(2,1)}, u32[]{:S(2)}, u32[]{:S(2)}) collective-permute-start(bf16[2,128,768]{2,1,0:T(8,128)(2,1)S(1)} %copy.41), channel_id=1, source_target_pairs={{0,8},{4,12},{8,0},{12,4},{16,24},{20,28},{24,16},{28,20},{1,9},{5... | collective-permute-start | bytes 1179656 | tf_op jit(solution)/shard_map/ppermute | solution.py:22
  57.5 27.2 %collective-permute-start.28 = (bf16[40,64,128]{2,1,0:T(8,128)(2,1)}, bf16[40,64,128]{2,1,0:T(8,128)(2,1)}, u32[]{:S(2)}, u32[]{:S(2)}) collective-permute-start(bf16[40,64,128]{2,1,0:T(8,128)(2,1)} %get-tuple-element.29.refs_0_), channel_id=1, source_target_pairs={{1,2},{2,1},{5,6},{6,5},{9,10},{10,9},{13,14},{14,13},{17,18},{18,... | collective-permute-start | bytes 1966088 | tf_op jit(solution)/shard_map/ppermute | solution.py:271
  59.0 37.3 %collective-permute-start.29 = (bf16[40,64,128]{2,1,0:T(8,128)(2,1)}, bf16[40,64,128]{2,1,0:T(8,128)(2,1)}, u32[]{:S(2)}, u32[]{:S(2)}) collective-permute-start(bf16[40,64,128]{2,1,0:T(8,128)(2,1)} %collective-permute-done.27.refs_1_), channel_id=1, source_target_pairs={{1,2},{2,1},{5,6},{6,5},{9,10},{10,9},{13,14},{14,13},{17,18},{18,... | collective-permute-start | bytes 1966088 | tf_op jit(solution)/shard_map/ppermute | solution.py:271
  66.6 34.2 %collective-permute-start.16 = (bf16[32,64,128]{2,1,0:T(8,128)(2,1)}, bf16[32,64,128]{2,1,0:T(8,128)(2,1)}, u32[]{:S(2)}, u32[]{:S(2)}) collective-permute-start(bf16[32,64,128]{2,1,0:T(8,128)(2,1)} %pack.4), channel_id=1, source_target_pairs={{2,3},{1,0},{6,7},{5,4},{10,11},{9,8},{14,15},{13,12},{18,19},{17,... | collective-permute-start | bytes 1572872 | tf_op jit(solution)/shard_map/ppermute | solution.py:278
  68.0 34.2 %collective-permute-start.17 = (bf16[32,64,128]{2,1,0:T(8,128)(2,1)}, bf16[32,64,128]{2,1,0:T(8,128)(2,1)}, u32[]{:S(2)}, u32[]{:S(2)}) collective-permute-start(bf16[32,64,128]{2,1,0:T(8,128)(2,1)} %pack.5), channel_id=1, source_target_pairs={{2,3},{1,0},{6,7},{5,4},{10,11},{9,8},{14,15},{13,12},{18,19},{17,... | collective-permute-start | bytes 1572872 | tf_op jit(solution)/shard_map/ppermute | solution.py:278
  73.5 1.2 copy-start.1
  82.1 29.1 %copy-start.14 = (f32[512]{0:T(512)}, f32[512]{0:T(512)S(1)}, u32[]{:S(2)}) copy-start(f32[512]{0:T(512)S(1)} %reduce) | copy-start | bytes 6148
  83.2 26.5 %collective-permute-start.9 = (f32[9,128]{1,0:T(8,128)S(1)}, f32[9,128]{1,0:T(8,128)S(1)}, u32[]{:S(2)}, u32[]{:S(2)}) collective-permute-start(f32[9,128]{1,0:T(8,128)S(1)} %pad_maximum_fusion.2), channel_id=1, source_target_pairs={{0,3},{1,2},{2,1},{3,0},{4,7},{5,6},{6,5},{7,4},{8,11},{9,10},{10,... | collective-permute-start | bytes 13832 | tf_op jit(solution)/shard_map/ppermute | solution.py:22
  84.8 26.4 %collective-permute-start.8 = (f32[9,128]{1,0:T(8,128)S(1)}, f32[9,128]{1,0:T(8,128)S(1)}, u32[]{:S(2)}, u32[]{:S(2)}) collective-permute-start(f32[9,128]{1,0:T(8,128)S(1)} %pad_maximum_fusion.2), channel_id=1, source_target_pairs={{0,2},{1,3},{2,0},{3,1},{4,6},{5,7},{6,4},{7,5},{8,10},{9,11},{10,... | collective-permute-start | bytes 13832 | tf_op jit(solution)/shard_map/ppermute | solution.py:22
  96.3 14.9 %collective-permute-start.7 = (f32[9,128]{1,0:T(8,128)S(1)}, f32[9,128]{1,0:T(8,128)S(1)}, u32[]{:S(2)}, u32[]{:S(2)}) collective-permute-start(f32[9,128]{1,0:T(8,128)S(1)} %pad_maximum_fusion.2), channel_id=1, source_target_pairs={{0,1},{1,0},{2,3},{3,2},{4,5},{5,4},{6,7},{7,6},{8,9},{9,8},{10,11... | collective-permute-start | bytes 13832 | tf_op jit(solution)/shard_map/ppermute | solution.py:22
  98.5 2.3 %copy-start.3 = (bf16[32,64,128]{2,1,0:T(8,128)(2,1)S(1)}, bf16[32,64,128]{2,1,0:T(8,128)(2,1)}, u32[]{:S(2)}) copy-start(bf16[32,64,128]{2,1,0:T(8,128)(2,1)} %pack.6) | copy-start | bytes 1572868
  100.8 10.5 %copy-start.20 = (f32[128]{0:T(128)S(1)}, f32[128]{0:T(128)}, u32[]{:S(2)}) copy-start(f32[128]{0:T(128)} %param.13) | copy-start | bytes 1540
  100.8 20.7 %collective-permute-start.30 = (bf16[32,64,128]{2,1,0:T(8,128)(2,1)S(1)}, bf16[32,64,128]{2,1,0:T(8,128)(2,1)S(1)}, u32[]{:S(2)}, u32[]{:S(2)}) collective-permute-start(bf16[32,64,128]{2,1,0:T(8,128)(2,1)S(1)} %copy-done.3), channel_id=1, source_target_pairs={{2,3},{1,0},{6,7},{5,4},{10,11},{9,8},{14,15},{13,12},{18,19},{17,... | collective-permute-start | bytes 1572872 | tf_op jit(solution)/shard_map/ppermute | solution.py:278
  102.1 25.7 %collective-permute-start.31 = (bf16[32,64,128]{2,1,0:T(8,128)(2,1)}, bf16[32,64,128]{2,1,0:T(8,128)(2,1)S(1)}, u32[]{:S(2)}, u32[]{:S(2)}) collective-permute-start(bf16[32,64,128]{2,1,0:T(8,128)(2,1)} %pack.7), channel_id=1, source_target_pairs={{2,3},{1,0},{6,7},{5,4},{10,11},{9,8},{14,15},{13,12},{18,19},{17,... | collective-permute-start | bytes 1572872 | tf_op jit(solution)/shard_map/ppermute | solution.py:278
  109.7 30.3 %collective-permute-start.18 = (bf16[64,1024]{1,0:T(8,128)(2,1)}, bf16[64,1024]{1,0:T(8,128)(2,1)S(1)}, u32[]{:S(2)}, u32[]{:S(2)}) collective-permute-start(bf16[64,1024]{1,0:T(8,128)(2,1)} %get-tuple-element.31), channel_id=1, source_target_pairs={{0,8},{4,12},{8,0},{12,4},{16,24},{20,28},{24,16},{28,20},{1,9},{5... | collective-permute-start | bytes 393224 | tf_op jit(solution)/shard_map/ppermute | solution.py:22
  111.3 23.7 %copy-start.15 = (f32[10,128]{1,0:T(8,128)}, f32[10,128]{1,0:T(8,128)S(1)}, u32[]{:S(2)}) copy-start(f32[10,128]{1,0:T(8,128)S(1)} %pad_maximum_fusion.3.refs_0_) | copy-start | bytes 15364
  111.3 23.7 %collective-permute-start.12 = (f32[10,128]{1,0:T(8,128)S(1)}, f32[10,128]{1,0:T(8,128)S(1)}, u32[]{:S(2)}, u32[]{:S(2)}) collective-permute-start(f32[10,128]{1,0:T(8,128)S(1)} %pad_maximum_fusion.3.refs_0_), channel_id=1, source_target_pairs={{0,24},{4,28},{8,16},{12,20},{16,8},{20,12},{24,0},{28,4},{1,25},{... | collective-permute-start | bytes 15368 | tf_op jit(solution)/shard_map/ppermute | solution.py:22
  112.8 24.0 %collective-permute-start.11 = (f32[10,128]{1,0:T(8,128)S(1)}, f32[10,128]{1,0:T(8,128)S(1)}, u32[]{:S(2)}, u32[]{:S(2)}) collective-permute-start(f32[10,128]{1,0:T(8,128)S(1)} %pad_maximum_fusion.3.refs_0_), channel_id=1, source_target_pairs={{0,16},{4,20},{8,24},{12,28},{16,0},{20,4},{24,8},{28,12},{1,17},{... | collective-permute-start | bytes 15368 | tf_op jit(solution)/shard_map/ppermute | solution.py:22
  121.5 7.4 %copy-start.4 = (bf16[32,64,128]{2,1,0:T(8,128)(2,1)}, bf16[32,64,128]{2,1,0:T(8,128)(2,1)S(1)}, u32[]{:S(2)}) copy-start(bf16[32,64,128]{2,1,0:T(8,128)(2,1)S(1)} %collective-permute-done.30.refs_4_) | copy-start | bytes 1572868
  121.5 16.0 %collective-permute-start.10 = (f32[10,128]{1,0:T(8,128)S(1)}, f32[10,128]{1,0:T(8,128)S(1)}, u32[]{:S(2)}, u32[]{:S(2)}) collective-permute-start(f32[10,128]{1,0:T(8,128)S(1)} %pad_maximum_fusion.3.refs_0_), channel_id=1, source_target_pairs={{0,8},{4,12},{8,0},{12,4},{16,24},{20,28},{24,16},{28,20},{1,9},{5... | collective-permute-start | bytes 15368 | tf_op jit(solution)/shard_map/ppermute | solution.py:22
  127.8 1.1 copy-start.5
  127.8 7.2 %copy-start.21 = (bf16[64,1024]{1,0:T(8,128)(2,1)S(1)}, bf16[64,1024]{1,0:T(8,128)(2,1)}, u32[]{:S(2)}) copy-start(bf16[64,1024]{1,0:T(8,128)(2,1)} %get-tuple-element.33) | copy-start | bytes 393220
  127.8 16.3 %collective-permute-start.19 = (bf16[64,1024]{1,0:T(8,128)(2,1)}, bf16[64,1024]{1,0:T(8,128)(2,1)S(1)}, u32[]{:S(2)}, u32[]{:S(2)}) collective-permute-start(bf16[64,1024]{1,0:T(8,128)(2,1)} %get-tuple-element.32), channel_id=1, source_target_pairs={{0,16},{4,20},{8,24},{12,28},{16,0},{20,4},{24,8},{28,12},{1,17},{... | collective-permute-start | bytes 393224 | tf_op jit(solution)/shard_map/ppermute | solution.py:22
  135.0 3.6 %copy-start.17 = (f32[10,128]{1,0:T(8,128)}, f32[10,128]{1,0:T(8,128)S(1)}, u32[]{:S(2)}) copy-start(f32[10,128]{1,0:T(8,128)S(1)} %collective-permute-done.12.refs_3_) | copy-start | bytes 15364
  135.0 9.1 %collective-permute-start.20 = (bf16[64,1024]{1,0:T(8,128)(2,1)S(1)}, bf16[64,1024]{1,0:T(8,128)(2,1)S(1)}, u32[]{:S(2)}, u32[]{:S(2)}) collective-permute-start(bf16[64,1024]{1,0:T(8,128)(2,1)S(1)} %copy-done.21), channel_id=1, source_target_pairs={{0,24},{4,28},{8,16},{12,20},{16,8},{20,12},{24,0},{28,4},{1,25},{... | collective-permute-start | bytes 393224 | tf_op jit(solution)/shard_map/ppermute | solution.py:22
  136.8 1.8 copy-start.18
  136.8 15.5 %collective-permute-start.32 = (bf16[64,1024]{1,0:T(8,128)(2,1)}, bf16[64,1024]{1,0:T(8,128)(2,1)S(1)}, u32[]{:S(2)}, u32[]{:S(2)}) collective-permute-start(bf16[64,1024]{1,0:T(8,128)(2,1)} %get-tuple-element.39), channel_id=1, source_target_pairs={{0,8},{4,12},{8,0},{12,4},{16,24},{20,28},{24,16},{28,20},{1,9},{5... | collective-permute-start | bytes 393224 | tf_op jit(solution)/shard_map/ppermute | solution.py:22
  137.5 1.1 copy-start.19
  137.5 14.8 %collective-permute-start.33 = (bf16[64,1024]{1,0:T(8,128)(2,1)}, bf16[64,1024]{1,0:T(8,128)(2,1)S(1)}, u32[]{:S(2)}, u32[]{:S(2)}) collective-permute-start(bf16[64,1024]{1,0:T(8,128)(2,1)} %get-tuple-element.40), channel_id=1, source_target_pairs={{0,16},{4,20},{8,24},{12,28},{16,0},{20,4},{24,8},{28,12},{1,17},{... | collective-permute-start | bytes 393224 | tf_op jit(solution)/shard_map/ppermute | solution.py:22
  140.0 4.2 %copy-start.8 = (bf16[64,1024]{1,0:T(8,128)(2,1)}, bf16[64,1024]{1,0:T(8,128)(2,1)S(1)}, u32[]{:S(2)}) copy-start(bf16[64,1024]{1,0:T(8,128)(2,1)S(1)} %collective-permute-done.18.refs_1_) | copy-start | bytes 393220
  140.0 12.4 %collective-permute-start.34 = (bf16[64,1024]{1,0:T(8,128)(2,1)}, bf16[64,1024]{1,0:T(8,128)(2,1)S(1)}, u32[]{:S(2)}, u32[]{:S(2)}) collective-permute-start(bf16[64,1024]{1,0:T(8,128)(2,1)} %get-tuple-element.41), channel_id=1, source_target_pairs={{0,24},{4,28},{8,16},{12,20},{16,8},{20,12},{24,0},{28,4},{1,25},{... | collective-permute-start | bytes 393224 | tf_op jit(solution)/shard_map/ppermute | solution.py:22
  144.1 0.7 copy-start.10
  152.4 0.7 copy-start.13
  153.1 7.7 %copy-start.2 = (bf16[2,512,768]{2,1,0:T(8,128)(2,1)S(1)}, bf16[2,512,768]{2,1,0:T(8,128)(2,1)}, u32[]{:S(2)}) copy-start(bf16[2,512,768]{2,1,0:T(8,128)(2,1)} %pad_maximum_fusion.x_ref) | copy-start | bytes 4718596
  164.1 6.4 %collective-permute-start.41 = (bf16[768,1024]{1,0:T(8,128)(2,1)}, bf16[768,1024]{1,0:T(8,128)(2,1)S(1)}, u32[]{:S(2)}, u32[]{:S(2)}) collective-permute-start(bf16[768,1024]{1,0:T(8,128)(2,1)} %convolution_convert_fusion), channel_id=1, source_target_pairs={{0,4},{4,0},{8,12},{12,8},{16,20},{20,16},{24,28},{28,24},{1,5},{5... | collective-permute-start | bytes 4718600 | tf_op jit(solution)/shard_map/ppermute | solution.py:22
  164.1 13.3 %collective-permute-start.21 = (bf16[2,64,768]{2,1,0:T(8,128)(2,1)}, bf16[2,64,768]{2,1,0:T(8,128)(2,1)}, u32[]{:S(2)}, u32[]{:S(2)}) collective-permute-start(bf16[2,64,768]{2,1,0:T(8,128)(2,1)} %get-tuple-element.35), channel_id=1, source_target_pairs={{0,8},{4,12},{8,0},{12,4},{16,24},{20,28},{24,16},{28,20},{1,9},{5... | collective-permute-start | bytes 589832 | tf_op jit(solution)/shard_map/ppermute | solution.py:22
  164.8 15.3 %collective-permute-start.22 = (bf16[2,64,768]{2,1,0:T(8,128)(2,1)}, bf16[2,64,768]{2,1,0:T(8,128)(2,1)}, u32[]{:S(2)}, u32[]{:S(2)}) collective-permute-start(bf16[2,64,768]{2,1,0:T(8,128)(2,1)} %get-tuple-element.36), channel_id=1, source_target_pairs={{0,16},{4,20},{8,24},{12,28},{16,0},{20,4},{24,8},{28,12},{1,17},{... | collective-permute-start | bytes 589832 | tf_op jit(solution)/shard_map/ppermute | solution.py:22
  165.9 14.2 %collective-permute-start.23 = (bf16[2,64,768]{2,1,0:T(8,128)(2,1)}, bf16[2,64,768]{2,1,0:T(8,128)(2,1)}, u32[]{:S(2)}, u32[]{:S(2)}) collective-permute-start(bf16[2,64,768]{2,1,0:T(8,128)(2,1)} %get-tuple-element.37), channel_id=1, source_target_pairs={{0,24},{4,28},{8,16},{12,20},{16,8},{20,12},{24,0},{28,4},{1,25},{... | collective-permute-start | bytes 589832 | tf_op jit(solution)/shard_map/ppermute | solution.py:22
  167.6 16.3 %collective-permute-start.35 = (bf16[2,64,768]{2,1,0:T(8,128)(2,1)}, bf16[2,64,768]{2,1,0:T(8,128)(2,1)S(1)}, u32[]{:S(2)}, u32[]{:S(2)}) collective-permute-start(bf16[2,64,768]{2,1,0:T(8,128)(2,1)} %get-tuple-element.44), channel_id=1, source_target_pairs={{0,8},{4,12},{8,0},{12,4},{16,24},{20,28},{24,16},{28,20},{1,9},{5... | collective-permute-start | bytes 589832 | tf_op jit(solution)/shard_map/ppermute | solution.py:22
  170.6 15.1 %collective-permute-start.36 = (bf16[2,64,768]{2,1,0:T(8,128)(2,1)}, bf16[2,64,768]{2,1,0:T(8,128)(2,1)S(1)}, u32[]{:S(2)}, u32[]{:S(2)}) collective-permute-start(bf16[2,64,768]{2,1,0:T(8,128)(2,1)} %get-tuple-element.45), channel_id=1, source_target_pairs={{0,16},{4,20},{8,24},{12,28},{16,0},{20,4},{24,8},{28,12},{1,17},{... | collective-permute-start | bytes 589832 | tf_op jit(solution)/shard_map/ppermute | solution.py:22
  173.5 6.6 %copy-start.7 = (bf16[2,64,768]{2,1,0:T(8,128)(2,1)S(1)}, bf16[2,64,768]{2,1,0:T(8,128)(2,1)}, u32[]{:S(2)}) copy-start(bf16[2,64,768]{2,1,0:T(8,128)(2,1)} %get-tuple-element.34) | copy-start | bytes 589828
  173.5 37.4 %all-to-all-start.1 = ((bf16[4,192,1024]{2,1,0:T(8,128)(2,1)}), bf16[4,192,1024]{2,1,0:T(8,128)(2,1)S(1)}, u32[]{:S(2)}, u32[]{:S(2)}) async-start(bf16[4,192,1024]{2,1,0:T(8,128)(2,1)} %bitcast.35), calls=%async_computation.1 | async-start | bytes 3145728 | tf_op jit(solution)/shard_map/all_to_all | solution.py:343
  177.4 24.4 %copy-start.6 = (bf16[2,64,768]{2,1,0:T(8,128)(2,1)S(1)}, bf16[2,64,768]{2,1,0:T(8,128)(2,1)}, u32[]{:S(2)}) copy-start(bf16[2,64,768]{2,1,0:T(8,128)(2,1)} %get-tuple-element.43) | copy-start | bytes 589828
  177.5 24.4 %collective-permute-start.37 = (bf16[2,64,768]{2,1,0:T(8,128)(2,1)}, bf16[2,64,768]{2,1,0:T(8,128)(2,1)S(1)}, u32[]{:S(2)}, u32[]{:S(2)}) collective-permute-start(bf16[2,64,768]{2,1,0:T(8,128)(2,1)} %get-tuple-element.46), channel_id=1, source_target_pairs={{0,24},{4,28},{8,16},{12,20},{16,8},{20,12},{24,0},{28,4},{1,25},{... | collective-permute-start | bytes 589832 | tf_op jit(solution)/shard_map/ppermute | solution.py:22
  182.1 22.5 %collective-permute-start.24 = (bf16[64,384]{1,0:T(8,128)(2,1)S(1)}, bf16[64,384]{1,0:T(8,128)(2,1)S(1)}, u32[]{:S(2)}, u32[]{:S(2)}) collective-permute-start(bf16[64,384]{1,0:T(8,128)(2,1)S(1)} %get-tuple-element.56), channel_id=1, source_target_pairs={{0,1},{1,0},{2,3},{3,2},{4,5},{5,4},{6,7},{7,6},{8,9},{9,8},{10,11... | collective-permute-start | bytes 147464 | tf_op jit(solution)/shard_map/ppermute | solution.py:22
  182.2 24.1 %collective-permute-start.26 = (bf16[64,384]{1,0:T(8,128)(2,1)S(1)}, bf16[64,384]{1,0:T(8,128)(2,1)S(1)}, u32[]{:S(2)}, u32[]{:S(2)}) collective-permute-start(bf16[64,384]{1,0:T(8,128)(2,1)S(1)} %get-tuple-element.57), channel_id=1, source_target_pairs={{0,3},{1,2},{2,1},{3,0},{4,7},{5,6},{6,5},{7,4},{8,11},{9,10},{10,... | collective-permute-start | bytes 147464 | tf_op jit(solution)/shard_map/ppermute | solution.py:22
  184.0 22.3 %collective-permute-start.25 = (bf16[64,384]{1,0:T(8,128)(2,1)S(1)}, bf16[64,384]{1,0:T(8,128)(2,1)S(1)}, u32[]{:S(2)}, u32[]{:S(2)}) collective-permute-start(bf16[64,384]{1,0:T(8,128)(2,1)S(1)} %get-tuple-element.58), channel_id=1, source_target_pairs={{0,2},{1,3},{2,0},{3,1},{4,6},{5,7},{6,4},{7,5},{8,10},{9,11},{10,... | collective-permute-start | bytes 147464 | tf_op jit(solution)/shard_map/ppermute | solution.py:22
  202.7 4.8 %collective-permute-start.38 = (bf16[64,384]{1,0:T(8,128)(2,1)S(1)}, bf16[64,384]{1,0:T(8,128)(2,1)S(1)}, u32[]{:S(2)}, u32[]{:S(2)}) collective-permute-start(bf16[64,384]{1,0:T(8,128)(2,1)S(1)} %get-tuple-element.59), channel_id=1, source_target_pairs={{0,1},{1,0},{2,3},{3,2},{4,5},{5,4},{6,7},{7,6},{8,9},{9,8},{10,11... | collective-permute-start | bytes 147464 | tf_op jit(solution)/shard_map/ppermute | solution.py:22
  202.8 6.1 %collective-permute-start.40 = (bf16[64,384]{1,0:T(8,128)(2,1)S(1)}, bf16[64,384]{1,0:T(8,128)(2,1)S(1)}, u32[]{:S(2)}, u32[]{:S(2)}) collective-permute-start(bf16[64,384]{1,0:T(8,128)(2,1)S(1)} %get-tuple-element.60), channel_id=1, source_target_pairs={{0,3},{1,2},{2,1},{3,0},{4,7},{5,6},{6,5},{7,4},{8,11},{9,10},{10,... | collective-permute-start | bytes 147464 | tf_op jit(solution)/shard_map/ppermute | solution.py:22
  204.6 5.6 %collective-permute-start.39 = (bf16[64,384]{1,0:T(8,128)(2,1)S(1)}, bf16[64,384]{1,0:T(8,128)(2,1)S(1)}, u32[]{:S(2)}, u32[]{:S(2)}) collective-permute-start(bf16[64,384]{1,0:T(8,128)(2,1)S(1)} %get-tuple-element.61), channel_id=1, source_target_pairs={{0,2},{1,3},{2,0},{3,1},{4,6},{5,7},{6,4},{7,5},{8,10},{9,11},{10,... | collective-permute-start | bytes 147464 | tf_op jit(solution)/shard_map/ppermute | solution.py:22
  (3 other events, 2.0 us)
where the time goes:
time: 214 us; the launch traced here: 212 us
  starting transfers between devices  82.3 us (38%)
  Pallas kernels  48.3 us (23%)
  waiting for transfers between devices  37.7 us (18%)
  local copies, waits for them, and re-layouts  17.9 us (8%)
  other arithmetic  17.5 us (8%)
  matrix products  7.24 us (3%)
    ppermute x32, starting transfers between devices, swap(): lax.ppermute(x, axis, [(i, i ^ bits) for i in range(lax.axis_size(axis))])  49.9 us
    ppermute x32, waiting for transfers between devices, swap(): lax.ppermute(x, axis, [(i, i ^ bits) for i in range(lax.axis_size(axis))])  24.7 us
    ppermute x6, starting transfers between devices, exchange(): lax.ppermute(moved[r - 1, i - 1], 'vocab', [(i, i + 1), (vocab - 1 - i, v...  18 us
    pallas_call x2, Pallas kernels, grads(): pl.pallas_call(functools.partial(grads_kernel, chips), grid_spec=pltpu.Pr...  15.1 us
    ppermute x4, waiting for transfers between devices, exchange(): packed.append(lax.ppermute(part, 'vocab', [(vocab - 2, vocab - 1), (1, 0)]))  13 us
    pallas_call x2, Pallas kernels, mapped_parts(): pl.pallas_call(functools.partial(mapped_kernel, chips), grid_spec=pltpu.P...  12.2 us
    pallas_call x4, Pallas kernels, pack(): pl.pallas_call(functools.partial(pack_kernel, first, vocab), grid_spec=pl...  8.86 us
    pallas_call x1, Pallas kernels, logits_parts(): pl.pallas_call(logits_kernel, grid_spec=pltpu.PrefetchScalarGridSpec(num_...  6.36 us
  transfers between devices with their start and end apart: 44, of which 8 were waited for; matrix products, arithmetic and copies ran while one was open for 15% of the time, Pallas kernels for 19%

commit v1 on v0

v1 whole, which is shorter than its diff:
```python
import functools

import jax
import jax.numpy as jnp
from jax import lax
from jax.experimental import pallas as pl
from jax.experimental.pallas import tpu as pltpu
from jax.sharding import PartitionSpec as P


BLOCK = 128
K = 2
HALVES = 2

ANY = pl.BlockSpec(memory_space=pl.ANY)
VMEM = pl.BlockSpec(memory_space=pltpu.VMEM)
F32 = jnp.float32
BF16 = jnp.bfloat16


def swap(x, axis, bits):
    return lax.ppermute(x, axis, [(i, i ^ bits) for i in range(lax.axis_size(axis))])


def probs_kernel(x_ref, out_ref):
    rows = out_ref.shape[2]
    for j in range(out_ref.shape[1]):
        block = jnp.exp(x_ref[:, j * BLOCK : (j + 1) * BLOCK]).astype(BF16)
        for n in range(HALVES):
            out_ref[n, j] = block[n * rows : (n + 1) * rows]


def teacher_blocks(logprobs):
    tokens, cols = logprobs.shape
    count = cols // BLOCK
    step = next(s for s in (8, 5, 4, 2, 1) if count % s == 0)
    rows = tokens // HALVES
    return pl.pallas_call(
        probs_kernel,
        grid=(count // step,),
        in_specs=[pl.BlockSpec((tokens, step * BLOCK), lambda i: (0, i))],
        out_specs=pl.BlockSpec((HALVES, step, rows, BLOCK), lambda i: (0, i, 0, 0)),
        out_shape=jax.ShapeDtypeStruct((HALVES, count, rows, BLOCK), BF16),
        name="probs",
    )(logprobs)


def flatten(sources):
    flat, views = [], []
    for source in sources:
        split = isinstance(source, list)
        views.append((len(flat), split))
        flat += source if split else [source]
    return flat, views


def half_of(refs, view, n):
    at, split = view
    return refs[at + n] if split else refs[at].at[n]


def pack_kernel(first, halves, views, vocab, tab_ref, *refs):
    out_ref, sem = refs[-2], refs[-1]
    v = tab_ref[6, 0]
    row = jnp.where(v == 1, 0, 1)

    def start(slot, carry):
        far, block = tab_ref[2 + row, first + slot], tab_ref[4 + row, first + slot]
        for i, view in enumerate(views):

            @pl.when(far == i + 1)
            def _(view=view):
                for k, n in enumerate(halves):
                    pltpu.make_async_copy(half_of(refs, view, n).at[block], out_ref.at[k, slot], sem).start()

        return carry

    @pl.when((v == 1) | (v == vocab - 2))
    def _():
        lax.fori_loop(0, out_ref.shape[1], start, 0)
        pltpu.make_async_copy(out_ref, out_ref, sem).wait()


def pack(tab, first, capacity, sources, halves, vocab):
    flat, views = flatten(sources)
    return pl.pallas_call(
        functools.partial(pack_kernel, first, halves, views, vocab),
        grid_spec=pltpu.PrefetchScalarGridSpec(
            num_scalar_prefetch=1,
            grid=(),
            in_specs=[ANY] * len(flat),
            out_specs=VMEM,
            scratch_shapes=[pltpu.SemaphoreType.DMA],
        ),
        out_shape=jax.ShapeDtypeStruct((len(halves), capacity) + flat[0].shape[-2:], BF16),
        name="pack",
    )(tab, *flat)


def mapped_kernel(pieces, views, tab_ref, *refs):
    tiles_ref, outs, buf, sem = refs[-len(pieces) - 3], refs[-len(pieces) - 2 : -2], refs[-2], refs[-1]
    me = tab_ref[6, 1]
    per = outs[0].shape[1] // BLOCK
    entries = per * K
    rows = buf.shape[1] // HALVES

    for at, piece in enumerate(pieces):
        base = lax.bitwise_xor(me, piece) * entries

        def start(p, carry, at=at, base=base):
            source, block = tab_ref[0, base + p], tab_ref[1, base + p]
            for i, view in enumerate(views):

                @pl.when(source == i)
                def _(view=view):
                    for n in range(HALVES):
                        pltpu.make_async_copy(
                            half_of(refs, view, n).at[block],
                            buf.at[at * entries + p, pl.ds(n * rows, rows)],
                            sem,
                        ).start()

            return carry

        lax.fori_loop(0, entries, start, 0)
    pltpu.make_async_copy(buf, buf, sem).wait()
    for at, (piece, out) in enumerate(zip(pieces, outs)):
        dest = lax.bitwise_xor(me, piece)
        for j in range(per):
            p = at * entries + K * j
            total = jnp.dot(buf[p], tiles_ref[dest * per + j, 0], preferred_element_type=F32)
            for k in range(1, K):
                total += jnp.dot(buf[p + k], tiles_ref[dest * per + j, k], preferred_element_type=F32)
            out[:, j * BLOCK : (j + 1) * BLOCK] = total.astype(BF16)


def mapped_parts(tab, sources, tiles, chips, pieces):
    flat, views = flatten(sources)
    tokens = HALVES * flat[0].shape[-2]
    cols = tiles.shape[0] * BLOCK // chips
    return pl.pallas_call(
        functools.partial(mapped_kernel, pieces, views),
        grid_spec=pltpu.PrefetchScalarGridSpec(
            num_scalar_prefetch=1,
            grid=(),
            in_specs=[ANY] * len(flat) + [VMEM],
            out_specs=[VMEM] * len(pieces),
            scratch_shapes=[
                pltpu.VMEM((len(pieces) * cols // BLOCK * K, tokens, BLOCK), BF16),
                pltpu.SemaphoreType.DMA,
            ],
        ),
        out_shape=[jax.ShapeDtypeStruct((tokens, cols), BF16)] * len(pieces),
        name="mapped",
    )(tab, *flat, tiles)


def turned(x):
    n = max(x.shape)
    full = jnp.broadcast_to(x, (n, n)).T
    return full[:, :1] if x.shape[0] == 1 else full[:1]


def logits_kernel(core_ref, x_ref, own_ref, other_ref, e_ref, s_ref):
    i, c = pl.program_id(0), core_ref[0]
    logits = jnp.dot(x_ref[c], own_ref[...], preferred_element_type=F32)
    logits += jnp.dot(x_ref[1 - c], other_ref[...], preferred_element_type=F32)
    top = jnp.max(logits, axis=1, keepdims=True)
    e = jnp.exp(logits - top)
    e_ref[0] = e
    s_ref[0, pl.ds(i, 1)] = turned(top)
    s_ref[1, pl.ds(i, 1)] = turned(jnp.sum(e, axis=1, keepdims=True))


def logits_parts(core, hidden, own, other, tokens):
    chips = hidden.shape[1] // tokens
    features, cols = own.shape
    fixed = pl.BlockSpec((features, cols), lambda i, core: (0, 0))
    return pl.pallas_call(
        logits_kernel,
        grid_spec=pltpu.PrefetchScalarGridSpec(
            num_scalar_prefetch=1,
            grid=(chips,),
            in_specs=[pl.BlockSpec((2, tokens, features), lambda i, core: (0, i, 0)), fixed, fixed],
            out_specs=[
                pl.BlockSpec((1, tokens, cols), lambda i, core: (i, 0, 0)),
                pl.BlockSpec((2, chips, tokens), lambda i, core: (0, 0, 0)),
            ],
        ),
        out_shape=[
            jax.ShapeDtypeStruct((chips, tokens, cols), F32),
            jax.ShapeDtypeStruct((2, chips, tokens), F32),
        ],
        name="logits",
    )(core, hidden, own, other)


def stats_kernel(order, own_ref, *refs):
    shares, a_ref, b_ref = refs[:-2], refs[-2], refs[-1]
    chips = len(shares)
    for k, piece in enumerate(order):
        rows = [order.index(piece ^ r) for r in range(chips)]
        tops = [shares[r][j : j + 1] for r, j in enumerate(rows)]
        top = functools.reduce(jnp.maximum, tops)
        total = sum(shares[r][chips + j : chips + j + 1] * jnp.exp(tops[r] - top) for r, j in enumerate(rows))
        mass = shares[piece][2 * chips : 2 * chips + 1]
        scale = shares[piece][2 * chips + 1 : 2 * chips + 2]
        a_ref[k] = turned(scale * mass * (jnp.exp(own_ref[0, k : k + 1] - top) / total))
        b_ref[k] = turned(scale)


def grads_kernel(core_ref, e_ref, a_ref, b_ref, own_ref, other_ref, *refs):
    count = e_ref.shape[0]
    mapped, dl_ref, outs = refs[:count], refs[-count - 1], refs[-count:]
    c = core_ref[0]
    for k in range(count):
        dl = (a_ref[k] * e_ref[k] - b_ref[k] * mapped[k][...].astype(F32)).astype(BF16)
        dl_ref[k] = dl
        for half, weight in ((c, own_ref), (1 - c, other_ref)):
            terms = lax.dot_general(dl, weight[...], (((1,), (1,)), ((), ())), preferred_element_type=F32)
            outs[k][half] = terms.astype(BF16)


def grads(part, core, e, a, b, own, other, mapped, dl):
    count, tokens = len(mapped), mapped[0].shape[0]
    features, cols = own.shape
    some = lambda n: pl.BlockSpec((count, tokens, n), lambda i, core: (part, 0, 0))
    whole = lambda *shape: pl.BlockSpec(shape, lambda i, core: (0,) * len(shape))
    return pl.pallas_call(
        grads_kernel,
        grid_spec=pltpu.PrefetchScalarGridSpec(
            num_scalar_prefetch=1,
            grid=(1,),
            in_specs=[some(cols), some(1), some(1), whole(features, cols), whole(features, cols)]
            + [whole(tokens, cols)] * count
            + ([] if dl is None else [ANY]),
            out_specs=[some(cols)] + [whole(2, tokens, features)] * count,
        ),
        out_shape=[jax.ShapeDtypeStruct(e.shape, BF16)]
        + [jax.ShapeDtypeStruct((2, tokens, features), BF16)] * count,
        input_output_aliases={} if dl is None else {6 + count: 0},
        name="grads",
    )(core, e, a, b, own, other, *mapped, *([] if dl is None else [dl]))


def body(student_hidden, head_weight, teacher_logprobs, align_index, align_tiles, grad_scale):
    vocab = lax.axis_size("vocab")
    dp = lax.axis_size("dp")
    v = lax.axis_index("vocab")
    d = lax.axis_index("dp")
    chips, chip, c = dp // 2, d // 2, d % 2
    core = c.astype(jnp.int32)[None]
    tokens, features = student_hidden.shape
    count = teacher_logprobs.shape[1] // BLOCK
    pairs = align_tiles.shape[0] * K
    capacity = (2 * pairs + vocab - 1) // vocab
    packs = (pairs + capacity - 1) // capacity
    if vocab < 4 or vocab & (vocab - 1) or dp & (dp - 1):
        raise ValueError("mesh sizes")
    groups = [[2 * i + j for i in range(chips)] for j in range(2)]

    blocks = teacher_blocks(teacher_logprobs)

    hops = [(r, i) for r in range(1, vocab - 1) for i in range(r - 1, vocab - 2)]
    number_of = [[0] * vocab for _ in range(vocab)]
    for i in range(1, vocab - 1):
        for o in range(vocab):
            if o != i:
                link = i - 1 if o < i else vocab - 2 - i
                number_of[i][o] = 1 + hops.index((abs(o - i), link))

    rows = align_index.reshape(vocab, pairs)
    ends = jnp.stack([rows[0], rows[vocab - 1]])
    end_owner, end_local = lax.div(ends, jnp.int32(count)), lax.rem(ends, jnp.int32(count))
    end_far = jnp.abs(end_owner - jnp.array([[0], [vocab - 1]]))
    number = jnp.arange(pairs)
    later = (end_far[:, None, :] > end_far[:, :, None]) | (
        (end_far[:, None, :] == end_far[:, :, None]) & (number[None, None, :] >= number[None, :, None])
    )
    end_slot = packs * capacity - jnp.sum((later & (end_far[:, None, :] > 0)).astype(jnp.int32), axis=2)
    end_slot = jnp.where(end_far > 0, end_slot, -1)
    own = lax.dynamic_index_in_dim(rows, v, 0, keepdims=False)
    own_owner, own_local = lax.div(own, jnp.int32(count)), lax.rem(own, jnp.int32(count))
    own_slot = jnp.where(v == 0, end_slot[0], end_slot[1])
    at_end = ((v == 0) | (v == vocab - 1)) & (own_owner != v)
    numbers = lax.dynamic_index_in_dim(jnp.array(number_of, jnp.int32), v, 0, keepdims=False)
    source = jnp.sum(
        jnp.where(own_owner[None, :] == jnp.arange(vocab)[:, None], numbers[:, None], 0), axis=0
    )
    source = jnp.where(at_end, 1 + len(hops) + lax.div(own_slot, jnp.int32(capacity)), source)
    place = jnp.where(at_end, lax.rem(own_slot, jnp.int32(capacity)), own_local)
    me = jnp.where(number == 0, v, chip)
    filled = (end_slot[:, None, :] == number[None, :, None]).astype(jnp.int32)
    slot_far = jnp.maximum(jnp.sum(filled * end_far[:, None, :], axis=2), 1)
    slot_local = jnp.sum(filled * end_local[:, None, :], axis=2)
    tab = jnp.concatenate([source[None], place[None], slot_far, slot_local, me[None]], axis=0).astype(jnp.int32)

    def hop(x, i):
        return lax.ppermute(x, "vocab", [(i, i + 1), (vocab - 1 - i, vocab - 2 - i)])

    moved = {(0, i): blocks for i in range(-1, vocab)}
    for r, i in hops:
        x = moved[r - 1, i - 1]
        if r == 1:
            moved[r, i] = hop(x, i)
        else:
            moved[r, i] = [hop(x[n], i) for n in range(HALVES)]
    near = [blocks] + [moved[r, vocab - 3] for r in range(1, vocab - 1)]

    def last(q, halves):
        part = pack(tab, q * capacity, capacity, near[: q - packs + vocab], halves, vocab)
        return lax.ppermute(part, "vocab", [(vocab - 2, vocab - 1), (1, 0)])

    packed = [last(q, range(HALVES)) for q in range(packs - 1)]
    packed.append([last(packs - 1, [n])[0] for n in range(HALVES)])
    sources = [blocks] + [moved[h] for h in hops] + packed

    weight_own = lax.all_to_all(head_weight, "dp", split_axis=1, concat_axis=0, axis_index_groups=groups, tiled=True)
    weight_other = swap(weight_own, "dp", 1)

    hidden = student_hidden.reshape(tokens, chips, 2, features // dp).transpose(2, 0, 1, 3)
    hidden = hidden.reshape(2, tokens, features // 2)
    others = [swap(hidden, "dp", 2 * j) for j in range(1, chips)]
    order = list(range(chips))[::-1]
    hidden = jnp.concatenate(others[::-1] + [hidden], axis=1)
    e, local = logits_parts(core, hidden, weight_own, weight_other, tokens)

    row_sums = jnp.sum(align_tiles.astype(F32), axis=3).reshape(pairs, BLOCK)
    all_sums = [row_sums] + [swap(row_sums, "vocab", t) for t in range(1, vocab)]
    all_rows = [own] + [lax.dynamic_index_in_dim(rows, v ^ t, 0, keepdims=False) for t in range(1, vocab)]
    hits = (jnp.concatenate(all_rows)[None, :] == (v * count + jnp.arange(count))[:, None]).astype(F32)
    entry_weight = jnp.dot(hits, jnp.concatenate(all_sums), precision=lax.Precision.HIGHEST)
    mass = jnp.sum(blocks.astype(F32) * entry_weight[None, :, None, :], axis=(1, 3)).reshape(tokens)

    share = jnp.concatenate([local.reshape(2 * chips, tokens), mass[None]])
    shares = [share] + [swap(share, "vocab", t) for t in range(1, vocab)]
    plane_top = functools.reduce(jnp.maximum, [s[:chips] for s in shares])
    plane_total = sum(s[chips : 2 * chips] * jnp.exp(s[:chips] - plane_top) for s in shares)
    plane_mass = sum(s[2 * chips] for s in shares)
    share = jnp.concatenate([plane_top, plane_total, plane_mass[None], grad_scale[None]])
    shares = [share] + [swap(share, "dp", 2 * j) for j in range(1, chips)]
    column = jax.ShapeDtypeStruct((chips, tokens, 1), F32)
    a, b = pl.pallas_call(
        functools.partial(stats_kernel, order),
        in_specs=[VMEM] * (chips + 1),
        out_specs=[VMEM, VMEM],
        out_shape=[column, column],
        name="stats",
    )(local, *shares)

    count = chips // 2
    columns, terms, dl = [], [], None
    for n in range(2):
        pieces = order[n * count : (n + 1) * count]
        parts = mapped_parts(tab, sources, align_tiles, chips, pieces)
        columns.append([x if j == 0 else swap(x, "dp", 2 * j) for x, j in zip(parts, pieces)])
    for n in range(2):
        pieces = order[n * count : (n + 1) * count]
        dl, *parts = grads(n, core, e, a, b, weight_own, weight_other, columns[n], dl)
        terms += [x if j == 0 else swap(x, "dp", 2 * j) for x, j in zip(parts, pieces)]
    rows_sum = sum([x.astype(F32) for x in terms[:-1]], terms[-1].astype(F32))
    rows_sum = rows_sum.astype(BF16).reshape(2, -1, chips, features // dp).transpose(1, 2, 0, 3)
    pieces = rows_sum.reshape(-1, vocab, features // vocab).transpose(1, 0, 2)
    piece = lambda t: lax.dynamic_index_in_dim(pieces, v ^ t, 0, keepdims=False)
    hidden_grad = piece(0).astype(F32)
    others = [swap(piece(t), "vocab", t) for t in range(1, vocab)]
    hidden_grad = sum([x.astype(F32) for x in others], hidden_grad).astype(BF16)
    dl = dl.reshape(chips * tokens, -1)

    def head_half(half):
        x = lax.dynamic_index_in_dim(hidden, half, 0, keepdims=False)
        return lax.dot_general(x, dl, (((0,), (0,)), ((), ())), preferred_element_type=F32).astype(BF16)

    half = head_half(1 - c)
    got = swap(half, "dp", 1)
    head_terms = (head_half(c).astype(F32) + got.astype(F32)).astype(BF16)
    head_grad = lax.all_to_all(
        head_terms, "dp", split_axis=0, concat_axis=1, axis_index_groups=groups, tiled=True
    )
    return (hidden_grad, head_grad)


def solution(mesh):
    placed = (
        P("dp", None),
        P("dp", "vocab"),
        P("dp", "vocab"),
        P(),
        P("vocab", None, None, None),
        P("dp"),
    )
    return jax.shard_map(
        body,
        mesh=mesh,
        in_specs=placed,
        out_specs=(P("dp", "vocab"), P("dp", "vocab")),
        check_vma=False,
    )
```

time: 214 us -> 238 us (1.11)
  waiting for transfers between devices: 37.7 us -> 106 us
  starting transfers between devices: 82.3 us -> 56.7 us
  Pallas kernels: 48.3 us -> 38.2 us
  other arithmetic: 17.5 us -> 9.91 us
    ppermute x32 -> x23, waiting for transfers between devices: 24.7 us -> 89.7 us  [swap(): lax.ppermute(x, axis, [(i, i ^ bits) for i in range(lax.axis_size(axis))])]
    ppermute x32 -> x23, starting transfers between devices: 49.9 us -> 32.5 us  [swap(): lax.ppermute(x, axis, [(i, i ^ bits) for i in range(lax.axis_size(axis))])]
    all_to_all x1, waiting for transfers between devices: 0.01 us -> 15.8 us  [body(): lax.all_to_all(head_weight, 'dp', split_axis=1, concat_axis=0, axis_index...]
    ppermute x10 -> x7, waiting for transfers between devices: 13 us -> 0.09 us  [the longest x4 0.08 us: hop(): lax.ppermute(x, 'vocab', [(i, i + 1), (vocab - 1 - i, vocab - 2 - i)])]
    pallas_call x9 -> x8, Pallas kernels: 37.6 us -> 27.3 us  [the longest x2 11 us: grads(): pl.pallas_call(grads_kernel, grid_spec=pltpu.PrefetchScalarGridSpec(num_s...]
    ppermute x10 -> x7, starting transfers between devices: 23.3 us -> 16 us  [the longest x4 11.9 us: hop(): lax.ppermute(x, 'vocab', [(i, i + 1), (vocab - 1 - i, vocab - 2 - i)])]
    unnamed x48 -> x65, local copies, waits for them, and re-layouts: 3.98 us -> 6.96 us
    squeeze x0 -> x1, local copies, waits for them, and re-layouts: none -> 2.44 us  [body(): moved[r, i] = [hop(x[n], i) for n in range(HALVES)]]
  transfers between devices with their start and end apart: 44 -> 32, of which waited for: 8 -> 13; matrix products, arithmetic and copies ran while one was open for 15% -> 10% of each run, Pallas kernels for 19% -> 12%
where the time goes in v1:
time: 238 us; the launch traced here: 237 us
  waiting for transfers between devices  106 us (45%)
  starting transfers between devices  56.7 us (24%)
  Pallas kernels  38.2 us (16%)
  local copies, waits for them, and re-layouts  18.6 us (8%)
  other arithmetic  9.91 us (4%)
  matrix products  6.64 us (3%)
    ppermute x23, waiting for transfers between devices, swap(): lax.ppermute(x, axis, [(i, i ^ bits) for i in range(lax.axis_size(axis))])  89.7 us
    ppermute x23, starting transfers between devices, swap(): lax.ppermute(x, axis, [(i, i ^ bits) for i in range(lax.axis_size(axis))])  32.5 us
    all_to_all x1, waiting for transfers between devices, body(): lax.all_to_all(head_weight, 'dp', split_axis=1, concat_axis=0, axis_index...  15.8 us
    ppermute x4, starting transfers between devices, hop(): lax.ppermute(x, 'vocab', [(i, i + 1), (vocab - 1 - i, vocab - 2 - i)])  11.9 us
    pallas_call x2, Pallas kernels, grads(): pl.pallas_call(grads_kernel, grid_spec=pltpu.PrefetchScalarGridSpec(num_s...  11 us
    pallas_call x2, Pallas kernels, mapped_parts(): pl.pallas_call(functools.partial(mapped_kernel, pieces, views), grid_spec...  9.55 us
    unnamed x65, local copies, waits for them, and re-layouts  6.96 us
    pallas_call x1, Pallas kernels, logits_parts(): pl.pallas_call(logits_kernel, grid_spec=pltpu.PrefetchScalarGridSpec(num_...  6.31 us
  transfers between devices with their start and end apart: 32, of which 13 were waited for; matrix products, arithmetic and copies ran while one was open for 10% of the time, Pallas kernels for 12%

profile of v1, /device:TPU:0, one launch (start us, length us, event | category | flops | bytes accessed | tf_op | source)
XLA Modules:
  0.0 236.8 jit_solution(4393303179419452935)
XLA Ops:
  0.6 4.6 %probs.1.refs_0_ = bf16[2,40,64,128]{3,2,1,0:T(8,128)(2,1)} custom-call(f32[128,5120]{1,0:T(8,128)} %x_ref.1), custom_call_target="tpu_custom_call" | custom-call | tf_op jit(solution)/shard_map/probs/pallas_call | solution.py:38
  5.2 0.9 collective-permute-start.14
  6.1 8.9 %collective-permute-start.13 = (bf16[2,40,64,128]{3,2,1,0:T(8,128)(2,1)}, bf16[2,40,64,128]{3,2,1,0:T(8,128)(2,1)}, u32[]{:S(2)}, u32[]{:S(2)}) collective-permute-start(bf16[2,40,64,128]{3,2,1,0:T(8,128)(2,1)} %probs.1.refs_0_), channel_id=1, source_target_pairs={{0,1},{3,2},{4,5},{7,6},{8,9},{11,10},{12,13},{15,14},{16,17},{19,... | collective-permute-start | bytes 3932168 | tf_op jit(solution)/shard_map/ppermute | solution.py:299
  15.0 1.3 convert_reduce_fusion
  16.2 1.3 collective-permute-start.6
  17.6 1.3 copy.49
  18.9 4.5 %all-to-all-start = ((bf16[192,4,1024]{2,0,1:T(8,128)(2,1)}), bf16[192,4,1024]{2,0,1:T(8,128)(2,1)}, u32[]{:S(2)}, u32[]{:S(2)}) async-start(bf16[192,4,1024]{2,0,1:T(8,128)(2,1)} %bitcast.75), calls=%async_computation | async-start | bytes 3145728 | tf_op jit(solution)/shard_map/all_to_all | solution.py:318
  26.3 15.8 %all-to-all-done = bf16[192,4,1024]{2,0,1:T(8,128)(2,1)} async-done(((bf16[192,4,1024]{2,0,1:T(8,128)(2,1)}), bf16[192,4,1024]{2,0,1:T(8,128)(2,1)}, u32[]{:S(2)}, u32[]{:S(2)}) %all-to-all-start) | async-done | bytes 1572896 | tf_op jit(solution)/shard_map/all_to_all | solution.py:318
  42.2 2.4 %slice_bitcast_fusion = (bf16[40,64,128]{2,1,0:T(8,128)(2,1)}, bf16[40,64,128]{2,1,0:T(8,128)(2,1)}) fusion(bf16[2,40,64,128]{3,2,1,0:T(8,128)(2,1)} %collective-permute-done.13.refs_1_), kind=kLoop, calls=%fused_computation.12 | loop fusion | bytes 2621440 | tf_op jit(solution)/shard_map/squeeze | solution.py:307
  45.9 1.5 collective-permute-start.15
  47.5 6.1 %collective-permute-start.5 = (f32[64,128]{1,0:T(8,128)}, f32[64,128]{1,0:T(8,128)}, u32[]{:S(2)}, u32[]{:S(2)}) collective-permute-start(f32[64,128]{1,0:T(8,128)} %bitcast.13), channel_id=1, source_target_pairs={{0,2},{1,3},{2,0},{3,1},{4,6},{5,7},{6,4},{7,5},{8,10},{9,11},{10,... | collective-permute-start | bytes 98312 | tf_op jit(solution)/shard_map/ppermute | solution.py:22
  53.7 1.9 copy.32
  55.6 1.8 copy.33
  57.4 1.9 copy.34
  59.3 19.9 %collective-permute-done.5 = f32[64,128]{1,0:T(8,128)} collective-permute-done((f32[64,128]{1,0:T(8,128)}, f32[64,128]{1,0:T(8,128)}, u32[]{:S(2)}, u32[]{:S(2)}) %collective-permute-start.5) | collective-permute-done | bytes 32800 | tf_op jit(solution)/shard_map/ppermute | solution.py:22
  79.2 1.5 collective-permute-start.2
  80.7 1.5 collective-permute-start.1
  82.2 1.3 concatenate.41.tab_ref
  83.5 1.7 pack.3
  85.2 1.3 collective-permute-start.17
  87.2 3.6 %collective-permute-start.4 = (f32[64,128]{1,0:T(8,128)}, f32[64,128]{1,0:T(8,128)}, u32[]{:S(2)}, u32[]{:S(2)}) collective-permute-start(f32[64,128]{1,0:T(8,128)} %bitcast.13), channel_id=1, source_target_pairs={{0,1},{1,0},{2,3},{3,2},{4,5},{5,4},{6,7},{7,6},{8,9},{9,8},{10,11... | collective-permute-start | bytes 98312 | tf_op jit(solution)/shard_map/ppermute | solution.py:22
  90.8 1.5 pack.5
  92.4 1.7 pack.4
  94.1 15.8 %collective-permute-done.4 = f32[64,128]{1,0:T(8,128)} collective-permute-done((f32[64,128]{1,0:T(8,128)}, f32[64,128]{1,0:T(8,128)}, u32[]{:S(2)}, u32[]{:S(2)}) %collective-permute-start.4) | collective-permute-done | bytes 32800 | tf_op jit(solution)/shard_map/ppermute | solution.py:22
  110.3 1.3 collective-permute-start.18
  111.6 1.5 collective-permute-start.19
  113.1 1.0 fusion.7
  114.6 4.2 %collective-permute-done = bf16[2,128,768]{2,1,0:T(8,128)(2,1)} collective-permute-done((bf16[2,128,768]{2,1,0:T(8,128)(2,1)}, bf16[2,128,768]{2,1,0:T(8,128)(2,1)}, u32[]{:S(2)}, u32[]{:S(2)}) %collective-permute-start) | collective-permute-done | bytes 393248 | tf_op jit(solution)/shard_map/ppermute | solution.py:22
  118.8 2.6 %pad_maximum_fusion.x_ref = bf16[2,512,768]{2,1,0:T(8,128)(2,1)} fusion(bf16[2,128,768]{2,1,0:T(8,128)(2,1)} %copy.34, bf16[2,128,768]{2,1,0:T(8,128)(2,1)} %collective-permute-done.2, bf16[2,128,768]{2,1,0:T(8,128)(2,1)} %collective-permute-done.1, bf16[2,128,768]{2,1,0:T(8,128)(2,1)} %collective-permute-done), kind=kLoop, calls=%fused_computation.6 | loop fusion | flops 6291456 | bytes 3145728 | tf_op jit(solution)/shard_map/concatenate | solution.py:325
  121.4 1.2 copy-done.3
  122.6 6.3 %logits.1 = (f32[4,128,1024]{2,1,0:T(8,128)}, f32[2,4,128]{2,1,0:T(4,128)}) custom-call(s32[1]{0:T(128)} %bitcast.core_ref, bf16[2,512,768]{2,1,0:T(8,128)(2,1)} %pad_maximum_fusion.x_ref, bf16[768,1024]{1,0:T(8,128)(2,1)} %bitcast.5.own_ref, bf16[768,1024]{1,0:T(8,128)(2,1)} %copy-done.3), custom_call_target="tpu_custom_call" | custom-call | tf_op jit(solution)/shard_map/logits/pallas_call | solution.py:179
  129.6 1.3 collective-permute-start.9
  131.0 3.0 %collective-permute-start.7 = (f32[9,128]{1,0:T(8,128)S(1)}, f32[9,128]{1,0:T(8,128)S(1)}, u32[]{:S(2)}, u32[]{:S(2)}) collective-permute-start(f32[9,128]{1,0:T(8,128)S(1)} %pad_maximum_fusion.1), channel_id=1, source_target_pairs={{0,1},{1,0},{2,3},{3,2},{4,5},{5,4},{6,7},{7,6},{8,9},{9,8},{10,11... | collective-permute-start | bytes 13832 | tf_op jit(solution)/shard_map/ppermute | solution.py:22
  134.0 0.8 copy-done.6
  134.8 4.8 %mapped.3 = (bf16[128,1024]{1,0:T(8,128)(2,1)}, bf16[128,1024]{1,0:T(8,128)(2,1)}) custom-call(s32[7,64]{1,0:T(8,128)} %concatenate.41.tab_ref, bf16[2,40,64,128]{3,2,1,0:T(8,128)(2,1)} %probs.1.refs_0_, bf16[2,40,64,128]{3,2,1,0:T(8,128)(2,1)} %collective-permute-done.13.refs_1_, bf16[2,40,64,128]{3,2,1,0:T(8,128)(2,1)} %copy-done.1, ...), custom_call_target="tpu_custom_call" | custom-call | tf_op jit(solution)/shard_map/mapped/pallas_call | solution.py:141
  139.6 1.2 collective-permute-start.21
  140.8 0.9 collective-permute-start.22
  141.6 4.8 %mapped.2 = (bf16[128,1024]{1,0:T(8,128)(2,1)}, bf16[128,1024]{1,0:T(8,128)(2,1)}) custom-call(s32[7,64]{1,0:T(8,128)} %concatenate.41.tab_ref, bf16[2,40,64,128]{3,2,1,0:T(8,128)(2,1)} %probs.1.refs_0_, bf16[2,40,64,128]{3,2,1,0:T(8,128)(2,1)} %collective-permute-done.13.refs_1_, bf16[2,40,64,128]{3,2,1,0:T(8,128)(2,1)} %copy-done.1, ...), custom_call_target="tpu_custom_call" | custom-call | tf_op jit(solution)/shard_map/mapped/pallas_call | solution.py:141
  146.4 1.6 collective-permute-start.20
  148.1 1.2 collective-permute-start.12
  149.2 0.9 collective-permute-start.11
  150.1 3.7 %collective-permute-done.12.refs_3_ = f32[10,128]{1,0:T(8,128)S(1)} collective-permute-done((f32[10,128]{1,0:T(8,128)S(1)}, f32[10,128]{1,0:T(8,128)S(1)}, u32[]{:S(2)}, u32[]{:S(2)}) %collective-permute-start.12) | collective-permute-done | bytes 5152 | tf_op jit(solution)/shard_map/ppermute | solution.py:22
  153.8 0.9 collective-permute-start.10
  154.7 2.8 %collective-permute-done.10.refs_1_ = f32[10,128]{1,0:T(8,128)S(1)} collective-permute-done((f32[10,128]{1,0:T(8,128)S(1)}, f32[10,128]{1,0:T(8,128)S(1)}, u32[]{:S(2)}, u32[]{:S(2)}) %collective-permute-start.10) | collective-permute-done | bytes 5152 | tf_op jit(solution)/shard_map/ppermute | solution.py:22
  158.1 1.8 stats.1
  160.7 5.4 %grads.2 = (bf16[4,128,1024]{2,1,0:T(8,128)(2,1)}, bf16[2,128,768]{2,1,0:T(8,128)(2,1)}, bf16[2,128,768]{2,1,0:T(8,128)(2,1)}) custom-call(s32[1]{0:T(128)} %bitcast.core_ref, f32[4,128,1024]{2,1,0:T(8,128)} %get-tuple-element.16.e_ref, f32[4,128,1]{2,1,0:T(8,128)} %get-tuple-element.18.a_ref, f32[4,128,1]{2,1,0:T(8,128)} %get-tuple-element.19.b_ref, ...), custom_call_target="tpu_custom_call" | custom-call | tf_op jit(solution)/shard_map/grads/pallas_call | solution.py:229
  166.2 0.7 copy-done.11
  166.9 5.6 %grads.3 = (bf16[4,128,1024]{2,1,0:T(8,128)(2,1)}, bf16[2,128,768]{2,1,0:T(8,128)(2,1)}, bf16[2,128,768]{2,1,0:T(8,128)(2,1)}) custom-call(s32[1]{0:T(128)} %bitcast.core_ref, f32[4,128,1024]{2,1,0:T(8,128)} %get-tuple-element.16.e_ref, f32[4,128,1]{2,1,0:T(8,128)} %get-tuple-element.18.a_ref, ...), custom_call_target="tpu_custom_call", output_to_operand_aliasing={{0}: (8, {})} | custom-call | tf_op jit(solution)/shard_map/grads/pallas_call | solution.py:229
  172.5 3.4 %convolution_convert_fusion = bf16[768,1024]{1,0:T(8,128)(2,1)} fusion(bf16[512,1024]{1,0:T(8,128)(2,1)} %bitcast.86, bf16[2,512,768]{2,1,0:T(8,128)(2,1)S(1)} %copy-done.5, s32[]{:T(128)S(6)} %select_n.97), kind=kOutput, calls=%fused_computation.3 | convolution fusion | flops 806092800 | bytes 3407876 | tf_op jit(solution)/shard_map/dot_general | solution.py:372
  175.9 2.2 convolution_convert_fusion.1
  178.1 1.4 collective-permute-done.29
  179.5 1.8 add_convert_fusion
  181.3 3.7 %all-to-all-start.1 = ((bf16[4,192,1024]{2,1,0:T(8,128)(2,1)}), bf16[4,192,1024]{2,1,0:T(8,128)(2,1)S(1)}, u32[]{:S(2)}, u32[]{:S(2)}) async-start(bf16[4,192,1024]{2,1,0:T(8,128)(2,1)} %bitcast.33), calls=%async_computation.1 | async-start | bytes 3145728 | tf_op jit(solution)/shard_map/all_to_all | solution.py:377
  185.0 2.0 collective-permute-start.25
  187.0 1.5 collective-permute-start.23
  188.6 25.5 %collective-permute-done.25 = bf16[2,128,768]{2,1,0:T(8,128)(2,1)S(1)} collective-permute-done((bf16[2,128,768]{2,1,0:T(8,128)(2,1)S(1)}, bf16[2,128,768]{2,1,0:T(8,128)(2,1)S(1)}, u32[]{:S(2)}, u32[]{:S(2)}) %collective-permute-start.25) | collective-permute-done | bytes 393248 | tf_op jit(solution)/shard_map/ppermute | solution.py:22
  214.1 8.5 %collective-permute-done.23 = bf16[2,128,768]{2,1,0:T(8,128)(2,1)S(1)} collective-permute-done((bf16[2,128,768]{2,1,0:T(8,128)(2,1)S(1)}, bf16[2,128,768]{2,1,0:T(8,128)(2,1)S(1)}, u32[]{:S(2)}, u32[]{:S(2)}) %collective-permute-start.23) | collective-permute-done | bytes 393248 | tf_op jit(solution)/shard_map/ppermute | solution.py:22
  223.2 1.4 collective-permute-start.28
  224.6 2.0 collective-permute-start.27
  226.6 2.4 collective-permute-done.26
  229.0 1.4 collective-permute-done.28
  230.4 4.3 %collective-permute-done.27 = bf16[128,384]{0,1:T(8,128)(2,1)S(1)} collective-permute-done((bf16[128,384]{0,1:T(8,128)(2,1)S(1)}, bf16[128,384]{0,1:T(8,128)(2,1)S(1)}, u32[]{:S(2)}, u32[]{:S(2)}) %collective-permute-start.27) | collective-permute-done | bytes 98336 | tf_op jit(solution)/shard_map/ppermute | solution.py:22
  234.7 0.8 copy.45
  235.5 1.3 copy.47
  (118 shorter events, 8.9 us)
Async XLA Ops:
  0.6 14.3 %copy-start.2 = (bf16[32,2,128,128]{3,2,1,0:T(8,128)(2,1)S(1)}, bf16[32,2,128,128]{3,2,1,0:T(8,128)(2,1)}, u32[]{:S(2)}) copy-start(bf16[32,2,128,128]{3,2,1,0:T(8,128)(2,1)} %refs_8_.3) | copy-start | bytes 6291460
  5.2 12.4 %copy-start.7 = (bf16[192,4096]{1,0:T(8,128)(2,1)S(1)}, bf16[192,4096]{1,0:T(8,128)(2,1)}, u32[]{:S(2)}) copy-start(bf16[192,4096]{1,0:T(8,128)(2,1)} %param.9) | copy-start | bytes 4718596
  5.2 75.5 %collective-permute-start.14 = (bf16[2,40,64,128]{3,2,1,0:T(8,128)(2,1)}, bf16[2,40,64,128]{3,2,1,0:T(8,128)(2,1)S(1)}, u32[]{:S(2)}, u32[]{:S(2)}) collective-permute-start(bf16[2,40,64,128]{3,2,1,0:T(8,128)(2,1)} %probs.1.refs_0_), channel_id=1, source_target_pairs={{1,2},{2,1},{5,6},{6,5},{9,10},{10,9},{13,14},{14,13},{17,18},{18,... | collective-permute-start | bytes 3932168 | tf_op jit(solution)/shard_map/ppermute | solution.py:299
  6.1 36.1 %collective-permute-start.13 = (bf16[2,40,64,128]{3,2,1,0:T(8,128)(2,1)}, bf16[2,40,64,128]{3,2,1,0:T(8,128)(2,1)}, u32[]{:S(2)}, u32[]{:S(2)}) collective-permute-start(bf16[2,40,64,128]{3,2,1,0:T(8,128)(2,1)} %probs.1.refs_0_), channel_id=1, source_target_pairs={{0,1},{3,2},{4,5},{7,6},{8,9},{11,10},{12,13},{15,14},{16,17},{19,... | collective-permute-start | bytes 3932168 | tf_op jit(solution)/shard_map/ppermute | solution.py:299
  16.2 31.2 %collective-permute-start.6 = (f32[64,128]{1,0:T(8,128)}, f32[64,128]{1,0:T(8,128)}, u32[]{:S(2)}, u32[]{:S(2)}) collective-permute-start(f32[64,128]{1,0:T(8,128)} %bitcast.13), channel_id=1, source_target_pairs={{0,3},{1,2},{2,1},{3,0},{4,7},{5,6},{6,5},{7,4},{8,11},{9,10},{10,... | collective-permute-start | bytes 98312 | tf_op jit(solution)/shard_map/ppermute | solution.py:22
  18.9 4.5 %copy-start.14 = (s32[128,2]{0,1:T(2,128)S(1)}, s32[128,2]{0,1:T(2,128)}, u32[]{:S(2)}) copy-start(s32[128,2]{0,1:T(2,128)} %param.11) | copy-start | bytes 3076
  18.9 23.2 %all-to-all-start = ((bf16[192,4,1024]{2,0,1:T(8,128)(2,1)}), bf16[192,4,1024]{2,0,1:T(8,128)(2,1)}, u32[]{:S(2)}, u32[]{:S(2)}) async-start(bf16[192,4,1024]{2,0,1:T(8,128)(2,1)} %bitcast.75), calls=%async_computation | async-start | bytes 3145728 | tf_op jit(solution)/shard_map/all_to_all | solution.py:318
  25.7 16.4 %copy-start.18 = (s32[1,64]{1,0:T(1,128)}, s32[1,64]{1,0:T(1,128)S(1)}, u32[]{:S(2)}) copy-start(s32[1,64]{1,0:T(1,128)S(1)} %get-tuple-element.37) | copy-start | bytes 772
  42.1 3.2 %copy-start.26 = (s32[64]{0:T(128)S(1)}, s32[64]{0:T(128)}, u32[]{:S(2)}) copy-start(s32[64]{0:T(128)} %select_reduce_fusion.2) | copy-start | bytes 772
  42.1 3.2 %copy-start.19 = (s32[1,64]{1,0:T(1,128)S(1)}, s32[1,64]{1,0:T(1,128)}, u32[]{:S(2)}) copy-start(s32[1,64]{1,0:T(1,128)} %copy-done.18) | copy-start | bytes 772
  42.1 79.3 %collective-permute-start.3 = (bf16[768,1024]{1,0:T(8,128)(2,1)}, bf16[768,1024]{1,0:T(8,128)(2,1)S(1)}, u32[]{:S(2)}, u32[]{:S(2)}) collective-permute-start(bf16[768,1024]{1,0:T(8,128)(2,1)} %bitcast.5.own_ref), channel_id=1, source_target_pairs={{0,4},{4,0},{8,12},{12,8},{16,20},{20,16},{24,28},{28,24},{1,5},{5... | collective-permute-start | bytes 4718600 | tf_op jit(solution)/shard_map/ppermute | solution.py:22
  44.6 40.6 %collective-permute-start.16 = (bf16[40,64,128]{2,1,0:T(8,128)(2,1)}, bf16[40,64,128]{2,1,0:T(8,128)(2,1)S(1)}, u32[]{:S(2)}, u32[]{:S(2)}) collective-permute-start(bf16[40,64,128]{2,1,0:T(8,128)(2,1)} %get-tuple-element.42), channel_id=1, source_target_pairs={{1,2},{2,1},{5,6},{6,5},{9,10},{10,9},{13,14},{14,13},{17,18},{18,... | collective-permute-start | bytes 1966088 | tf_op jit(solution)/shard_map/ppermute | solution.py:299
  45.9 41.3 %collective-permute-start.15 = (bf16[40,64,128]{2,1,0:T(8,128)(2,1)}, bf16[40,64,128]{2,1,0:T(8,128)(2,1)}, u32[]{:S(2)}, u32[]{:S(2)}) collective-permute-start(bf16[40,64,128]{2,1,0:T(8,128)(2,1)} %get-tuple-element.43), channel_id=1, source_target_pairs={{1,2},{2,1},{5,6},{6,5},{9,10},{10,9},{13,14},{14,13},{17,18},{18,... | collective-permute-start | bytes 1966088 | tf_op jit(solution)/shard_map/ppermute | solution.py:299
  47.5 31.7 %collective-permute-start.5 = (f32[64,128]{1,0:T(8,128)}, f32[64,128]{1,0:T(8,128)}, u32[]{:S(2)}, u32[]{:S(2)}) collective-permute-start(f32[64,128]{1,0:T(8,128)} %bitcast.13), channel_id=1, source_target_pairs={{0,2},{1,3},{2,0},{3,1},{4,6},{5,7},{6,4},{7,5},{8,10},{9,11},{10,... | collective-permute-start | bytes 98312 | tf_op jit(solution)/shard_map/ppermute | solution.py:22
  53.7 28.5 %copy-start.24 = (s32[1,64]{1,0:T(1,128)S(1)}, s32[1,64]{1,0:T(1,128)}, u32[]{:S(2)}) copy-start(s32[1,64]{1,0:T(1,128)} %get-tuple-element.53) | copy-start | bytes 772
  79.2 31.2 %collective-permute-start.2 = (bf16[2,128,768]{2,1,0:T(8,128)(2,1)}, bf16[2,128,768]{2,1,0:T(8,128)(2,1)}, u32[]{:S(2)}, u32[]{:S(2)}) collective-permute-start(bf16[2,128,768]{2,1,0:T(8,128)(2,1)} %copy.34), channel_id=1, source_target_pairs={{0,8},{4,12},{8,0},{12,4},{16,24},{20,28},{24,16},{28,20},{1,9},{5... | collective-permute-start | bytes 1179656 | tf_op jit(solution)/shard_map/ppermute | solution.py:22
  80.7 2.8 %copy-start.1 = (bf16[2,40,64,128]{3,2,1,0:T(8,128)(2,1)}, bf16[2,40,64,128]{3,2,1,0:T(8,128)(2,1)S(1)}, u32[]{:S(2)}) copy-start(bf16[2,40,64,128]{3,2,1,0:T(8,128)(2,1)S(1)} %collective-permute-done.14.refs_1_.refs_2_) | copy-start | bytes 3932164
  80.7 30.9 %collective-permute-start.1 = (bf16[2,128,768]{2,1,0:T(8,128)(2,1)}, bf16[2,128,768]{2,1,0:T(8,128)(2,1)}, u32[]{:S(2)}, u32[]{:S(2)}) collective-permute-start(bf16[2,128,768]{2,1,0:T(8,128)(2,1)} %copy.34), channel_id=1, source_target_pairs={{0,16},{4,20},{8,24},{12,28},{16,0},{20,4},{24,8},{28,12},{1,17},{... | collective-permute-start | bytes 1179656 | tf_op jit(solution)/shard_map/ppermute | solution.py:22
  83.5 3.1 %copy-start.20 = (s32[64]{0:T(128)S(1)}, s32[64]{0:T(128)}, u32[]{:S(2)}) copy-start(s32[64]{0:T(128)} %get-tuple-element.47) | copy-start | bytes 772
  83.5 3.1 %copy-start.21 = (s32[64]{0:T(128)S(1)}, s32[64]{0:T(128)}, u32[]{:S(2)}) copy-start(s32[64]{0:T(128)} %get-tuple-element.48) | copy-start | bytes 772
  83.5 3.1 %copy-start.22 = (s32[64]{0:T(128)S(1)}, s32[64]{0:T(128)}, u32[]{:S(2)}) copy-start(s32[64]{0:T(128)} %get-tuple-element.49) | copy-start | bytes 772
  83.5 3.1 %copy-start.23 = (s32[64]{0:T(128)S(1)}, s32[64]{0:T(128)}, u32[]{:S(2)}) copy-start(s32[64]{0:T(128)} %get-tuple-element.50) | copy-start | bytes 772
  85.2 5.6 %copy-start.4 = (bf16[40,64,128]{2,1,0:T(8,128)(2,1)}, bf16[40,64,128]{2,1,0:T(8,128)(2,1)S(1)}, u32[]{:S(2)}) copy-start(bf16[40,64,128]{2,1,0:T(8,128)(2,1)S(1)} %collective-permute-done.16.refs_3_.refs_4_) | copy-start | bytes 1966084
  85.2 45.7 %collective-permute-start.17 = (bf16[2,32,64,128]{3,2,1,0:T(8,128)(2,1)}, bf16[2,32,64,128]{3,2,1,0:T(8,128)(2,1)}, u32[]{:S(2)}, u32[]{:S(2)}) collective-permute-start(bf16[2,32,64,128]{3,2,1,0:T(8,128)(2,1)} %pack.3), channel_id=1, source_target_pairs={{2,3},{1,0},{6,7},{5,4},{10,11},{9,8},{14,15},{13,12},{18,19},{17,... | collective-permute-start | bytes 3145736 | tf_op jit(solution)/shard_map/ppermute | solution.py:312
  87.2 22.6 %collective-permute-start.4 = (f32[64,128]{1,0:T(8,128)}, f32[64,128]{1,0:T(8,128)}, u32[]{:S(2)}, u32[]{:S(2)}) collective-permute-start(f32[64,128]{1,0:T(8,128)} %bitcast.13), channel_id=1, source_target_pairs={{0,1},{1,0},{2,3},{3,2},{4,5},{5,4},{6,7},{7,6},{8,9},{9,8},{10,11... | collective-permute-start | bytes 98312 | tf_op jit(solution)/shard_map/ppermute | solution.py:22
  92.4 20.8 %copy-start.25 = (s32[256]{0:T(256)S(1)}, s32[256]{0:T(256)}, u32[]{:S(2)}) copy-start(s32[256]{0:T(256)} %pad_add_fusion) | copy-start | bytes 3076
  92.4 21.8 %copy-start = (bf16[2,40,64,128]{3,2,1,0:T(8,128)(2,1)S(1)}, bf16[2,40,64,128]{3,2,1,0:T(8,128)(2,1)}, u32[]{:S(2)}) copy-start(bf16[2,40,64,128]{3,2,1,0:T(8,128)(2,1)} %probs.1.refs_0_) | copy-start | bytes 3932164
  109.9 9.0 %collective-permute-start = (bf16[2,128,768]{2,1,0:T(8,128)(2,1)}, bf16[2,128,768]{2,1,0:T(8,128)(2,1)}, u32[]{:S(2)}, u32[]{:S(2)}) collective-permute-start(bf16[2,128,768]{2,1,0:T(8,128)(2,1)} %copy.34), channel_id=1, source_target_pairs={{0,24},{4,28},{8,16},{12,20},{16,8},{20,12},{24,0},{28,4},{1,25},{... | collective-permute-start | bytes 1179656 | tf_op jit(solution)/shard_map/ppermute | solution.py:22
  110.3 23.7 %collective-permute-start.18 = (bf16[1,32,64,128]{3,2,1,0:T(8,128)(2,1)}, bf16[1,32,64,128]{3,2,1,0:T(8,128)(2,1)S(1)}, u32[]{:S(2)}, u32[]{:S(2)}) collective-permute-start(bf16[1,32,64,128]{3,2,1,0:T(8,128)(2,1)} %pack.4), channel_id=1, source_target_pairs={{2,3},{1,0},{6,7},{5,4},{10,11},{9,8},{14,15},{13,12},{18,19},{17,... | collective-permute-start | bytes 1572872 | tf_op jit(solution)/shard_map/ppermute | solution.py:312
  111.6 22.4 %collective-permute-start.19 = (bf16[1,32,64,128]{3,2,1,0:T(8,128)(2,1)}, bf16[1,32,64,128]{3,2,1,0:T(8,128)(2,1)}, u32[]{:S(2)}, u32[]{:S(2)}) collective-permute-start(bf16[1,32,64,128]{3,2,1,0:T(8,128)(2,1)} %pack.5), channel_id=1, source_target_pairs={{2,3},{1,0},{6,7},{5,4},{10,11},{9,8},{14,15},{13,12},{18,19},{17,... | collective-permute-start | bytes 1572872 | tf_op jit(solution)/shard_map/ppermute | solution.py:312
  121.4 1.2 copy-start.3
  129.6 16.8 %collective-permute-start.9 = (f32[9,128]{1,0:T(8,128)S(1)}, f32[9,128]{1,0:T(8,128)S(1)}, u32[]{:S(2)}, u32[]{:S(2)}) collective-permute-start(f32[9,128]{1,0:T(8,128)S(1)} %pad_maximum_fusion.1), channel_id=1, source_target_pairs={{0,3},{1,2},{2,1},{3,0},{4,7},{5,6},{6,5},{7,4},{8,11},{9,10},{10,... | collective-permute-start | bytes 13832 | tf_op jit(solution)/shard_map/ppermute | solution.py:22
  131.0 17.0 %collective-permute-start.8 = (f32[9,128]{1,0:T(8,128)S(1)}, f32[9,128]{1,0:T(8,128)S(1)}, u32[]{:S(2)}, u32[]{:S(2)}) collective-permute-start(f32[9,128]{1,0:T(8,128)S(1)} %pad_maximum_fusion.1), channel_id=1, source_target_pairs={{0,2},{1,3},{2,0},{3,1},{4,6},{5,7},{6,4},{7,5},{8,10},{9,11},{10,... | collective-permute-start | bytes 13832 | tf_op jit(solution)/shard_map/ppermute | solution.py:22
  131.0 17.0 %collective-permute-start.7 = (f32[9,128]{1,0:T(8,128)S(1)}, f32[9,128]{1,0:T(8,128)S(1)}, u32[]{:S(2)}, u32[]{:S(2)}) collective-permute-start(f32[9,128]{1,0:T(8,128)S(1)} %pad_maximum_fusion.1), channel_id=1, source_target_pairs={{0,1},{1,0},{2,3},{3,2},{4,5},{5,4},{6,7},{7,6},{8,9},{9,8},{10,11... | collective-permute-start | bytes 13832 | tf_op jit(solution)/shard_map/ppermute | solution.py:22
  134.0 0.8 copy-start.6
  139.6 20.3 %collective-permute-start.21 = (bf16[128,1024]{1,0:T(8,128)(2,1)}, bf16[128,1024]{1,0:T(8,128)(2,1)S(1)}, u32[]{:S(2)}, u32[]{:S(2)}) collective-permute-start(bf16[128,1024]{1,0:T(8,128)(2,1)} %get-tuple-element.22), channel_id=1, source_target_pairs={{0,24},{4,28},{8,16},{12,20},{16,8},{20,12},{24,0},{28,4},{1,25},{... | collective-permute-start | bytes 786440 | tf_op jit(solution)/shard_map/ppermute | solution.py:22
  140.7 7.2 %copy-start.12 = (f32[2,4,128]{2,1,0:T(4,128)S(1)}, f32[2,4,128]{2,1,0:T(4,128)}, u32[]{:S(2)}) copy-start(f32[2,4,128]{2,1,0:T(4,128)} %get-tuple-element.17.own_ref) | copy-start | bytes 12292
  140.8 7.3 %copy-start.27 = (f32[128]{0:T(128)S(1)}, f32[128]{0:T(128)}, u32[]{:S(2)}) copy-start(f32[128]{0:T(128)} %param.13) | copy-start | bytes 1540
  140.8 19.2 %collective-permute-start.22 = (bf16[128,1024]{1,0:T(8,128)(2,1)}, bf16[128,1024]{1,0:T(8,128)(2,1)S(1)}, u32[]{:S(2)}, u32[]{:S(2)}) collective-permute-start(bf16[128,1024]{1,0:T(8,128)(2,1)} %get-tuple-element.23), channel_id=1, source_target_pairs={{0,16},{4,20},{8,24},{12,28},{16,0},{20,4},{24,8},{28,12},{1,17},{... | collective-permute-start | bytes 786440 | tf_op jit(solution)/shard_map/ppermute | solution.py:22
  146.4 19.7 %collective-permute-start.20 = (bf16[128,1024]{1,0:T(8,128)(2,1)}, bf16[128,1024]{1,0:T(8,128)(2,1)S(1)}, u32[]{:S(2)}, u32[]{:S(2)}) collective-permute-start(bf16[128,1024]{1,0:T(8,128)(2,1)} %get-tuple-element.20), channel_id=1, source_target_pairs={{0,8},{4,12},{8,0},{12,4},{16,24},{20,28},{24,16},{28,20},{1,9},{5... | collective-permute-start | bytes 786440 | tf_op jit(solution)/shard_map/ppermute | solution.py:22
  148.1 9.4 %copy-start.13 = (f32[10,128]{1,0:T(8,128)}, f32[10,128]{1,0:T(8,128)S(1)}, u32[]{:S(2)}) copy-start(f32[10,128]{1,0:T(8,128)S(1)} %pad_maximum_fusion.2.refs_0_) | copy-start | bytes 15364
  148.1 5.8 %collective-permute-start.12 = (f32[10,128]{1,0:T(8,128)S(1)}, f32[10,128]{1,0:T(8,128)S(1)}, u32[]{:S(2)}, u32[]{:S(2)}) collective-permute-start(f32[10,128]{1,0:T(8,128)S(1)} %pad_maximum_fusion.2.refs_0_), channel_id=1, source_target_pairs={{0,24},{4,28},{8,16},{12,20},{16,8},{20,12},{24,0},{28,4},{1,25},{... | collective-permute-start | bytes 15368 | tf_op jit(solution)/shard_map/ppermute | solution.py:22
  149.2 5.4 %collective-permute-start.11 = (f32[10,128]{1,0:T(8,128)S(1)}, f32[10,128]{1,0:T(8,128)S(1)}, u32[]{:S(2)}, u32[]{:S(2)}) collective-permute-start(f32[10,128]{1,0:T(8,128)S(1)} %pad_maximum_fusion.2.refs_0_), channel_id=1, source_target_pairs={{0,16},{4,20},{8,24},{12,28},{16,0},{20,4},{24,8},{28,12},{1,17},{... | collective-permute-start | bytes 15368 | tf_op jit(solution)/shard_map/ppermute | solution.py:22
  153.8 3.7 %copy-start.15 = (f32[10,128]{1,0:T(8,128)}, f32[10,128]{1,0:T(8,128)S(1)}, u32[]{:S(2)}) copy-start(f32[10,128]{1,0:T(8,128)S(1)} %collective-permute-done.12.refs_3_) | copy-start | bytes 15364
  153.8 3.7 %collective-permute-start.10 = (f32[10,128]{1,0:T(8,128)S(1)}, f32[10,128]{1,0:T(8,128)S(1)}, u32[]{:S(2)}, u32[]{:S(2)}) collective-permute-start(f32[10,128]{1,0:T(8,128)S(1)} %pad_maximum_fusion.2.refs_0_), channel_id=1, source_target_pairs={{0,8},{4,12},{8,0},{12,4},{16,24},{20,28},{24,16},{28,20},{1,9},{5... | collective-permute-start | bytes 15368 | tf_op jit(solution)/shard_map/ppermute | solution.py:22
  154.7 2.8 %copy-start.16 = (f32[10,128]{1,0:T(8,128)}, f32[10,128]{1,0:T(8,128)S(1)}, u32[]{:S(2)}) copy-start(f32[10,128]{1,0:T(8,128)S(1)} %collective-permute-done.11.refs_2_) | copy-start | bytes 15364
  157.5 0.6 copy-start.17
  159.9 0.7 copy-start.9
  159.9 0.8 copy-start.10
  166.2 0.7 copy-start.11
  166.9 5.6 %copy-start.5 = (bf16[2,512,768]{2,1,0:T(8,128)(2,1)S(1)}, bf16[2,512,768]{2,1,0:T(8,128)(2,1)}, u32[]{:S(2)}) copy-start(bf16[2,512,768]{2,1,0:T(8,128)(2,1)} %pad_maximum_fusion.x_ref) | copy-start | bytes 4718596
  175.9 3.6 %collective-permute-start.29 = (bf16[768,1024]{1,0:T(8,128)(2,1)}, bf16[768,1024]{1,0:T(8,128)(2,1)S(1)}, u32[]{:S(2)}, u32[]{:S(2)}) collective-permute-start(bf16[768,1024]{1,0:T(8,128)(2,1)} %convolution_convert_fusion), channel_id=1, source_target_pairs={{0,4},{4,0},{8,12},{12,8},{16,20},{20,16},{24,28},{28,24},{1,5},{5... | collective-permute-start | bytes 4718600 | tf_op jit(solution)/shard_map/ppermute | solution.py:22
  181.3 3.7 %copy-start.30 = (bf16[2,128,768]{2,1,0:T(8,128)(2,1)S(1)}, bf16[2,128,768]{2,1,0:T(8,128)(2,1)}, u32[]{:S(2)}) copy-start(bf16[2,128,768]{2,1,0:T(8,128)(2,1)} %get-tuple-element.28) | copy-start | bytes 1179652
  181.3 5.7 %copy-start.29 = (bf16[2,128,768]{2,1,0:T(8,128)(2,1)S(1)}, bf16[2,128,768]{2,1,0:T(8,128)(2,1)}, u32[]{:S(2)}) copy-start(bf16[2,128,768]{2,1,0:T(8,128)(2,1)} %get-tuple-element.26) | copy-start | bytes 1179652
  181.3 7.2 %copy-start.28 = (bf16[2,128,768]{2,1,0:T(8,128)(2,1)S(1)}, bf16[2,128,768]{2,1,0:T(8,128)(2,1)}, u32[]{:S(2)}) copy-start(bf16[2,128,768]{2,1,0:T(8,128)(2,1)} %get-tuple-element.27) | copy-start | bytes 1179652
  181.3 41.3 %copy-start.8 = (bf16[2,128,768]{2,1,0:T(8,128)(2,1)S(1)}, bf16[2,128,768]{2,1,0:T(8,128)(2,1)}, u32[]{:S(2)}) copy-start(bf16[2,128,768]{2,1,0:T(8,128)(2,1)} %get-tuple-element.25) | copy-start | bytes 1179652
  181.3 54.1 %all-to-all-start.1 = ((bf16[4,192,1024]{2,1,0:T(8,128)(2,1)}), bf16[4,192,1024]{2,1,0:T(8,128)(2,1)S(1)}, u32[]{:S(2)}, u32[]{:S(2)}) async-start(bf16[4,192,1024]{2,1,0:T(8,128)(2,1)} %bitcast.33), calls=%async_computation.1 | async-start | bytes 3145728 | tf_op jit(solution)/shard_map/all_to_all | solution.py:377
  185.0 29.0 %collective-permute-start.25 = (bf16[2,128,768]{2,1,0:T(8,128)(2,1)S(1)}, bf16[2,128,768]{2,1,0:T(8,128)(2,1)S(1)}, u32[]{:S(2)}, u32[]{:S(2)}) collective-permute-start(bf16[2,128,768]{2,1,0:T(8,128)(2,1)S(1)} %copy-done.30), channel_id=1, source_target_pairs={{0,8},{4,12},{8,0},{12,4},{16,24},{20,28},{24,16},{28,20},{1,9},{5... | collective-permute-start | bytes 1179656 | tf_op jit(solution)/shard_map/ppermute | solution.py:22
  187.0 35.6 %collective-permute-start.23 = (bf16[2,128,768]{2,1,0:T(8,128)(2,1)S(1)}, bf16[2,128,768]{2,1,0:T(8,128)(2,1)S(1)}, u32[]{:S(2)}, u32[]{:S(2)}) collective-permute-start(bf16[2,128,768]{2,1,0:T(8,128)(2,1)S(1)} %copy-done.29), channel_id=1, source_target_pairs={{0,24},{4,28},{8,16},{12,20},{16,8},{20,12},{24,0},{28,4},{1,25},{... | collective-permute-start | bytes 1179656 | tf_op jit(solution)/shard_map/ppermute | solution.py:22
  188.5 34.1 %collective-permute-start.24 = (bf16[2,128,768]{2,1,0:T(8,128)(2,1)S(1)}, bf16[2,128,768]{2,1,0:T(8,128)(2,1)S(1)}, u32[]{:S(2)}, u32[]{:S(2)}) collective-permute-start(bf16[2,128,768]{2,1,0:T(8,128)(2,1)S(1)} %copy-done.28), channel_id=1, source_target_pairs={{0,16},{4,20},{8,24},{12,28},{16,0},{20,4},{24,8},{28,12},{1,17},{... | collective-permute-start | bytes 1179656 | tf_op jit(solution)/shard_map/ppermute | solution.py:22
  223.1 5.9 %collective-permute-start.26 = (bf16[128,384]{0,1:T(8,128)(2,1)S(1)}, bf16[128,384]{0,1:T(8,128)(2,1)S(1)}, u32[]{:S(2)}, u32[]{:S(2)}) collective-permute-start(bf16[128,384]{0,1:T(8,128)(2,1)S(1)} %get-tuple-element.44), channel_id=1, source_target_pairs={{0,1},{1,0},{2,3},{3,2},{4,5},{5,4},{6,7},{7,6},{8,9},{9,8},{10,11... | collective-permute-start | bytes 294920 | tf_op jit(solution)/shard_map/ppermute | solution.py:22
  223.2 7.2 %collective-permute-start.28 = (bf16[128,384]{0,1:T(8,128)(2,1)S(1)}, bf16[128,384]{0,1:T(8,128)(2,1)S(1)}, u32[]{:S(2)}, u32[]{:S(2)}) collective-permute-start(bf16[128,384]{0,1:T(8,128)(2,1)S(1)} %get-tuple-element.45), channel_id=1, source_target_pairs={{0,3},{1,2},{2,1},{3,0},{4,7},{5,6},{6,5},{7,4},{8,11},{9,10},{10,... | collective-permute-start | bytes 294920 | tf_op jit(solution)/shard_map/ppermute | solution.py:22
  224.6 10.0 %collective-permute-start.27 = (bf16[128,384]{0,1:T(8,128)(2,1)S(1)}, bf16[128,384]{0,1:T(8,128)(2,1)S(1)}, u32[]{:S(2)}, u32[]{:S(2)}) collective-permute-start(bf16[128,384]{0,1:T(8,128)(2,1)S(1)} %get-tuple-element.46), channel_id=1, source_target_pairs={{0,2},{1,3},{2,0},{3,1},{4,6},{5,7},{6,4},{7,5},{8,10},{9,11},{10,... | collective-permute-start | bytes 294920 | tf_op jit(solution)/shard_map/ppermute | solution.py:22

commit v2 on v1

v2 whole, which is shorter than its diff:
```python
import functools

import jax
import jax.numpy as jnp
from jax import lax
from jax.experimental import pallas as pl
from jax.experimental.pallas import tpu as pltpu
from jax.sharding import PartitionSpec as P


BLOCK = 128
K = 2
SPLIT = (64, 64)
HALVES = len(SPLIT)

ANY = pl.BlockSpec(memory_space=pl.ANY)
VMEM = pl.BlockSpec(memory_space=pltpu.VMEM)
F32 = jnp.float32
BF16 = jnp.bfloat16


def swap(x, axis, bits):
    return lax.ppermute(x, axis, [(i, i ^ bits) for i in range(lax.axis_size(axis))])


def parts_of(tokens):
    return [tokens * sum(SPLIT[:n]) // sum(SPLIT) for n in range(HALVES + 1)]


def probs_kernel(peers, tab_ref, x_ref, *out_refs):
    count = len(out_refs) // HALVES
    ends = parts_of(x_ref.shape[0])

    def block(at):
        return jnp.exp(x_ref[:, pl.ds(pl.multiple_of(at * BLOCK, BLOCK), BLOCK)]).astype(BF16)

    def store(list_number, slot, value):
        for n in range(HALVES):
            out_refs[n * count + list_number][slot] = value[ends[n] : ends[n + 1]]

    def convert(slot, carry):
        store(0, slot, block(slot))
        return carry

    lax.fori_loop(0, out_refs[0].shape[0], convert, 0)
    for t in range(1, peers):

        def copy(slot, carry, t=t):
            at = tab_ref[2 + t, slot]
            for n in range(HALVES):
                out_refs[n * count + t][slot] = out_refs[n * count][at]
            return carry

        lax.fori_loop(0, out_refs[t].shape[0], copy, 0)


def teacher_lists(tab, logprobs, peers, length):
    tokens, cols = logprobs.shape
    ends = parts_of(tokens)
    lengths = [cols // BLOCK] + [length] * (peers - 1)
    shapes = [(n, y - x, BLOCK) for x, y in zip(ends, ends[1:]) for n in lengths]
    return pl.pallas_call(
        functools.partial(probs_kernel, peers),
        grid_spec=pltpu.PrefetchScalarGridSpec(
            num_scalar_prefetch=1, grid=(), in_specs=[VMEM], out_specs=[VMEM] * len(shapes)
        ),
        out_shape=[jax.ShapeDtypeStruct(shape, BF16) for shape in shapes],
        name="probs",
    )(tab, logprobs)


def mapped_kernel(pieces, tab_ref, *refs):
    sources, tiles_ref, outs = refs[: -len(pieces) - 3], refs[-len(pieces) - 3], refs[-len(pieces) - 2 : -2]
    buf, sem = refs[-2], refs[-1]
    me = tab_ref[2, 0]
    per = outs[0].shape[1] // BLOCK

    def start(p, carry):
        source, block = tab_ref[0, p], tab_ref[1, p]
        for i, ref in enumerate(sources):

            @pl.when(source == i)
            def _(ref=ref):
                pltpu.make_async_copy(ref.at[block], buf.at[p], sem).start()

        return carry

    lax.fori_loop(0, buf.shape[0], start, 0)
    pltpu.make_async_copy(buf, buf, sem).wait()
    for piece, out in zip(pieces, outs):
        dest = lax.bitwise_xor(me, piece)
        for j in range(per):
            b = dest * per + j
            total = jnp.dot(buf[K * b], tiles_ref[b, 0], preferred_element_type=F32)
            for k in range(1, K):
                total += jnp.dot(buf[K * b + k], tiles_ref[b, k], preferred_element_type=F32)
            out[:, j * BLOCK : (j + 1) * BLOCK] = total.astype(BF16)


def mapped_parts(tab, sources, tiles, pieces):
    rows = sources[0].shape[1]
    cols = tiles.shape[0] * BLOCK // len(pieces)
    return pl.pallas_call(
        functools.partial(mapped_kernel, pieces),
        grid_spec=pltpu.PrefetchScalarGridSpec(
            num_scalar_prefetch=1,
            grid=(),
            in_specs=[ANY] * len(sources) + [VMEM],
            out_specs=[VMEM] * len(pieces),
            scratch_shapes=[pltpu.VMEM((tab.shape[1], rows, BLOCK), BF16), pltpu.SemaphoreType.DMA],
        ),
        out_shape=[jax.ShapeDtypeStruct((rows, cols), BF16)] * len(pieces),
        name="mapped",
    )(tab, *sources, tiles)


def turned(x):
    n = max(x.shape)
    full = jnp.broadcast_to(x, (n, n)).T
    return full[:, :1] if x.shape[0] == 1 else full[:1]


def logits_kernel(core_ref, x_ref, own_ref, other_ref, e_ref, s_ref):
    i, c = pl.program_id(0), core_ref[0]
    logits = jnp.dot(x_ref[c], own_ref[...], preferred_element_type=F32)
    logits += jnp.dot(x_ref[1 - c], other_ref[...], preferred_element_type=F32)
    top = jnp.max(logits, axis=1, keepdims=True)
    e = jnp.exp(logits - top)
    e_ref[0] = e
    s_ref[0, pl.ds(i, 1)] = turned(top)
    s_ref[1, pl.ds(i, 1)] = turned(jnp.sum(e, axis=1, keepdims=True))


def logits_parts(core, hidden, own, other, tokens):
    chips = hidden.shape[1] // tokens
    features, cols = own.shape
    fixed = pl.BlockSpec((features, cols), lambda i, core: (0, 0))
    return pl.pallas_call(
        logits_kernel,
        grid_spec=pltpu.PrefetchScalarGridSpec(
            num_scalar_prefetch=1,
            grid=(chips,),
            in_specs=[pl.BlockSpec((2, tokens, features), lambda i, core: (0, i, 0)), fixed, fixed],
            out_specs=[
                pl.BlockSpec((1, tokens, cols), lambda i, core: (i, 0, 0)),
                pl.BlockSpec((2, chips, tokens), lambda i, core: (0, 0, 0)),
            ],
        ),
        out_shape=[
            jax.ShapeDtypeStruct((chips, tokens, cols), F32),
            jax.ShapeDtypeStruct((2, chips, tokens), F32),
        ],
        name="logits",
    )(core, hidden, own, other)


def stats_kernel(order, own_ref, *refs):
    shares, a_ref, b_ref = refs[:-2], refs[-2], refs[-1]
    chips = len(shares)
    for k, piece in enumerate(order):
        rows = [order.index(piece ^ r) for r in range(chips)]
        tops = [shares[r][j : j + 1] for r, j in enumerate(rows)]
        top = functools.reduce(jnp.maximum, tops)
        total = sum(shares[r][chips + j : chips + j + 1] * jnp.exp(tops[r] - top) for r, j in enumerate(rows))
        mass = shares[piece][2 * chips : 2 * chips + 1]
        scale = shares[piece][2 * chips + 1 : 2 * chips + 2]
        a_ref[k] = turned(scale * mass * (jnp.exp(own_ref[0, k : k + 1] - top) / total))
        b_ref[k] = turned(scale)


def grads_kernel(core_ref, e_ref, a_ref, b_ref, own_ref, other_ref, *refs):
    count = e_ref.shape[0]
    mapped, dl_ref, outs = refs[:count], refs[-count - 1], refs[-count:]
    c = core_ref[0]
    for k in range(count):
        dl_ref[k] = (a_ref[k] * e_ref[k] - b_ref[k] * mapped[k][...].astype(F32)).astype(BF16)
    rows = dl_ref.shape[1]
    dl = dl_ref[...].reshape(count * rows, -1)
    for half, weight in ((c, own_ref), (1 - c, other_ref)):
        terms = lax.dot_general(dl, weight[...], (((1,), (1,)), ((), ())), preferred_element_type=F32)
        for k in range(count):
            outs[k][half] = terms[k * rows : (k + 1) * rows].astype(BF16)


def grads(part, core, e, a, b, own, other, mapped, dl):
    count, rows = len(mapped), mapped[0].shape[0]
    features, cols = own.shape
    at = parts_of(e.shape[1])[part] // rows
    some = lambda n: pl.BlockSpec((count, rows, n), lambda i, core: (0, at, 0))
    whole = lambda *shape: pl.BlockSpec(shape, lambda i, core: (0,) * len(shape))
    return pl.pallas_call(
        grads_kernel,
        grid_spec=pltpu.PrefetchScalarGridSpec(
            num_scalar_prefetch=1,
            grid=(1,),
            in_specs=[some(cols), some(1), some(1), whole(features, cols), whole(features, cols)]
            + [whole(rows, cols)] * count
            + ([] if dl is None else [ANY]),
            out_specs=[some(cols)] + [whole(2, rows, features)] * count,
        ),
        out_shape=[jax.ShapeDtypeStruct(e.shape, BF16)]
        + [jax.ShapeDtypeStruct((2, rows, features), BF16)] * count,
        input_output_aliases={} if dl is None else {6 + count: 0},
        name="grads",
    )(core, e, a, b, own, other, *mapped, *([] if dl is None else [dl]))


def plan(align_index, pairs, count, chip):
    vocab = lax.axis_size("vocab")
    v = lax.axis_index("vocab")
    rows = align_index.reshape(vocab, pairs)
    owner, local = lax.div(rows, jnp.int32(count)), lax.rem(rows, jnp.int32(count))
    number = jnp.arange(pairs)
    same = rows[:, :, None] == rows[:, None, :]
    first = ~jnp.any(same & (number[None, None, :] < number[None, :, None]), axis=2)
    less = (owner[:, :, None] == owner[:, None, :]) & (rows[:, None, :] < rows[:, :, None]) & first[:, None, :]
    rank = jnp.sum(less.astype(jnp.int32), axis=2)
    here = jnp.arange(vocab)[:, None]
    longest = jnp.max(jnp.where(owner != here, rank + 1, 0))
    pick = lambda x, i: lax.dynamic_index_in_dim(x, i, 0, keepdims=False)
    own_owner = pick(owner, v)
    source = own_owner ^ v
    place = jnp.where(own_owner == v, pick(local, v), pick(rank, v))
    asked = (owner == v)[:, None, :] & (rank[:, None, :] == number[None, :, None]) & first[:, None, :]
    lists = jnp.sum(jnp.where(asked, local[:, None, :], 0), axis=2)
    mine = jnp.where(number == 0, chip, 0)
    tab = jnp.stack([source, place, mine] + [pick(lists, v ^ t) for t in range(1, vocab)])
    return tab.astype(jnp.int32), longest


def body(student_hidden, head_weight, teacher_logprobs, align_index, align_tiles, grad_scale):
    vocab = lax.axis_size("vocab")
    chips = lax.axis_size("dp") // 2
    count = teacher_logprobs.shape[1] // BLOCK
    pairs = align_tiles.shape[0] * K
    capacity = (2 * pairs + vocab - 1) // vocab
    if vocab & (vocab - 1) or chips & (chips - 1):
        raise ValueError("mesh sizes")
    tab, longest = plan(align_index, pairs, count, lax.axis_index("dp") // 2)
    operands = (student_hidden, head_weight, teacher_logprobs, align_index, align_tiles, grad_scale, tab)
    lengths = (3 * capacity // 4, capacity)

    def branch(n):
        def run(*args):
            return step(lengths[n], *args)

        return run

    return lax.cond(longest <= lengths[0], branch(0), branch(1), *operands)


def step(length, student_hidden, head_weight, teacher_logprobs, align_index, align_tiles, grad_scale, tab):
    vocab = lax.axis_size("vocab")
    dp = lax.axis_size("dp")
    v = lax.axis_index("vocab")
    d = lax.axis_index("dp")
    chips, c = dp // 2, d % 2
    core = c.astype(jnp.int32)[None]
    tokens, features = student_hidden.shape
    count = teacher_logprobs.shape[1] // BLOCK
    pairs = align_tiles.shape[0] * K
    groups = [[2 * i + j for i in range(chips)] for j in range(2)]

    lists = teacher_lists(tab, teacher_logprobs, vocab, length)
    lists = [lists[n * vocab : (n + 1) * vocab] for n in range(HALVES)]
    blocks, sources = [x[0] for x in lists], []
    for n in range(HALVES):
        got = []
        for t in range(1, vocab):
            got.append(swap(lists[n][t], "vocab", t))
        sources.append([blocks[n]] + got)

    weight_own = lax.all_to_all(head_weight, "dp", split_axis=1, concat_axis=0, axis_index_groups=groups, tiled=True)
    weight_other = swap(weight_own, "dp", 1)

    hidden = student_hidden.reshape(tokens, chips, 2, features // dp).transpose(2, 0, 1, 3)
    hidden = lax.optimization_barrier(hidden.reshape(2, tokens, features // 2))
    others = [swap(hidden, "dp", 2 * j) for j in range(1, chips)]
    order = list(range(chips))[::-1]
    hidden = jnp.concatenate(others[::-1] + [hidden], axis=1)
    e, local = logits_parts(core, hidden, weight_own, weight_other, tokens)

    row_sums = jnp.sum(align_tiles.astype(F32), axis=3).reshape(pairs, BLOCK)
    all_sums = [row_sums] + [swap(row_sums, "vocab", t) for t in range(1, vocab)]
    rows = align_index.reshape(vocab, pairs)
    all_rows = [lax.dynamic_index_in_dim(rows, v ^ t, 0, keepdims=False) for t in range(vocab)]
    hits = (jnp.concatenate(all_rows)[None, :] == (v * count + jnp.arange(count))[:, None]).astype(F32)
    entry_weight = jnp.dot(hits, jnp.concatenate(all_sums), precision=lax.Precision.HIGHEST)
    mass = jnp.concatenate(
        [jnp.sum(part.astype(F32) * entry_weight[:, None, :], axis=(0, 2)) for part in blocks]
    )

    share = jnp.concatenate([local.reshape(2 * chips, tokens), mass[None]])
    shares = [share] + [swap(share, "vocab", t) for t in range(1, vocab)]
    plane_top = functools.reduce(jnp.maximum, [s[:chips] for s in shares])
    plane_total = sum(s[chips : 2 * chips] * jnp.exp(s[:chips] - plane_top) for s in shares)
    plane_mass = sum(s[2 * chips] for s in shares)
    share = jnp.concatenate([plane_top, plane_total, plane_mass[None], grad_scale[None]])
    shares = [share] + [swap(share, "dp", 2 * j) for j in range(1, chips)]
    column = jax.ShapeDtypeStruct((chips, tokens, 1), F32)
    a, b = pl.pallas_call(
        functools.partial(stats_kernel, order),
        in_specs=[VMEM] * (chips + 1),
        out_specs=[VMEM, VMEM],
        out_shape=[column, column],
        name="stats",
    )(local, *shares)

    dl, hidden_parts = None, []
    for n in range(HALVES):
        parts = mapped_parts(tab, sources[n], align_tiles, order)
        parts = [x if j == 0 else swap(x, "dp", 2 * j) for x, j in zip(parts, order)]
        dl, *terms = grads(n, core, e, a, b, weight_own, weight_other, parts, dl)
        terms = [x if j == 0 else swap(x, "dp", 2 * j) for x, j in zip(terms, order)]
        rows_sum = sum([x.astype(F32) for x in terms[:-1]], terms[-1].astype(F32))
        rows_sum = rows_sum.astype(BF16).reshape(2, -1, chips, features // dp).transpose(1, 2, 0, 3)
        pieces = rows_sum.reshape(-1, vocab, features // vocab).transpose(1, 0, 2)
        hidden_parts.append(pieces)
    pieces = jnp.concatenate(hidden_parts, axis=1)
    piece = lambda t: lax.dynamic_index_in_dim(pieces, v ^ t, 0, keepdims=False)
    hidden_grad = piece(0).astype(F32)
    others = [swap(piece(t), "vocab", t) for t in range(1, vocab)]
    hidden_grad = sum([x.astype(F32) for x in others], hidden_grad).astype(BF16)
    dl = dl.reshape(chips * tokens, -1)

    def head_half(half):
        x = lax.dynamic_index_in_dim(hidden, half, 0, keepdims=False)
        return lax.dot_general(x, dl, (((0,), (0,)), ((), ())), preferred_element_type=F32).astype(BF16)

    half = head_half(1 - c)
    got = swap(half, "dp", 1)
    half = head_half(c)
    head_terms = (half.astype(F32) + got.astype(F32)).astype(BF16)
    head_grad = lax.all_to_all(
        head_terms, "dp", split_axis=0, concat_axis=1, axis_index_groups=groups, tiled=True
    )
    return (hidden_grad, head_grad)


def solution(mesh):
    placed = (
        P("dp", None),
        P("dp", "vocab"),
        P("dp", "vocab"),
        P(),
        P("vocab", None, None, None),
        P("dp"),
    )
    return jax.shard_map(
        body,
        mesh=mesh,
        in_specs=placed,
        out_specs=(P("dp", "vocab"), P("dp", "vocab")),
        check_vma=False,
    )
```

time: 238 us -> 204 us (0.86)
  waiting for transfers between devices: 106 us -> 69.7 us
  blocking collectives: 0 us -> 25 us
  local copies, waits for them, and re-layouts: 18.6 us -> 7.52 us
  Pallas kernels: 38.2 us -> 29.7 us
    all_to_all x0 -> x1, blocking collectives: none -> 25 us  [step(): lax.all_to_all(head_weight, 'dp', split_axis=1, concat_axis=0, axis_index...]
    ppermute x23 -> x35, waiting for transfers between devices: 89.7 us -> 69.7 us  [swap(): lax.ppermute(x, axis, [(i, i ^ bits) for i in range(lax.axis_size(axis))])]
    ppermute x23 -> x35, starting transfers between devices: 32.5 us -> 50.9 us  [swap(): lax.ppermute(x, axis, [(i, i ^ bits) for i in range(lax.axis_size(axis))])]
    ppermute x7 -> x0, starting transfers between devices: 16 us -> none  [the longest x4 11.9 us: hop(): lax.ppermute(x, 'vocab', [(i, i + 1), (vocab - 1 - i, vocab - 2 - i)])]
    all_to_all x2 -> x1, waiting for transfers between devices: 15.8 us -> 0.01 us  [step(): lax.all_to_all(head_terms, 'dp', split_axis=0, concat_axis=1, axis_index_...]
    pallas_call x7 -> x4, Pallas kernels: 20.9 us -> 14.1 us  [the longest x2 6.69 us: mapped_parts(): pl.pallas_call(functools.partial(mapped_kernel, pieces), grid_spec=pltpu....]
    all_to_all x2 -> x1, starting transfers between devices: 8.19 us -> 3.97 us  [step(): lax.all_to_all(head_terms, 'dp', split_axis=0, concat_axis=1, axis_index_...]
    unnamed x65 -> x51, local copies, waits for them, and re-layouts: 6.96 us -> 3.42 us
  transfers between devices with their start and end apart: 32 -> 36, of which waited for: 13 -> 12; matrix products, arithmetic and copies ran while one was open for 10% -> 5% of each run, Pallas kernels for 12% -> 12%
where the time goes in v2:
time: 204 us
  waiting for transfers between devices  69.7 us (34%)
  starting transfers between devices  54.8 us (27%)
  Pallas kernels  29.7 us (15%)
  blocking collectives  25 us (12%)
  other arithmetic  8.7 us (4%)
  local copies, waits for them, and re-layouts  7.52 us (4%)
  matrix products  5.82 us (3%)
    ppermute x35, waiting for transfers between devices, swap(): lax.ppermute(x, axis, [(i, i ^ bits) for i in range(lax.axis_size(axis))])  69.7 us
    ppermute x35, starting transfers between devices, swap(): lax.ppermute(x, axis, [(i, i ^ bits) for i in range(lax.axis_size(axis))])  50.9 us
    all_to_all x1, blocking collectives, step(): lax.all_to_all(head_weight, 'dp', split_axis=1, concat_axis=0, axis_index...  25 us
    pallas_call x2, Pallas kernels, grads(): pl.pallas_call(grads_kernel, grid_spec=pltpu.PrefetchScalarGridSpec(num_s...  9.34 us
    pallas_call x2, Pallas kernels, mapped_parts(): pl.pallas_call(functools.partial(mapped_kernel, pieces), grid_spec=pltpu....  6.69 us
    pallas_call x1, Pallas kernels, logits_parts(): pl.pallas_call(logits_kernel, grid_spec=pltpu.PrefetchScalarGridSpec(num_...  6.3 us
    dot_general x2, matrix products, head_half(): lax.dot_general(x, dl, (((0,), (0,)), ((), ())), preferred_element_type=F32)  5.61 us
    pallas_call x1, Pallas kernels, teacher_lists(): pl.pallas_call(functools.partial(probs_kernel, peers), grid_spec=pltpu.Pr...  5.58 us
  transfers between devices with their start and end apart: 36, of which 12 were waited for; matrix products, arithmetic and copies ran while one was open for 5% of the time, Pallas kernels for 12%

profile of v2, /device:TPU:0, one launch (start us, length us, event | category | flops | bytes accessed | tf_op | source)
XLA Modules:
  0.0 203.7 jit_solution(13872708558682226124)
XLA Ops:
  0.6 0.8 copy.94
  2.6 1.3 fusion.80
  4.6 197.9 %conditional.4 = (bf16[192,4096]{1,0:T(8,128)(2,1)S(1)}, bf16[128,384]{1,0:T(8,128)(2,1)S(1)}) conditional(s32[]{:T(128)} %convert_element_type.159, (bf16[128,1536]{1,0:T(8,128)(2,1)}, bf16[192,4096]{1,0:T(8,128)(2,1)}, s32[6,64]{1,0:T(8,128)S(1)}, f32[128,5120]{1,0:T(8,128)}, s32[128,2]{0,1:T(2,128)}, ...), branch_computations={%region_4.8_spmd, %region_8.12_spmd} | conditional | flops 1644281088 | bytes 111401856
  4.8 1.5 copy.107
  6.4 25.0 %all_to_all.61 = bf16[192,4,1024]{2,0,1:T(8,128)(2,1)} all-to-all(bf16[192,4,1024]{2,0,1:T(8,128)(2,1)S(1)} %bitcast.155), channel_id=1, replica_groups={{0,8,16,24},{4,12,20,28},{1,9,17,25},{5,13,21,29},{2,10,18,26},{6,14,22..., dimensions={1} | all-to-all | bytes 3145728 | tf_op jit(solution)/shard_map/cond/branch_1_fun/all_to_all | solution.py:273
  31.4 0.6 convert_reduce_fusion.1
  32.1 1.6 collective-permute-start.39
  33.7 2.6 %collective-permute-start.40 = (f32[64,128]{1,0:T(8,128)S(1)}, f32[64,128]{1,0:T(8,128)S(1)}, u32[]{:S(2)}, u32[]{:S(2)}) collective-permute-start(f32[64,128]{1,0:T(8,128)S(1)} %bitcast.181), channel_id=1, source_target_pairs={{0,2},{1,3},{2,0},{3,1},{4,6},{5,7},{6,4},{7,5},{8,10},{9,11},{10,... | collective-permute-start | bytes 98312 | tf_op jit(solution)/shard_map/cond/branch_1_fun/ppermute | solution.py:23
  36.7 1.0 collective-permute-start.35
  37.7 1.5 collective-permute-start.36
  39.8 5.6 %probs.3 = (bf16[40,64,128]{2,1,0:T(8,128)(2,1)}, bf16[24,64,128]{2,1,0:T(8,128)(2,1)}, bf16[24,64,128]{2,1,0:T(8,128)(2,1)}, bf16[24,64,128]{2,1,0:T(8,128)(2,1...) custom-call(s32[6,64]{1,0:T(8,128)S(1)} %get-tuple-element.77.tab_re, ...), custom_call_target="tpu_custom_call" | custom-call | tf_op jit(solution)/shard_map/cond/branch_1_fun/probs/pallas_call | solution.py:62
  45.4 1.1 collective-permute-start.37
  46.5 0.7 collective-permute-start.54
  47.4 2.3 %collective-permute-done.35 = bf16[2,128,768]{2,1,0:T(8,128)(2,1)S(1)} collective-permute-done((bf16[2,128,768]{2,1,0:T(8,128)(2,1)S(1)}, bf16[2,128,768]{2,1,0:T(8,128)(2,1)S(1)}, u32[]{:S(2)}, u32[]{:S(2)}) %collective-permute-start.35) | collective-permute-done | bytes 393248 | tf_op jit(solution)/shard_map/cond/branch_1_fun/ppermute | solution.py:23
  49.7 1.2 collective-permute-start.55
  50.9 5.9 %collective-permute-done.36 = bf16[2,128,768]{2,1,0:T(8,128)(2,1)S(1)} collective-permute-done((bf16[2,128,768]{2,1,0:T(8,128)(2,1)S(1)}, bf16[2,128,768]{2,1,0:T(8,128)(2,1)S(1)}, u32[]{:S(2)}, u32[]{:S(2)}) %collective-permute-start.36) | collective-permute-done | bytes 393248 | tf_op jit(solution)/shard_map/cond/branch_1_fun/ppermute | solution.py:23
  57.1 1.7 multiply_reduce_fusion.3
  58.8 1.3 pad_maximum_fusion.3.x_ref
  60.1 6.3 %logits.3 = (f32[4,128,1024]{2,1,0:T(8,128)}, f32[2,4,128]{2,1,0:T(4,128)}) custom-call(s32[1]{0:T(128)} %bitcast.36.core_ref, bf16[2,512,768]{2,1,0:T(8,128)(2,1)} %pad_maximum_fusion.3.x_ref, bf16[768,1024]{1,0:T(8,128)(2,1)} %bitcast.38.own_ref, bf16[768,1024]{1,0:T(8,128)(2,1)} %collective-permute-done.38.other_ref), custom_call_target="tpu_custom_call" | custom-call | tf_op jit(solution)/shard_map/cond/branch_1_fun/logits/pallas_call | solution.py:138
  66.4 0.7 pad_maximum_fusion.4
  67.1 0.7 collective-permute-start.42
  67.7 3.5 %collective-permute-start.43 = (f32[9,128]{1,0:T(8,128)S(1)}, f32[9,128]{1,0:T(8,128)S(1)}, u32[]{:S(2)}, u32[]{:S(2)}) collective-permute-start(f32[9,128]{1,0:T(8,128)S(1)} %pad_maximum_fusion.4), channel_id=1, source_target_pairs={{0,2},{1,3},{2,0},{3,1},{4,6},{5,7},{6,4},{7,5},{8,10},{9,11},{10,... | collective-permute-start | bytes 13832 | tf_op jit(solution)/shard_map/cond/branch_1_fun/ppermute | solution.py:23
  71.4 8.0 %collective-permute-done.55.refs_2_ = bf16[24,64,128]{2,1,0:T(8,128)(2,1)} collective-permute-done((bf16[24,64,128]{2,1,0:T(8,128)(2,1)}, bf16[24,64,128]{2,1,0:T(8,128)(2,1)}, u32[]{:S(2)}, u32[]{:S(2)}) %collective-permute-start.55) | collective-permute-done | bytes 393248 | tf_op jit(solution)/shard_map/cond/branch_1_fun/ppermute | solution.py:23
  79.5 6.9 %collective-permute-start.49 = (bf16[24,64,128]{2,1,0:T(8,128)(2,1)}, bf16[24,64,128]{2,1,0:T(8,128)(2,1)S(1)}, u32[]{:S(2)}, u32[]{:S(2)}) collective-permute-start(bf16[24,64,128]{2,1,0:T(8,128)(2,1)} %get-tuple-element.87), channel_id=1, source_target_pairs={{0,2},{1,3},{2,0},{3,1},{4,6},{5,7},{6,4},{7,5},{8,10},{9,11},{10,... | collective-permute-start | bytes 1179656 | tf_op jit(solution)/shard_map/cond/branch_1_fun/ppermute | solution.py:23
  86.4 3.4 %mapped.7 = (bf16[64,1024]{1,0:T(8,128)(2,1)}, bf16[64,1024]{1,0:T(8,128)(2,1)}, bf16[64,1024]{1,0:T(8,128)(2,1)}, bf16[64,1024]{1,0:T(8,128)(2,1)}) custom-call(s32[6,64]{1,0:T(8,128)S(1)} %get-tuple-element.77.tab_ref, bf16[40,64,128]{2,1,0:T(8,128)(2,1)} %get-tuple-element.79.refs_0_, bf16[24,64,128]{2,1,0:T(8,128)(2,1)} %collective-permute-done.54.refs_1_, ...), custom_call_target="tpu_custom_call" | custom-call | tf_op jit(solution)/shard_map/cond/branch_1_fun/mapped/pallas_call | solution.py:103
  89.8 3.1 %collective-permute-start.50 = (bf16[24,64,128]{2,1,0:T(8,128)(2,1)}, bf16[24,64,128]{2,1,0:T(8,128)(2,1)S(1)}, u32[]{:S(2)}, u32[]{:S(2)}) collective-permute-start(bf16[24,64,128]{2,1,0:T(8,128)(2,1)} %get-tuple-element.88), channel_id=1, source_target_pairs={{0,3},{1,2},{2,1},{3,0},{4,7},{5,6},{6,5},{7,4},{8,11},{9,10},{10,... | collective-permute-start | bytes 1179656 | tf_op jit(solution)/shard_map/cond/branch_1_fun/ppermute | solution.py:23
  92.9 0.8 collective-permute-start.57
  93.9 1.5 collective-permute-start.45
  95.4 1.2 collective-permute-start.46
  96.6 16.3 %collective-permute-done.49.refs_2_ = bf16[24,64,128]{2,1,0:T(8,128)(2,1)S(1)} collective-permute-done((bf16[24,64,128]{2,1,0:T(8,128)(2,1)}, bf16[24,64,128]{2,1,0:T(8,128)(2,1)S(1)}, u32[]{:S(2)}, u32[]{:S(2)}) %collective-permute-start.49) | collective-permute-done | bytes 393248 | tf_op jit(solution)/shard_map/cond/branch_1_fun/ppermute | solution.py:23
  112.9 1.2 collective-permute-start.47
  114.1 1.5 collective-permute-start.58
  115.6 3.3 %mapped.6 = (bf16[64,1024]{1,0:T(8,128)(2,1)}, bf16[64,1024]{1,0:T(8,128)(2,1)}, bf16[64,1024]{1,0:T(8,128)(2,1)}, bf16[64,1024]{1,0:T(8,128)(2,1)}) custom-call(s32[6,64]{1,0:T(8,128)S(1)} %get-tuple-element.77.tab_ref, bf16[40,64,128]{2,1,0:T(8,128)(2,1)} %get-tuple-element.82.refs_0_, bf16[24,64,128]{2,1,0:T(8,128)(2,1)} %copy-done.10, ...), custom_call_target="tpu_custom_call" | custom-call | tf_op jit(solution)/shard_map/cond/branch_1_fun/mapped/pallas_call | solution.py:103
  119.0 0.9 collective-permute-start.59
  119.9 1.4 collective-permute-start.51
  121.3 1.3 collective-permute-start.52
  122.5 0.8 collective-permute-start.53
  123.4 1.8 stats.3
  125.2 0.6 copy-done.20
  125.9 4.7 %grads.6 = (bf16[4,128,1024]{2,1,0:T(8,128)(2,1)}, bf16[2,64,768]{2,1,0:T(8,128)(2,1)}, bf16[2,64,768]{2,1,0:T(8,128)(2,1)}, bf16[2,64,768]{2,1,0:T(8,128)(2,1)}, bf16[2,64,768]{2,1,0:T(8,128)(2,1)}) custom-call(s32[1]{0:T(128)} %bitcast.36.core_ref, f32[4,128,1024]{2,1,0:T(8,128)} %get-tuple-element.75.e_ref, f32[4,128,1]{2,1,0:T(8,128)} %get-tuple-element.84.a_ref, ...), custom_call_target="tpu_custom_call" | custom-call | tf_op jit(solution)/shard_map/cond/branch_1_fun/grads/pallas_call | solution.py:191
  130.6 0.6 copy-done.24
  131.3 4.7 %grads.7 = (bf16[4,128,1024]{2,1,0:T(8,128)(2,1)}, bf16[2,64,768]{2,1,0:T(8,128)(2,1)}, bf16[2,64,768]{2,1,0:T(8,128)(2,1)}, bf16[2,64,768]{2,1,0:T(8,128)(2,1)}, bf16[2,64,768]{2,1,0:T(8,128)(2,1)}) custom-call(s32[1]{0:T(128)} %bitcast.36.core_ref, f32[4,128,1024]{2,1,0:T(8,128)} %get-tuple-element.75.e_ref, ...), custom_call_target="tpu_custom_call", output_to_operand_aliasing={{0}: (10, {})} | custom-call | tf_op jit(solution)/shard_map/cond/branch_1_fun/grads/pallas_call | solution.py:191
  136.0 3.4 %convolution_convert_fusion.2 = bf16[768,1024]{1,0:T(8,128)(2,1)} fusion(bf16[512,1024]{1,0:T(8,128)(2,1)} %bitcast.176, bf16[2,512,768]{2,1,0:T(8,128)(2,1)S(1)} %copy-done.3, s32[]{:T(128)S(6)} %select_n.91), kind=kOutput, calls=%fused_computation.78 | convolution fusion | flops 806092800 | bytes 3407876 | tf_op jit(solution)/shard_map/cond/branch_1_fun/dot_general | solution.py:328
  139.4 2.2 %convolution_convert_fusion.3 = bf16[768,1024]{1,0:T(8,128)(2,1)S(1)} fusion(bf16[512,1024]{1,0:T(8,128)(2,1)} %bitcast.177, bf16[2,512,768]{2,1,0:T(8,128)(2,1)S(1)} %copy-done.3, s32[]{:T(128)S(6)} %select_n.86), kind=kOutput, calls=%fused_computation.79 | convolution fusion | flops 806092800 | bytes 3407876 | tf_op jit(solution)/shard_map/cond/branch_1_fun/dot_general | solution.py:328
  141.6 1.4 collective-permute-done.60
  143.0 1.8 add_convert_fusion.3
  144.9 4.0 %all-to-all-start.3 = ((bf16[4,192,1024]{2,1,0:T(8,128)(2,1)}), bf16[4,192,1024]{2,1,0:T(8,128)(2,1)S(1)}, u32[]{:S(2)}, u32[]{:S(2)}) async-start(bf16[4,192,1024]{2,1,0:T(8,128)(2,1)} %bitcast.54), calls=%async_computation.3 | async-start | bytes 3145728 | tf_op jit(solution)/shard_map/cond/branch_1_fun/all_to_all | solution.py:334
  148.9 2.6 %collective-permute-start.64 = (bf16[2,64,768]{2,1,0:T(8,128)(2,1)S(1)}, bf16[2,64,768]{2,1,0:T(8,128)(2,1)S(1)}, u32[]{:S(2)}, u32[]{:S(2)}) collective-permute-start(bf16[2,64,768]{2,1,0:T(8,128)(2,1)S(1)} %copy-done.50), channel_id=1, source_target_pairs={{0,24},{4,28},{8,16},{12,20},{16,8},{20,12},{24,0},{28,4},{1,25},{... | collective-permute-start | bytes 589832 | tf_op jit(solution)/shard_map/cond/branch_1_fun/ppermute | solution.py:23
  151.5 0.6 collective-permute-start.65
  152.1 0.4 collective-permute-start.66
  152.4 2.5 %collective-permute-start.61 = (bf16[2,64,768]{2,1,0:T(8,128)(2,1)}, bf16[2,64,768]{2,1,0:T(8,128)(2,1)S(1)}, u32[]{:S(2)}, u32[]{:S(2)}) collective-permute-start(bf16[2,64,768]{2,1,0:T(8,128)(2,1)} %get-tuple-element.103), channel_id=1, source_target_pairs={{0,24},{4,28},{8,16},{12,20},{16,8},{20,12},{24,0},{28,4},{1,25},{... | collective-permute-start | bytes 589832 | tf_op jit(solution)/shard_map/cond/branch_1_fun/ppermute | solution.py:23
  155.0 0.6 collective-permute-start.62
  155.6 18.8 %collective-permute-done.64 = bf16[2,64,768]{2,1,0:T(8,128)(2,1)S(1)} collective-permute-done((bf16[2,64,768]{2,1,0:T(8,128)(2,1)S(1)}, bf16[2,64,768]{2,1,0:T(8,128)(2,1)S(1)}, u32[]{:S(2)}, u32[]{:S(2)}) %collective-permute-start.64) | collective-permute-done | bytes 196640 | tf_op jit(solution)/shard_map/cond/branch_1_fun/ppermute | solution.py:23
  174.4 0.5 collective-permute-start.63
  174.9 3.4 %collective-permute-done.65 = bf16[2,64,768]{2,1,0:T(8,128)(2,1)S(1)} collective-permute-done((bf16[2,64,768]{2,1,0:T(8,128)(2,1)S(1)}, bf16[2,64,768]{2,1,0:T(8,128)(2,1)S(1)}, u32[]{:S(2)}, u32[]{:S(2)}) %collective-permute-start.65) | collective-permute-done | bytes 196640 | tf_op jit(solution)/shard_map/cond/branch_1_fun/ppermute | solution.py:23
  178.6 0.3 copy.93
  179.1 3.8 %collective-permute-done.61 = bf16[2,64,768]{2,1,0:T(8,128)(2,1)S(1)} collective-permute-done((bf16[2,64,768]{2,1,0:T(8,128)(2,1)}, bf16[2,64,768]{2,1,0:T(8,128)(2,1)S(1)}, u32[]{:S(2)}, u32[]{:S(2)}) %collective-permute-start.61) | collective-permute-done | bytes 196640 | tf_op jit(solution)/shard_map/cond/branch_1_fun/ppermute | solution.py:23
  182.9 2.3 %collective-permute-done.62 = bf16[2,64,768]{2,1,0:T(8,128)(2,1)S(1)} collective-permute-done((bf16[2,64,768]{2,1,0:T(8,128)(2,1)S(1)}, bf16[2,64,768]{2,1,0:T(8,128)(2,1)S(1)}, u32[]{:S(2)}, u32[]{:S(2)}) %collective-permute-start.62) | collective-permute-done | bytes 196640 | tf_op jit(solution)/shard_map/cond/branch_1_fun/ppermute | solution.py:23
  186.2 6.0 %collective-permute-start.67 = (bf16[128,384]{1,0:T(8,128)(2,1)S(1)}, bf16[128,384]{1,0:T(8,128)(2,1)S(1)}, u32[]{:S(2)}, u32[]{:S(2)}) collective-permute-start(bf16[128,384]{1,0:T(8,128)(2,1)S(1)} %get-tuple-element.193), channel_id=1, source_target_pairs={{0,1},{1,0},{2,3},{3,2},{4,5},{5,4},{6,7},{7,6},{8,9},{9,8},{10,11... | collective-permute-start | bytes 294920 | tf_op jit(solution)/shard_map/cond/branch_1_fun/ppermute | solution.py:23
  192.2 0.7 collective-permute-start.68
  192.9 1.7 collective-permute-start.69
  194.7 0.7 collective-permute-done.67
  195.4 6.5 %collective-permute-done.68 = bf16[128,384]{1,0:T(8,128)(2,1)S(1)} collective-permute-done((bf16[128,384]{1,0:T(8,128)(2,1)S(1)}, bf16[128,384]{1,0:T(8,128)(2,1)S(1)}, u32[]{:S(2)}, u32[]{:S(2)}) %collective-permute-start.68) | collective-permute-done | bytes 98336 | tf_op jit(solution)/shard_map/cond/branch_1_fun/ppermute | solution.py:23
  202.5 1.1 copy-done.4
  (117 shorter events, 4.9 us)
Async XLA Ops:
  6.4 25.0 %copy-start.1 = (bf16[32,2,128,128]{3,2,1,0:T(8,128)(2,1)S(1)}, bf16[32,2,128,128]{3,2,1,0:T(8,128)(2,1)}, u32[]{:S(2)}) copy-start(bf16[32,2,128,128]{3,2,1,0:T(8,128)(2,1)} %get-tuple-element.81.refs_4_) | copy-start | bytes 6291460
  31.4 4.9 %copy-start.6 = (bf16[128,1536]{1,0:T(8,128)(2,1)S(1)}, bf16[128,1536]{1,0:T(8,128)(2,1)}, u32[]{:S(2)}) copy-start(bf16[128,1536]{1,0:T(8,128)(2,1)} %get-tuple-element.168) | copy-start | bytes 1179652
  31.4 28.7 %collective-permute-start.38 = (bf16[768,1024]{1,0:T(8,128)(2,1)}, bf16[768,1024]{1,0:T(8,128)(2,1)}, u32[]{:S(2)}, u32[]{:S(2)}) collective-permute-start(bf16[768,1024]{1,0:T(8,128)(2,1)} %bitcast.38.own_ref), channel_id=1, source_target_pairs={{0,4},{4,0},{8,12},{12,8},{16,20},{20,16},{24,28},{28,24},{1,5},{5... | collective-permute-start | bytes 4718600 | tf_op jit(solution)/shard_map/cond/branch_1_fun/ppermute | solution.py:23
  32.1 7.1 %copy-start.35 = (s32[128,2]{0,1:T(2,128)S(1)}, s32[128,2]{0,1:T(2,128)}, u32[]{:S(2)}) copy-start(s32[128,2]{0,1:T(2,128)} %get-tuple-element.172) | copy-start | bytes 3076
  32.1 7.5 %collective-permute-start.39 = (f32[64,128]{1,0:T(8,128)S(1)}, f32[64,128]{1,0:T(8,128)S(1)}, u32[]{:S(2)}, u32[]{:S(2)}) collective-permute-start(f32[64,128]{1,0:T(8,128)S(1)} %bitcast.180), channel_id=1, source_target_pairs={{0,1},{1,0},{2,3},{3,2},{4,5},{5,4},{6,7},{7,6},{8,9},{9,8},{10,11... | collective-permute-start | bytes 98312 | tf_op jit(solution)/shard_map/cond/branch_1_fun/ppermute | solution.py:23
  33.7 11.7 %collective-permute-start.40 = (f32[64,128]{1,0:T(8,128)S(1)}, f32[64,128]{1,0:T(8,128)S(1)}, u32[]{:S(2)}, u32[]{:S(2)}) collective-permute-start(f32[64,128]{1,0:T(8,128)S(1)} %bitcast.181), channel_id=1, source_target_pairs={{0,2},{1,3},{2,0},{3,1},{4,6},{5,7},{6,4},{7,5},{8,10},{9,11},{10,... | collective-permute-start | bytes 98312 | tf_op jit(solution)/shard_map/cond/branch_1_fun/ppermute | solution.py:23
  36.7 13.0 %collective-permute-start.35 = (bf16[2,128,768]{2,1,0:T(8,128)(2,1)S(1)}, bf16[2,128,768]{2,1,0:T(8,128)(2,1)S(1)}, u32[]{:S(2)}, u32[]{:S(2)}) collective-permute-start(bf16[2,128,768]{2,1,0:T(8,128)(2,1)S(1)} %copy.86), channel_id=1, source_target_pairs={{0,24},{4,28},{8,16},{12,20},{16,8},{20,12},{24,0},{28,4},{1,25},{... | collective-permute-start | bytes 1179656 | tf_op jit(solution)/shard_map/cond/branch_1_fun/ppermute | solution.py:23
  37.7 19.1 %collective-permute-start.36 = (bf16[2,128,768]{2,1,0:T(8,128)(2,1)S(1)}, bf16[2,128,768]{2,1,0:T(8,128)(2,1)S(1)}, u32[]{:S(2)}, u32[]{:S(2)}) collective-permute-start(bf16[2,128,768]{2,1,0:T(8,128)(2,1)S(1)} %copy.86), channel_id=1, source_target_pairs={{0,16},{4,20},{8,24},{12,28},{16,0},{20,4},{24,8},{28,12},{1,17},{... | collective-permute-start | bytes 1179656 | tf_op jit(solution)/shard_map/cond/branch_1_fun/ppermute | solution.py:23
  39.5 6.9 %collective-permute-start.41 = (f32[64,128]{1,0:T(8,128)S(1)}, f32[64,128]{1,0:T(8,128)S(1)}, u32[]{:S(2)}, u32[]{:S(2)}) collective-permute-start(f32[64,128]{1,0:T(8,128)S(1)} %bitcast.182), channel_id=1, source_target_pairs={{0,3},{1,2},{2,1},{3,0},{4,7},{5,6},{6,5},{7,4},{8,11},{9,10},{10,... | collective-permute-start | bytes 98312 | tf_op jit(solution)/shard_map/cond/branch_1_fun/ppermute | solution.py:23
  45.4 13.5 %collective-permute-start.37 = (bf16[2,128,768]{2,1,0:T(8,128)(2,1)S(1)}, bf16[2,128,768]{2,1,0:T(8,128)(2,1)S(1)}, u32[]{:S(2)}, u32[]{:S(2)}) collective-permute-start(bf16[2,128,768]{2,1,0:T(8,128)(2,1)S(1)} %copy.86), channel_id=1, source_target_pairs={{0,8},{4,12},{8,0},{12,4},{16,24},{20,28},{24,16},{28,20},{1,9},{5... | collective-permute-start | bytes 1179656 | tf_op jit(solution)/shard_map/cond/branch_1_fun/ppermute | solution.py:23
  46.5 24.8 %collective-permute-start.54 = (bf16[24,64,128]{2,1,0:T(8,128)(2,1)}, bf16[24,64,128]{2,1,0:T(8,128)(2,1)}, u32[]{:S(2)}, u32[]{:S(2)}) collective-permute-start(bf16[24,64,128]{2,1,0:T(8,128)(2,1)} %get-tuple-element.93), channel_id=1, source_target_pairs={{0,1},{1,0},{2,3},{3,2},{4,5},{5,4},{6,7},{7,6},{8,9},{9,8},{10,11... | collective-permute-start | bytes 1179656 | tf_op jit(solution)/shard_map/cond/branch_1_fun/ppermute | solution.py:23
  49.7 29.8 %collective-permute-start.55 = (bf16[24,64,128]{2,1,0:T(8,128)(2,1)}, bf16[24,64,128]{2,1,0:T(8,128)(2,1)}, u32[]{:S(2)}, u32[]{:S(2)}) collective-permute-start(bf16[24,64,128]{2,1,0:T(8,128)(2,1)} %get-tuple-element.94), channel_id=1, source_target_pairs={{0,2},{1,3},{2,0},{3,1},{4,6},{5,7},{6,4},{7,5},{8,10},{9,11},{10,... | collective-permute-start | bytes 1179656 | tf_op jit(solution)/shard_map/cond/branch_1_fun/ppermute | solution.py:23
  56.8 22.6 %collective-permute-start.56 = (bf16[24,64,128]{2,1,0:T(8,128)(2,1)}, bf16[24,64,128]{2,1,0:T(8,128)(2,1)}, u32[]{:S(2)}, u32[]{:S(2)}) collective-permute-start(bf16[24,64,128]{2,1,0:T(8,128)(2,1)} %get-tuple-element.95), channel_id=1, source_target_pairs={{0,3},{1,2},{2,1},{3,0},{4,7},{5,6},{6,5},{7,4},{8,11},{9,10},{10,... | collective-permute-start | bytes 1179656 | tf_op jit(solution)/shard_map/cond/branch_1_fun/ppermute | solution.py:23
  67.1 22.7 %collective-permute-start.42 = (f32[9,128]{1,0:T(8,128)S(1)}, f32[9,128]{1,0:T(8,128)S(1)}, u32[]{:S(2)}, u32[]{:S(2)}) collective-permute-start(f32[9,128]{1,0:T(8,128)S(1)} %pad_maximum_fusion.4), channel_id=1, source_target_pairs={{0,1},{1,0},{2,3},{3,2},{4,5},{5,4},{6,7},{7,6},{8,9},{9,8},{10,11... | collective-permute-start | bytes 13832 | tf_op jit(solution)/shard_map/cond/branch_1_fun/ppermute | solution.py:23
  67.7 25.2 %collective-permute-start.43 = (f32[9,128]{1,0:T(8,128)S(1)}, f32[9,128]{1,0:T(8,128)S(1)}, u32[]{:S(2)}, u32[]{:S(2)}) collective-permute-start(f32[9,128]{1,0:T(8,128)S(1)} %pad_maximum_fusion.4), channel_id=1, source_target_pairs={{0,2},{1,3},{2,0},{3,1},{4,6},{5,7},{6,4},{7,5},{8,10},{9,11},{10,... | collective-permute-start | bytes 13832 | tf_op jit(solution)/shard_map/cond/branch_1_fun/ppermute | solution.py:23
  71.2 22.5 %collective-permute-start.44 = (f32[9,128]{1,0:T(8,128)S(1)}, f32[9,128]{1,0:T(8,128)S(1)}, u32[]{:S(2)}, u32[]{:S(2)}) collective-permute-start(f32[9,128]{1,0:T(8,128)S(1)} %pad_maximum_fusion.4), channel_id=1, source_target_pairs={{0,3},{1,2},{2,1},{3,0},{4,7},{5,6},{6,5},{7,4},{8,11},{9,10},{10,... | collective-permute-start | bytes 13832 | tf_op jit(solution)/shard_map/cond/branch_1_fun/ppermute | solution.py:23
  79.5 15.9 %collective-permute-start.48 = (bf16[24,64,128]{2,1,0:T(8,128)(2,1)}, bf16[24,64,128]{2,1,0:T(8,128)(2,1)S(1)}, u32[]{:S(2)}, u32[]{:S(2)}) collective-permute-start(bf16[24,64,128]{2,1,0:T(8,128)(2,1)} %get-tuple-element.86), channel_id=1, source_target_pairs={{0,1},{1,0},{2,3},{3,2},{4,5},{5,4},{6,7},{7,6},{8,9},{9,8},{10,11... | collective-permute-start | bytes 1179656 | tf_op jit(solution)/shard_map/cond/branch_1_fun/ppermute | solution.py:23
  79.5 14.3 %copy-start.31 = (f32[2,4,128]{2,1,0:T(4,128)S(1)}, f32[2,4,128]{2,1,0:T(4,128)}, u32[]{:S(2)}) copy-start(f32[2,4,128]{2,1,0:T(4,128)} %get-tuple-element.76.own_ref) | copy-start | bytes 12292
  79.5 14.4 %copy-start.40 = (f32[128]{0:T(128)S(1)}, f32[128]{0:T(128)}, u32[]{:S(2)}) copy-start(f32[128]{0:T(128)} %get-tuple-element.83) | copy-start | bytes 1540
  79.5 33.4 %collective-permute-start.49 = (bf16[24,64,128]{2,1,0:T(8,128)(2,1)}, bf16[24,64,128]{2,1,0:T(8,128)(2,1)S(1)}, u32[]{:S(2)}, u32[]{:S(2)}) collective-permute-start(bf16[24,64,128]{2,1,0:T(8,128)(2,1)} %get-tuple-element.87), channel_id=1, source_target_pairs={{0,2},{1,3},{2,0},{3,1},{4,6},{5,7},{6,4},{7,5},{8,10},{9,11},{10,... | collective-permute-start | bytes 1179656 | tf_op jit(solution)/shard_map/cond/branch_1_fun/ppermute | solution.py:23
  89.8 24.3 %collective-permute-start.50 = (bf16[24,64,128]{2,1,0:T(8,128)(2,1)}, bf16[24,64,128]{2,1,0:T(8,128)(2,1)S(1)}, u32[]{:S(2)}, u32[]{:S(2)}) collective-permute-start(bf16[24,64,128]{2,1,0:T(8,128)(2,1)} %get-tuple-element.88), channel_id=1, source_target_pairs={{0,3},{1,2},{2,1},{3,0},{4,7},{5,6},{6,5},{7,4},{8,11},{9,10},{10,... | collective-permute-start | bytes 1179656 | tf_op jit(solution)/shard_map/cond/branch_1_fun/ppermute | solution.py:23
  92.9 26.0 %collective-permute-start.57 = (bf16[64,1024]{1,0:T(8,128)(2,1)}, bf16[64,1024]{1,0:T(8,128)(2,1)S(1)}, u32[]{:S(2)}, u32[]{:S(2)}) collective-permute-start(bf16[64,1024]{1,0:T(8,128)(2,1)} %get-tuple-element.96), channel_id=1, source_target_pairs={{0,24},{4,28},{8,16},{12,20},{16,8},{20,12},{24,0},{28,4},{1,25},{... | collective-permute-start | bytes 393224 | tf_op jit(solution)/shard_map/cond/branch_1_fun/ppermute | solution.py:23
  93.9 29.5 %copy-start.33 = (f32[10,128]{1,0:T(8,128)}, f32[10,128]{1,0:T(8,128)S(1)}, u32[]{:S(2)}) copy-start(f32[10,128]{1,0:T(8,128)S(1)} %pad_maximum_fusion.5.refs_0_) | copy-start | bytes 15364
  93.9 26.0 %collective-permute-start.45 = (f32[10,128]{1,0:T(8,128)S(1)}, f32[10,128]{1,0:T(8,128)}, u32[]{:S(2)}, u32[]{:S(2)}) collective-permute-start(f32[10,128]{1,0:T(8,128)S(1)} %pad_maximum_fusion.5.refs_0_), channel_id=1, source_target_pairs={{0,8},{4,12},{8,0},{12,4},{16,24},{20,28},{24,16},{28,20},{1,9},{5... | collective-permute-start | bytes 15368 | tf_op jit(solution)/shard_map/cond/branch_1_fun/ppermute | solution.py:23
  95.4 20.2 %copy-start.10 = (bf16[24,64,128]{2,1,0:T(8,128)(2,1)}, bf16[24,64,128]{2,1,0:T(8,128)(2,1)S(1)}, u32[]{:S(2)}) copy-start(bf16[24,64,128]{2,1,0:T(8,128)(2,1)S(1)} %collective-permute-done.48.refs_1_) | copy-start | bytes 1179652
  95.4 25.9 %collective-permute-start.46 = (f32[10,128]{1,0:T(8,128)S(1)}, f32[10,128]{1,0:T(8,128)}, u32[]{:S(2)}, u32[]{:S(2)}) collective-permute-start(f32[10,128]{1,0:T(8,128)S(1)} %pad_maximum_fusion.5.refs_0_), channel_id=1, source_target_pairs={{0,16},{4,20},{8,24},{12,28},{16,0},{20,4},{24,8},{28,12},{1,17},{... | collective-permute-start | bytes 15368 | tf_op jit(solution)/shard_map/cond/branch_1_fun/ppermute | solution.py:23
  112.9 2.7 %copy-start.11 = (bf16[24,64,128]{2,1,0:T(8,128)(2,1)}, bf16[24,64,128]{2,1,0:T(8,128)(2,1)S(1)}, u32[]{:S(2)}) copy-start(bf16[24,64,128]{2,1,0:T(8,128)(2,1)S(1)} %collective-permute-done.49.refs_2_) | copy-start | bytes 1179652
  112.9 9.6 %collective-permute-start.47 = (f32[10,128]{1,0:T(8,128)S(1)}, f32[10,128]{1,0:T(8,128)}, u32[]{:S(2)}, u32[]{:S(2)}) collective-permute-start(f32[10,128]{1,0:T(8,128)S(1)} %pad_maximum_fusion.5.refs_0_), channel_id=1, source_target_pairs={{0,24},{4,28},{8,16},{12,20},{16,8},{20,12},{24,0},{28,4},{1,25},{... | collective-permute-start | bytes 15368 | tf_op jit(solution)/shard_map/cond/branch_1_fun/ppermute | solution.py:23
  114.1 1.5 copy-start.12
  114.1 11.1 %collective-permute-start.58 = (bf16[64,1024]{1,0:T(8,128)(2,1)}, bf16[64,1024]{1,0:T(8,128)(2,1)S(1)}, u32[]{:S(2)}, u32[]{:S(2)}) collective-permute-start(bf16[64,1024]{1,0:T(8,128)(2,1)} %get-tuple-element.97), channel_id=1, source_target_pairs={{0,16},{4,20},{8,24},{12,28},{16,0},{20,4},{24,8},{28,12},{1,17},{... | collective-permute-start | bytes 393224 | tf_op jit(solution)/shard_map/cond/branch_1_fun/ppermute | solution.py:23
  118.9 6.3 %copy-start.18 = (bf16[64,1024]{1,0:T(8,128)(2,1)}, bf16[64,1024]{1,0:T(8,128)(2,1)S(1)}, u32[]{:S(2)}) copy-start(bf16[64,1024]{1,0:T(8,128)(2,1)S(1)} %collective-permute-done.57.refs_0_) | copy-start | bytes 393220
  119.0 6.2 %collective-permute-start.59 = (bf16[64,1024]{1,0:T(8,128)(2,1)}, bf16[64,1024]{1,0:T(8,128)(2,1)S(1)}, u32[]{:S(2)}, u32[]{:S(2)}) collective-permute-start(bf16[64,1024]{1,0:T(8,128)(2,1)} %get-tuple-element.98), channel_id=1, source_target_pairs={{0,8},{4,12},{8,0},{12,4},{16,24},{20,28},{24,16},{28,20},{1,9},{5... | collective-permute-start | bytes 393224 | tf_op jit(solution)/shard_map/cond/branch_1_fun/ppermute | solution.py:23
  119.9 10.7 %collective-permute-start.51 = (bf16[64,1024]{1,0:T(8,128)(2,1)}, bf16[64,1024]{1,0:T(8,128)(2,1)S(1)}, u32[]{:S(2)}, u32[]{:S(2)}) collective-permute-start(bf16[64,1024]{1,0:T(8,128)(2,1)} %get-tuple-element.89), channel_id=1, source_target_pairs={{0,24},{4,28},{8,16},{12,20},{16,8},{20,12},{24,0},{28,4},{1,25},{... | collective-permute-start | bytes 393224 | tf_op jit(solution)/shard_map/cond/branch_1_fun/ppermute | solution.py:23
  121.3 9.3 %collective-permute-start.52 = (bf16[64,1024]{1,0:T(8,128)(2,1)}, bf16[64,1024]{1,0:T(8,128)(2,1)S(1)}, u32[]{:S(2)}, u32[]{:S(2)}) collective-permute-start(bf16[64,1024]{1,0:T(8,128)(2,1)} %get-tuple-element.90), channel_id=1, source_target_pairs={{0,16},{4,20},{8,24},{12,28},{16,0},{20,4},{24,8},{28,12},{1,17},{... | collective-permute-start | bytes 393224 | tf_op jit(solution)/shard_map/cond/branch_1_fun/ppermute | solution.py:23
  122.5 8.1 %collective-permute-start.53 = (bf16[64,1024]{1,0:T(8,128)(2,1)}, bf16[64,1024]{1,0:T(8,128)(2,1)S(1)}, u32[]{:S(2)}, u32[]{:S(2)}) collective-permute-start(bf16[64,1024]{1,0:T(8,128)(2,1)} %get-tuple-element.91), channel_id=1, source_target_pairs={{0,8},{4,12},{8,0},{12,4},{16,24},{20,28},{24,16},{28,20},{1,9},{5... | collective-permute-start | bytes 393224 | tf_op jit(solution)/shard_map/cond/branch_1_fun/ppermute | solution.py:23
  125.2 0.7 copy-start.20
  125.2 0.7 copy-start.22
  130.6 0.7 copy-start.24
  130.6 0.7 copy-start.26
  130.6 0.7 copy-start.28
  131.3 4.7 %copy-start.3 = (bf16[2,512,768]{2,1,0:T(8,128)(2,1)S(1)}, bf16[2,512,768]{2,1,0:T(8,128)(2,1)}, u32[]{:S(2)}) copy-start(bf16[2,512,768]{2,1,0:T(8,128)(2,1)} %pad_maximum_fusion.3.x_ref) | copy-start | bytes 4718596
  139.4 3.6 %collective-permute-start.60 = (bf16[768,1024]{1,0:T(8,128)(2,1)}, bf16[768,1024]{1,0:T(8,128)(2,1)S(1)}, u32[]{:S(2)}, u32[]{:S(2)}) collective-permute-start(bf16[768,1024]{1,0:T(8,128)(2,1)} %convolution_convert_fusion.2), channel_id=1, source_target_pairs={{0,4},{4,0},{8,12},{12,8},{16,20},{20,16},{24,28},{28,24},{1,5},{5... | collective-permute-start | bytes 4718600 | tf_op jit(solution)/shard_map/cond/branch_1_fun/ppermute | solution.py:23
  144.9 4.0 %copy-start.50 = (bf16[2,64,768]{2,1,0:T(8,128)(2,1)S(1)}, bf16[2,64,768]{2,1,0:T(8,128)(2,1)}, u32[]{:S(2)}) copy-start(bf16[2,64,768]{2,1,0:T(8,128)(2,1)} %get-tuple-element.107) | copy-start | bytes 589828
  144.9 6.6 %copy-start.48 = (bf16[2,64,768]{2,1,0:T(8,128)(2,1)S(1)}, bf16[2,64,768]{2,1,0:T(8,128)(2,1)}, u32[]{:S(2)}) copy-start(bf16[2,64,768]{2,1,0:T(8,128)(2,1)} %get-tuple-element.108) | copy-start | bytes 589828
  144.9 7.2 %copy-start.46 = (bf16[2,64,768]{2,1,0:T(8,128)(2,1)S(1)}, bf16[2,64,768]{2,1,0:T(8,128)(2,1)}, u32[]{:S(2)}) copy-start(bf16[2,64,768]{2,1,0:T(8,128)(2,1)} %get-tuple-element.109) | copy-start | bytes 589828
  144.9 10.1 %copy-start.44 = (bf16[2,64,768]{2,1,0:T(8,128)(2,1)S(1)}, bf16[2,64,768]{2,1,0:T(8,128)(2,1)}, u32[]{:S(2)}) copy-start(bf16[2,64,768]{2,1,0:T(8,128)(2,1)} %get-tuple-element.104) | copy-start | bytes 589828
  144.9 29.5 %copy-start.42 = (bf16[2,64,768]{2,1,0:T(8,128)(2,1)S(1)}, bf16[2,64,768]{2,1,0:T(8,128)(2,1)}, u32[]{:S(2)}) copy-start(bf16[2,64,768]{2,1,0:T(8,128)(2,1)} %get-tuple-element.105) | copy-start | bytes 589828
  144.9 33.4 %copy-start.16 = (bf16[2,64,768]{2,1,0:T(8,128)(2,1)S(1)}, bf16[2,64,768]{2,1,0:T(8,128)(2,1)}, u32[]{:S(2)}) copy-start(bf16[2,64,768]{2,1,0:T(8,128)(2,1)} %get-tuple-element.106) | copy-start | bytes 589828
  144.9 57.1 %all-to-all-start.3 = ((bf16[4,192,1024]{2,1,0:T(8,128)(2,1)}), bf16[4,192,1024]{2,1,0:T(8,128)(2,1)S(1)}, u32[]{:S(2)}, u32[]{:S(2)}) async-start(bf16[4,192,1024]{2,1,0:T(8,128)(2,1)} %bitcast.54), calls=%async_computation.3 | async-start | bytes 3145728 | tf_op jit(solution)/shard_map/cond/branch_1_fun/all_to_all | solution.py:334
  148.9 36.5 %copy-start.14 = (bf16[2,64,768]{2,1,0:T(8,128)(2,1)S(1)}, bf16[2,64,768]{2,1,0:T(8,128)(2,1)}, u32[]{:S(2)}) copy-start(bf16[2,64,768]{2,1,0:T(8,128)(2,1)} %get-tuple-element.102) | copy-start | bytes 589828
  148.9 25.5 %collective-permute-start.64 = (bf16[2,64,768]{2,1,0:T(8,128)(2,1)S(1)}, bf16[2,64,768]{2,1,0:T(8,128)(2,1)S(1)}, u32[]{:S(2)}, u32[]{:S(2)}) collective-permute-start(bf16[2,64,768]{2,1,0:T(8,128)(2,1)S(1)} %copy-done.50), channel_id=1, source_target_pairs={{0,24},{4,28},{8,16},{12,20},{16,8},{20,12},{24,0},{28,4},{1,25},{... | collective-permute-start | bytes 589832 | tf_op jit(solution)/shard_map/cond/branch_1_fun/ppermute | solution.py:23
  151.5 26.8 %collective-permute-start.65 = (bf16[2,64,768]{2,1,0:T(8,128)(2,1)S(1)}, bf16[2,64,768]{2,1,0:T(8,128)(2,1)S(1)}, u32[]{:S(2)}, u32[]{:S(2)}) collective-permute-start(bf16[2,64,768]{2,1,0:T(8,128)(2,1)S(1)} %copy-done.48), channel_id=1, source_target_pairs={{0,16},{4,20},{8,24},{12,28},{16,0},{20,4},{24,8},{28,12},{1,17},{... | collective-permute-start | bytes 589832 | tf_op jit(solution)/shard_map/cond/branch_1_fun/ppermute | solution.py:23
  152.1 26.2 %collective-permute-start.66 = (bf16[2,64,768]{2,1,0:T(8,128)(2,1)S(1)}, bf16[2,64,768]{2,1,0:T(8,128)(2,1)S(1)}, u32[]{:S(2)}, u32[]{:S(2)}) collective-permute-start(bf16[2,64,768]{2,1,0:T(8,128)(2,1)S(1)} %copy-done.46), channel_id=1, source_target_pairs={{0,8},{4,12},{8,0},{12,4},{16,24},{20,28},{24,16},{28,20},{1,9},{5... | collective-permute-start | bytes 589832 | tf_op jit(solution)/shard_map/cond/branch_1_fun/ppermute | solution.py:23
  152.4 30.4 %collective-permute-start.61 = (bf16[2,64,768]{2,1,0:T(8,128)(2,1)}, bf16[2,64,768]{2,1,0:T(8,128)(2,1)S(1)}, u32[]{:S(2)}, u32[]{:S(2)}) collective-permute-start(bf16[2,64,768]{2,1,0:T(8,128)(2,1)} %get-tuple-element.103), channel_id=1, source_target_pairs={{0,24},{4,28},{8,16},{12,20},{16,8},{20,12},{24,0},{28,4},{1,25},{... | collective-permute-start | bytes 589832 | tf_op jit(solution)/shard_map/cond/branch_1_fun/ppermute | solution.py:23
  155.0 30.2 %collective-permute-start.62 = (bf16[2,64,768]{2,1,0:T(8,128)(2,1)S(1)}, bf16[2,64,768]{2,1,0:T(8,128)(2,1)S(1)}, u32[]{:S(2)}, u32[]{:S(2)}) collective-permute-start(bf16[2,64,768]{2,1,0:T(8,128)(2,1)S(1)} %copy-done.44), channel_id=1, source_target_pairs={{0,16},{4,20},{8,24},{12,28},{16,0},{20,4},{24,8},{28,12},{1,17},{... | collective-permute-start | bytes 589832 | tf_op jit(solution)/shard_map/cond/branch_1_fun/ppermute | solution.py:23
  174.4 10.9 %collective-permute-start.63 = (bf16[2,64,768]{2,1,0:T(8,128)(2,1)S(1)}, bf16[2,64,768]{2,1,0:T(8,128)(2,1)S(1)}, u32[]{:S(2)}, u32[]{:S(2)}) collective-permute-start(bf16[2,64,768]{2,1,0:T(8,128)(2,1)S(1)} %copy-done.42), channel_id=1, source_target_pairs={{0,8},{4,12},{8,0},{12,4},{16,24},{20,28},{24,16},{28,20},{1,9},{5... | collective-permute-start | bytes 589832 | tf_op jit(solution)/shard_map/cond/branch_1_fun/ppermute | solution.py:23
  186.2 9.2 %collective-permute-start.67 = (bf16[128,384]{1,0:T(8,128)(2,1)S(1)}, bf16[128,384]{1,0:T(8,128)(2,1)S(1)}, u32[]{:S(2)}, u32[]{:S(2)}) collective-permute-start(bf16[128,384]{1,0:T(8,128)(2,1)S(1)} %get-tuple-element.193), channel_id=1, source_target_pairs={{0,1},{1,0},{2,3},{3,2},{4,5},{5,4},{6,7},{7,6},{8,9},{9,8},{10,11... | collective-permute-start | bytes 294920 | tf_op jit(solution)/shard_map/cond/branch_1_fun/ppermute | solution.py:23
  192.2 9.7 %collective-permute-start.68 = (bf16[128,384]{1,0:T(8,128)(2,1)S(1)}, bf16[128,384]{1,0:T(8,128)(2,1)S(1)}, u32[]{:S(2)}, u32[]{:S(2)}) collective-permute-start(bf16[128,384]{1,0:T(8,128)(2,1)S(1)} %get-tuple-element.194), channel_id=1, source_target_pairs={{0,2},{1,3},{2,0},{3,1},{4,6},{5,7},{6,4},{7,5},{8,10},{9,11},{10,... | collective-permute-start | bytes 294920 | tf_op jit(solution)/shard_map/cond/branch_1_fun/ppermute | solution.py:23
  192.9 9.0 %collective-permute-start.69 = (bf16[128,384]{1,0:T(8,128)(2,1)S(1)}, bf16[128,384]{1,0:T(8,128)(2,1)S(1)}, u32[]{:S(2)}, u32[]{:S(2)}) collective-permute-start(bf16[128,384]{1,0:T(8,128)(2,1)S(1)} %get-tuple-element.195), channel_id=1, source_target_pairs={{0,3},{1,2},{2,1},{3,0},{4,7},{5,6},{6,5},{7,4},{8,11},{9,10},{10,... | collective-permute-start | bytes 294920 | tf_op jit(solution)/shard_map/cond/branch_1_fun/ppermute | solution.py:23
  202.5 1.1 copy-start.4
  202.5 1.1 copy-start.29

commit v3 on v2

--- a/solution.py
+++ b/solution.py
@@ -27,42 +27,35 @@
     return [tokens * sum(SPLIT[:n]) // sum(SPLIT) for n in range(HALVES + 1)]
 
 
-def probs_kernel(peers, tab_ref, x_ref, *out_refs):
-    count = len(out_refs) // HALVES
-    ends = parts_of(x_ref.shape[0])
-
-    def block(at):
-        return jnp.exp(x_ref[:, pl.ds(pl.multiple_of(at * BLOCK, BLOCK), BLOCK)]).astype(BF16)
-
-    def store(list_number, slot, value):
-        for n in range(HALVES):
-            out_refs[n * count + list_number][slot] = value[ends[n] : ends[n + 1]]
-
-    def convert(slot, carry):
-        store(0, slot, block(slot))
+def probs_kernel(tab_ref, x_ref, own_ref, *out_refs):
+    def convert(block, carry):
+        columns = pl.ds(pl.multiple_of(block * BLOCK, BLOCK), BLOCK)
+        own_ref[block] = jnp.exp(x_ref[:, columns]).astype(BF16)
         return carry
 
-    lax.fori_loop(0, out_refs[0].shape[0], convert, 0)
-    for t in range(1, peers):
-
-        def copy(slot, carry, t=t):
-            at = tab_ref[2 + t, slot]
-            for n in range(HALVES):
-                out_refs[n * count + t][slot] = out_refs[n * count][at]
+    lax.fori_loop(0, own_ref.shape[0], convert, 0, unroll=4)
+    for t, out in enumerate(out_refs):
+
+        def copy(slot, carry, t=t, out=out):
+            out[slot] = own_ref[tab_ref[3 + t, slot]]
             return carry
 
-        lax.fori_loop(0, out_refs[t].shape[0], copy, 0)
-
-
-def teacher_lists(tab, logprobs, peers, length):
+        lax.fori_loop(0, out.shape[0], copy, 0, unroll=4)
+
+
+def teacher_lists(part, tab, logprobs, lengths):
     tokens, cols = logprobs.shape
     ends = parts_of(tokens)
-    lengths = [cols // BLOCK] + [length] * (peers - 1)
-    shapes = [(n, y - x, BLOCK) for x, y in zip(ends, ends[1:]) for n in lengths]
+    rows = ends[part + 1] - ends[part]
+    shapes = [(n, rows, BLOCK) for n in [cols // BLOCK] + lengths]
+    whole = lambda shape: pl.BlockSpec(shape, lambda i, tab: (0, 0, 0))
     return pl.pallas_call(
-        functools.partial(probs_kernel, peers),
+        probs_kernel,
         grid_spec=pltpu.PrefetchScalarGridSpec(
-            num_scalar_prefetch=1, grid=(), in_specs=[VMEM], out_specs=[VMEM] * len(shapes)
+            num_scalar_prefetch=1,
+            grid=(1,),
+            in_specs=[pl.BlockSpec((rows, cols), lambda i, tab: (ends[part] // rows, 0))],
+            out_specs=[whole(shape) for shape in shapes],
         ),
         out_shape=[jax.ShapeDtypeStruct(shape, BF16) for shape in shapes],
         name="probs",
@@ -169,40 +162,36 @@
 
 
 def grads_kernel(core_ref, e_ref, a_ref, b_ref, own_ref, other_ref, *refs):
-    count = e_ref.shape[0]
-    mapped, dl_ref, outs = refs[:count], refs[-count - 1], refs[-count:]
+    count, tokens = e_ref.shape[:2]
+    mapped, dl_ref, outs = refs[: HALVES * count], refs[-count - 1], refs[-count:]
+    ends = parts_of(tokens)
     c = core_ref[0]
-    for k in range(count):
-        dl_ref[k] = (a_ref[k] * e_ref[k] - b_ref[k] * mapped[k][...].astype(F32)).astype(BF16)
-    rows = dl_ref.shape[1]
-    dl = dl_ref[...].reshape(count * rows, -1)
+    for n in range(HALVES):
+        some = slice(ends[n], ends[n + 1])
+        for k in range(count):
+            columns = mapped[n * count + k][...].astype(F32)
+            dl_ref[k, some] = (a_ref[k, some] * e_ref[k, some] - b_ref[k, some] * columns).astype(BF16)
+    dl = dl_ref[...].reshape(count * tokens, -1)
     for half, weight in ((c, own_ref), (1 - c, other_ref)):
         terms = lax.dot_general(dl, weight[...], (((1,), (1,)), ((), ())), preferred_element_type=F32)
         for k in range(count):
-            outs[k][half] = terms[k * rows : (k + 1) * rows].astype(BF16)
-
-
-def grads(part, core, e, a, b, own, other, mapped, dl):
-    count, rows = len(mapped), mapped[0].shape[0]
-    features, cols = own.shape
-    at = parts_of(e.shape[1])[part] // rows
-    some = lambda n: pl.BlockSpec((count, rows, n), lambda i, core: (0, at, 0))
-    whole = lambda *shape: pl.BlockSpec(shape, lambda i, core: (0,) * len(shape))
+            outs[k][half] = terms[k * tokens : (k + 1) * tokens].astype(BF16)
+
+
+def grads(core, e, a, b, own, other, mapped):
+    count, tokens = e.shape[:2]
     return pl.pallas_call(
         grads_kernel,
         grid_spec=pltpu.PrefetchScalarGridSpec(
             num_scalar_prefetch=1,
-            grid=(1,),
-            in_specs=[some(cols), some(1), some(1), whole(features, cols), whole(features, cols)]
-            + [whole(rows, cols)] * count
-            + ([] if dl is None else [ANY]),
-            out_specs=[some(cols)] + [whole(2, rows, features)] * count,
+            grid=(),
+            in_specs=[VMEM] * (5 + len(mapped)),
+            out_specs=[VMEM] * (1 + count),
         ),
         out_shape=[jax.ShapeDtypeStruct(e.shape, BF16)]
-        + [jax.ShapeDtypeStruct((2, rows, features), BF16)] * count,
-        input_output_aliases={} if dl is None else {6 + count: 0},
+        + [jax.ShapeDtypeStruct((2, tokens, own.shape[0]), BF16)] * count,
         name="grads",
-    )(core, e, a, b, own, other, *mapped, *([] if dl is None else [dl]))
+    )(core, e, a, b, own, other, *mapped)
 
 
 def plan(align_index, pairs, count, chip):
@@ -216,7 +205,7 @@
     less = (owner[:, :, None] == owner[:, None, :]) & (rows[:, None, :] < rows[:, :, None]) & first[:, None, :]
     rank = jnp.sum(less.astype(jnp.int32), axis=2)
     here = jnp.arange(vocab)[:, None]
-    longest = jnp.max(jnp.where(owner != here, rank + 1, 0))
+    longest = jnp.max(jnp.where((owner ^ here) >= vocab // 2, rank + 1, 0))
     pick = lambda x, i: lax.dynamic_index_in_dim(x, i, 0, keepdims=False)
     own_owner = pick(owner, v)
     source = own_owner ^ v
@@ -238,7 +227,7 @@
         raise ValueError("mesh sizes")
     tab, longest = plan(align_index, pairs, count, lax.axis_index("dp") // 2)
     operands = (student_hidden, head_weight, teacher_logprobs, align_index, align_tiles, grad_scale, tab)
-    lengths = (3 * capacity // 4, capacity)
+    lengths = (11 * capacity // 16, capacity)
 
     def branch(n):
         def run(*args):
@@ -261,14 +250,16 @@
     pairs = align_tiles.shape[0] * K
     groups = [[2 * i + j for i in range(chips)] for j in range(2)]
 
-    lists = teacher_lists(tab, teacher_logprobs, vocab, length)
-    lists = [lists[n * vocab : (n + 1) * vocab] for n in range(HALVES)]
-    blocks, sources = [x[0] for x in lists], []
+    capacity = (2 * pairs + vocab - 1) // vocab
+    lengths = [length if t >= vocab // 2 else capacity for t in range(1, vocab)]
+    blocks, sources = [], []
     for n in range(HALVES):
+        own, *lists = teacher_lists(n, tab, teacher_logprobs, lengths)
         got = []
         for t in range(1, vocab):
-            got.append(swap(lists[n][t], "vocab", t))
-        sources.append([blocks[n]] + got)
+            got.append(swap(lists[t - 1], "vocab", t))
+        blocks.append(own)
+        sources.append([own] + got)
 
     weight_own = lax.all_to_all(head_weight, "dp", split_axis=1, concat_axis=0, axis_index_groups=groups, tiled=True)
     weight_other = swap(weight_own, "dp", 1)
@@ -306,17 +297,15 @@
         name="stats",
     )(local, *shares)
 
-    dl, hidden_parts = None, []
+    columns = []
     for n in range(HALVES):
         parts = mapped_parts(tab, sources[n], align_tiles, order)
-        parts = [x if j == 0 else swap(x, "dp", 2 * j) for x, j in zip(parts, order)]
-        dl, *terms = grads(n, core, e, a, b, weight_own, weight_other, parts, dl)
-        terms = [x if j == 0 else swap(x, "dp", 2 * j) for x, j in zip(terms, order)]
-        rows_sum = sum([x.astype(F32) for x in terms[:-1]], terms[-1].astype(F32))
-        rows_sum = rows_sum.astype(BF16).reshape(2, -1, chips, features // dp).transpose(1, 2, 0, 3)
-        pieces = rows_sum.reshape(-1, vocab, features // vocab).transpose(1, 0, 2)
-        hidden_parts.append(pieces)
-    pieces = jnp.concatenate(hidden_parts, axis=1)
+        columns += [x if j == 0 else swap(x, "dp", 2 * j) for x, j in zip(parts, order)]
+    dl, *terms = grads(core, e, a, b, weight_own, weight_other, columns)
+    terms = [x if j == 0 else swap(x, "dp", 2 * j) for x, j in zip(terms, order)]
+    rows_sum = sum([x.astype(F32) for x in terms[:-1]], terms[-1].astype(F32))
+    rows_sum = rows_sum.astype(BF16).reshape(2, tokens, chips, features // dp).transpose(1, 2, 0, 3)
+    pieces = rows_sum.reshape(tokens, vocab, features // vocab).transpose(1, 0, 2)
     piece = lambda t: lax.dynamic_index_in_dim(pieces, v ^ t, 0, keepdims=False)
     hidden_grad = piece(0).astype(F32)
     others = [swap(piece(t), "vocab", t) for t in range(1, vocab)]

time: 204 us -> 206 us (level)
  waiting for transfers between devices: 69.7 us -> 78.3 us
  starting transfers between devices: 54.8 us -> 49.7 us
    ppermute x35 -> x32, waiting for transfers between devices: 69.7 us -> 78.3 us  [swap(): lax.ppermute(x, axis, [(i, i ^ bits) for i in range(lax.axis_size(axis))])]
    ppermute x35 -> x32, starting transfers between devices: 50.9 us -> 46 us  [swap(): lax.ppermute(x, axis, [(i, i ^ bits) for i in range(lax.axis_size(axis))])]
    pallas_call x2 -> x1, Pallas kernels: 9.34 us -> 6.16 us  [grads(): pl.pallas_call(grads_kernel, grid_spec=pltpu.PrefetchScalarGridSpec(num_s...]
    pallas_call x1 -> x2, Pallas kernels: 5.58 us -> 7.52 us  [teacher_lists(): pl.pallas_call(probs_kernel, grid_spec=pltpu.PrefetchScalarGridSpec(num_s...]
  transfers between devices with their start and end apart: 36 -> 33, of which waited for: 12 -> 14; matrix products, arithmetic and copies ran while one was open for 5% -> 5% of each run, Pallas kernels for 12% -> 11%
where the time goes in v3:
time: 206 us; the launch traced here: 205 us
  waiting for transfers between devices  78.3 us (38%)
  starting transfers between devices  49.7 us (24%)
  Pallas kernels  28.4 us (14%)
  blocking collectives  25 us (12%)
  other arithmetic  9.03 us (4%)
  matrix products  6.63 us (3%)
  local copies, waits for them, and re-layouts  6.43 us (3%)
    ppermute x32, waiting for transfers between devices, swap(): lax.ppermute(x, axis, [(i, i ^ bits) for i in range(lax.axis_size(axis))])  78.3 us
    ppermute x32, starting transfers between devices, swap(): lax.ppermute(x, axis, [(i, i ^ bits) for i in range(lax.axis_size(axis))])  46 us
    all_to_all x1, blocking collectives, step(): lax.all_to_all(head_weight, 'dp', split_axis=1, concat_axis=0, axis_index...  25 us
    pallas_call x2, Pallas kernels, teacher_lists(): pl.pallas_call(probs_kernel, grid_spec=pltpu.PrefetchScalarGridSpec(num_s...  7.52 us
    pallas_call x2, Pallas kernels, mapped_parts(): pl.pallas_call(functools.partial(mapped_kernel, pieces), grid_spec=pltpu....  6.67 us
    pallas_call x1, Pallas kernels, logits_parts(): pl.pallas_call(logits_kernel, grid_spec=pltpu.PrefetchScalarGridSpec(num_...  6.3 us
    pallas_call x1, Pallas kernels, grads(): pl.pallas_call(grads_kernel, grid_spec=pltpu.PrefetchScalarGridSpec(num_s...  6.16 us
    dot_general x2, matrix products, head_half(): lax.dot_general(x, dl, (((0,), (0,)), ((), ())), preferred_element_type=F32)  5.61 us
  transfers between devices with their start and end apart: 33, of which 14 were waited for; matrix products, arithmetic and copies ran while one was open for 5% of the time, Pallas kernels for 11%

profile of v3, /device:TPU:0, one launch (start us, length us, event | category | flops | bytes accessed | tf_op | source)
XLA Modules:
  0.0 205.4 jit_solution(9691270605566161326)
XLA Ops:
  0.8 0.8 copy.90
  1.9 0.3 convert_reduce_fusion.2
  2.6 1.3 fusion.62
  4.6 200.0 %conditional.4 = (bf16[192,4096]{1,0:T(8,128)(2,1)}, bf16[128,384]{0,1:T(8,128)(2,1)S(1)}) conditional(s32[]{:T(128)} %convert_element_type.129, (bf16[128,1536]{1,0:T(8,128)(2,1)}, bf16[192,4096]{1,0:T(8,128)(2,1)}, s32[6,64]{1,0:T(8,128)S(1)}, f32[128,5120]{1,0:T(8,128)}, s32[128,2]{0,1:T(2,128)}, /*index=5*/bf16[32,2,128,128]{3,2,1,0:T(8,128)(2,1)}, ...), branch_computations={%region_4.8_spmd, %region_8.12_spmd} | conditional | flops 1643494656 | bytes 111663808
  4.8 1.5 copy.104
  6.4 25.0 %all_to_all.61 = bf16[192,4,1024]{2,0,1:T(8,128)(2,1)} all-to-all(bf16[192,4,1024]{2,0,1:T(8,128)(2,1)S(1)} %bitcast.143), channel_id=1, replica_groups={{0,8,16,24},{4,12,20,28},{1,9,17,25},{5,13,21,29},{2,10,18,26},{6,14,22..., dimensions={1} | all-to-all | bytes 3145728 | tf_op jit(solution)/shard_map/cond/branch_1_fun/all_to_all | solution.py:264
  31.4 1.3 convert_reduce_fusion.1
  32.6 3.6 %collective-permute-start.38 = (f32[64,128]{1,0:T(8,128)}, f32[64,128]{1,0:T(8,128)}, u32[]{:S(2)}, u32[]{:S(2)}) collective-permute-start(f32[64,128]{1,0:T(8,128)} %bitcast.45), channel_id=1, source_target_pairs={{0,3},{1,2},{2,1},{3,0},{4,7},{5,6},{6,5},{7,4},{8,11},{9,10},{10,... | collective-permute-start | bytes 98312 | tf_op jit(solution)/shard_map/cond/branch_1_fun/ppermute | solution.py:23
  36.2 0.8 collective-permute-start.36
  37.5 1.0 collective-permute-start.34
  38.8 3.7 %probs.6 = (bf16[40,64,128]{2,1,0:T(8,128)(2,1)}, bf16[32,64,128]{2,1,0:T(8,128)(2,1)}, bf16[22,64,128]{2,1,0:T(8,128)(2,1)}, bf16[22,64,128]{2,1,0:T(8,128)(2,1)}) custom-call(s32[6,64]{1,0:T(8,128)S(1)} %get-tuple-element.72.tab_ref, f32[128,5120]{1,0:T(8,128)} %get-tuple-element.73.x_ref), custom_call_target="tpu_custom_call" | custom-call | tf_op jit(solution)/shard_map/cond/branch_1_fun/probs/pallas_call | solution.py:52
  42.5 3.8 %probs.7 = (bf16[40,64,128]{2,1,0:T(8,128)(2,1)}, bf16[32,64,128]{2,1,0:T(8,128)(2,1)}, bf16[22,64,128]{2,1,0:T(8,128)(2,1)}, bf16[22,64,128]{2,1,0:T(8,128)(2,1)}) custom-call(s32[6,64]{1,0:T(8,128)S(1)} %get-tuple-element.72.tab_ref, f32[128,5120]{1,0:T(8,128)} %get-tuple-element.73.x_ref), custom_call_target="tpu_custom_call" | custom-call | tf_op jit(solution)/shard_map/cond/branch_1_fun/probs/pallas_call | solution.py:52
  46.3 0.6 collective-permute-start.33
  46.9 2.0 collective-permute-start.32
  48.9 1.2 collective-permute-start.45
  50.1 1.0 fusion.36
  51.2 1.5 multiply_reduce_fusion.3
  52.6 3.0 %collective-permute-start.46 = (bf16[22,64,128]{2,1,0:T(8,128)(2,1)}, bf16[22,64,128]{2,1,0:T(8,128)(2,1)S(1)}, u32[]{:S(2)}, u32[]{:S(2)}) collective-permute-start(bf16[22,64,128]{2,1,0:T(8,128)(2,1)} %get-tuple-element.82), channel_id=1, source_target_pairs={{0,2},{1,3},{2,0},{3,1},{4,6},{5,7},{6,4},{7,5},{8,10},{9,11},{10,... | collective-permute-start | bytes 1081352 | tf_op jit(solution)/shard_map/cond/branch_1_fun/ppermute | solution.py:23
  55.6 9.6 %collective-permute-done.33 = bf16[2,128,768]{2,1,0:T(8,128)(2,1)S(1)} collective-permute-done((bf16[2,128,768]{2,1,0:T(8,128)(2,1)S(1)}, bf16[2,128,768]{2,1,0:T(8,128)(2,1)S(1)}, u32[]{:S(2)}, u32[]{:S(2)}) %collective-permute-start.33) | collective-permute-done | bytes 393248 | tf_op jit(solution)/shard_map/cond/branch_1_fun/ppermute | solution.py:23
  65.2 3.5 %collective-permute-start.47 = (bf16[22,64,128]{2,1,0:T(8,128)(2,1)}, bf16[22,64,128]{2,1,0:T(8,128)(2,1)}, u32[]{:S(2)}, u32[]{:S(2)}) collective-permute-start(bf16[22,64,128]{2,1,0:T(8,128)(2,1)} %get-tuple-element.83), channel_id=1, source_target_pairs={{0,3},{1,2},{2,1},{3,0},{4,7},{5,6},{6,5},{7,4},{8,11},{9,10},{10,... | collective-permute-start | bytes 1081352 | tf_op jit(solution)/shard_map/cond/branch_1_fun/ppermute | solution.py:23
  68.8 1.2 pad_maximum_fusion.3.x_ref
  70.1 6.3 %logits.3 = (f32[4,128,1024]{2,1,0:T(8,128)}, f32[2,4,128]{2,1,0:T(4,128)}) custom-call(s32[1]{0:T(128)} %bitcast.35.core_ref, bf16[2,512,768]{2,1,0:T(8,128)(2,1)} %pad_maximum_fusion.3.x_ref, bf16[768,1024]{1,0:T(8,128)(2,1)} %bitcast.37.own_ref, bf16[768,1024]{1,0:T(8,128)(2,1)} %collective-permute-done.35.other_ref), custom_call_target="tpu_custom_call" | custom-call | tf_op jit(solution)/shard_map/cond/branch_1_fun/logits/pallas_call | solution.py:131
  76.4 0.7 pad_maximum_fusion.4
  77.1 0.3 collective-permute-start.41
  77.3 0.6 collective-permute-start.40
  77.9 3.5 %collective-permute-start.39 = (f32[9,128]{1,0:T(8,128)S(1)}, f32[9,128]{1,0:T(8,128)S(1)}, u32[]{:S(2)}, u32[]{:S(2)}) collective-permute-start(f32[9,128]{1,0:T(8,128)S(1)} %pad_maximum_fusion.4), channel_id=1, source_target_pairs={{0,1},{1,0},{2,3},{3,2},{4,5},{5,4},{6,7},{7,6},{8,9},{9,8},{10,11... | collective-permute-start | bytes 13832 | tf_op jit(solution)/shard_map/cond/branch_1_fun/ppermute | solution.py:23
  81.5 6.8 %collective-permute-start.52 = (bf16[22,64,128]{2,1,0:T(8,128)(2,1)}, bf16[22,64,128]{2,1,0:T(8,128)(2,1)S(1)}, u32[]{:S(2)}, u32[]{:S(2)}) collective-permute-start(bf16[22,64,128]{2,1,0:T(8,128)(2,1)} %get-tuple-element.89), channel_id=1, source_target_pairs={{0,2},{1,3},{2,0},{3,1},{4,6},{5,7},{6,4},{7,5},{8,10},{9,11},{10,... | collective-permute-start | bytes 1081352 | tf_op jit(solution)/shard_map/cond/branch_1_fun/ppermute | solution.py:23
  88.3 2.0 collective-permute-start.53
  90.3 3.3 %mapped.6 = (bf16[64,1024]{1,0:T(8,128)(2,1)}, bf16[64,1024]{1,0:T(8,128)(2,1)}, bf16[64,1024]{1,0:T(8,128)(2,1)}, bf16[64,1024]{1,0:T(8,128)(2,1)}) custom-call(s32[6,64]{1,0:T(8,128)S(1)} %get-tuple-element.72.tab_ref, bf16[40,64,128]{2,1,0:T(8,128)(2,1)} %get-tuple-element.74.refs_0_, bf16[32,64,128]{2,1,0:T(8,128)(2,1)} %collective-permute-done.45.refs_1_, ...), custom_call_target="tpu_custom_call" | custom-call | tf_op jit(solution)/shard_map/cond/branch_1_fun/mapped/pallas_call | solution.py:96
  93.7 1.0 collective-permute-start.48
  94.8 2.1 %collective-permute-start.44 = (f32[10,128]{1,0:T(8,128)S(1)}, f32[10,128]{1,0:T(8,128)S(1)}, u32[]{:S(2)}, u32[]{:S(2)}) collective-permute-start(f32[10,128]{1,0:T(8,128)S(1)} %pad_maximum_fusion.5.refs_0_), channel_id=1, source_target_pairs={{0,24},{4,28},{8,16},{12,20},{16,8},{20,12},{24,0},{28,4},{1,25},{... | collective-permute-start | bytes 15368 | tf_op jit(solution)/shard_map/cond/branch_1_fun/ppermute | solution.py:23
  96.9 16.3 %collective-permute-done.52.refs_2_ = bf16[22,64,128]{2,1,0:T(8,128)(2,1)S(1)} collective-permute-done((bf16[22,64,128]{2,1,0:T(8,128)(2,1)}, bf16[22,64,128]{2,1,0:T(8,128)(2,1)S(1)}, u32[]{:S(2)}, u32[]{:S(2)}) %collective-permute-start.52) | collective-permute-done | bytes 360480 | tf_op jit(solution)/shard_map/cond/branch_1_fun/ppermute | solution.py:23
  113.2 0.9 collective-permute-start.43
  114.2 0.6 collective-permute-start.42
  114.7 5.8 %collective-permute-done.51.refs_1_ = bf16[32,64,128]{2,1,0:T(8,128)(2,1)S(1)} collective-permute-done((bf16[32,64,128]{2,1,0:T(8,128)(2,1)}, bf16[32,64,128]{2,1,0:T(8,128)(2,1)S(1)}, u32[]{:S(2)}, u32[]{:S(2)}) %collective-permute-start.51) | collective-permute-done | bytes 524320 | tf_op jit(solution)/shard_map/cond/branch_1_fun/ppermute | solution.py:23
  120.6 0.9 collective-permute-start.49
  121.5 3.3 %mapped.7 = (bf16[64,1024]{1,0:T(8,128)(2,1)}, bf16[64,1024]{1,0:T(8,128)(2,1)}, bf16[64,1024]{1,0:T(8,128)(2,1)}, bf16[64,1024]{1,0:T(8,128)(2,1)}) custom-call(s32[6,64]{1,0:T(8,128)S(1)} %get-tuple-element.72.tab_ref, bf16[40,64,128]{2,1,0:T(8,128)(2,1)} %get-tuple-element.77.refs_0_, bf16[32,64,128]{2,1,0:T(8,128)(2,1)} %copy-done.10, ...), custom_call_target="tpu_custom_call" | custom-call | tf_op jit(solution)/shard_map/cond/branch_1_fun/mapped/pallas_call | solution.py:96
  124.9 0.8 collective-permute-start.50
  125.7 1.8 collective-permute-start.54
  127.5 0.9 collective-permute-start.55
  128.4 0.8 collective-permute-start.56
  129.2 1.8 stats.3
  131.0 0.5 collective-permute-done.50.refs_2_
  131.5 2.1 %collective-permute-done.54.refs_4_ = bf16[64,1024]{1,0:T(8,128)(2,1)S(1)} collective-permute-done((bf16[64,1024]{1,0:T(8,128)(2,1)}, bf16[64,1024]{1,0:T(8,128)(2,1)S(1)}, u32[]{:S(2)}, u32[]{:S(2)}) %collective-permute-start.54) | collective-permute-done | bytes 131104 | tf_op jit(solution)/shard_map/cond/branch_1_fun/ppermute | solution.py:23
  133.6 0.5 collective-permute-done.55.refs_5_
  134.1 0.5 collective-permute-done.56.refs_6_
  134.7 0.5 copy-done.26
  135.2 6.2 %grads.3 = (bf16[4,128,1024]{2,1,0:T(8,128)(2,1)}, bf16[2,128,768]{2,1,0:T(8,128)(2,1)}, bf16[2,128,768]{2,1,0:T(8,128)(2,1)}, bf16[2,128,768]{2,1,0:T(8,128)(2,1)}, bf16[2,128,768]{2,1,0:T(8,128)(2,1)}) custom-call(s32[1]{0:T(128)} %bitcast.35.core_ref, f32[4,128,1024]{2,1,0:T(8,128)} %get-tuple-element.70.e_ref, f32[4,128,1]{2,1,0:T(8,128)} %get-tuple-element.79.a_ref, ...), custom_call_target="tpu_custom_call" | custom-call | tf_op jit(solution)/shard_map/cond/branch_1_fun/grads/pallas_call | solution.py:183
  141.4 3.4 %convolution_convert_fusion.2 = bf16[768,1024]{1,0:T(8,128)(2,1)} fusion(bf16[512,1024]{1,0:T(8,128)(2,1)} %bitcast.164, bf16[2,512,768]{2,1,0:T(8,128)(2,1)S(1)} %copy-done.3, s32[]{:T(128)S(6)} %select_n.91), kind=kOutput, calls=%fused_computation.63 | convolution fusion | flops 806092800 | bytes 3407876 | tf_op jit(solution)/shard_map/cond/branch_1_fun/dot_general | solution.py:317
  144.7 2.2 %convolution_convert_fusion.3 = bf16[768,1024]{1,0:T(8,128)(2,1)S(1)} fusion(bf16[512,1024]{1,0:T(8,128)(2,1)} %bitcast.165, bf16[2,512,768]{2,1,0:T(8,128)(2,1)S(1)} %copy-done.3, s32[]{:T(128)S(6)} %select_n.86), kind=kOutput, calls=%fused_computation.64 | convolution fusion | flops 806092800 | bytes 3407876 | tf_op jit(solution)/shard_map/cond/branch_1_fun/dot_general | solution.py:317
  147.0 1.4 collective-permute-done.57
  148.4 1.8 add_convert_fusion.2
  150.2 3.7 %all-to-all-start.3 = ((bf16[4,192,1024]{2,1,0:T(8,128)(2,1)}), bf16[4,192,1024]{2,1,0:T(8,128)(2,1)S(1)}, u32[]{:S(2)}, u32[]{:S(2)}) async-start(bf16[4,192,1024]{2,1,0:T(8,128)(2,1)} %bitcast.53), calls=%async_computation.3 | async-start | bytes 3145728 | tf_op jit(solution)/shard_map/cond/branch_1_fun/all_to_all | solution.py:323
  153.9 2.9 %collective-permute-start.58 = (bf16[2,128,768]{2,1,0:T(8,128)(2,1)S(1)}, bf16[2,128,768]{2,1,0:T(8,128)(2,1)S(1)}, u32[]{:S(2)}, u32[]{:S(2)}) collective-permute-start(bf16[2,128,768]{2,1,0:T(8,128)(2,1)S(1)} %copy-done.46), channel_id=1, source_target_pairs={{0,24},{4,28},{8,16},{12,20},{16,8},{20,12},{24,0},{28,4},{1,25},{... | collective-permute-start | bytes 1179656 | tf_op jit(solution)/shard_map/cond/branch_1_fun/ppermute | solution.py:23
  156.8 0.6 collective-permute-start.59
  157.5 26.4 %collective-permute-done.58 = bf16[2,128,768]{2,1,0:T(8,128)(2,1)S(1)} collective-permute-done((bf16[2,128,768]{2,1,0:T(8,128)(2,1)S(1)}, bf16[2,128,768]{2,1,0:T(8,128)(2,1)S(1)}, u32[]{:S(2)}, u32[]{:S(2)}) %collective-permute-start.58) | collective-permute-done | bytes 393248 | tf_op jit(solution)/shard_map/cond/branch_1_fun/ppermute | solution.py:23
  183.9 6.6 %collective-permute-done.59 = bf16[2,128,768]{2,1,0:T(8,128)(2,1)S(1)} collective-permute-done((bf16[2,128,768]{2,1,0:T(8,128)(2,1)S(1)}, bf16[2,128,768]{2,1,0:T(8,128)(2,1)S(1)}, u32[]{:S(2)}, u32[]{:S(2)}) %collective-permute-start.59) | collective-permute-done | bytes 393248 | tf_op jit(solution)/shard_map/cond/branch_1_fun/ppermute | solution.py:23
  191.1 1.4 collective-permute-start.61
  192.5 2.3 %collective-permute-start.63 = (bf16[128,384]{0,1:T(8,128)(2,1)S(1)}, bf16[128,384]{0,1:T(8,128)(2,1)S(1)}, u32[]{:S(2)}, u32[]{:S(2)}) collective-permute-start(bf16[128,384]{0,1:T(8,128)(2,1)S(1)} %get-tuple-element.183), channel_id=1, source_target_pairs={{0,3},{1,2},{2,1},{3,0},{4,7},{5,6},{6,5},{7,4},{8,11},{9,10},{10,... | collective-permute-start | bytes 294920 | tf_op jit(solution)/shard_map/cond/branch_1_fun/ppermute | solution.py:23
  194.8 1.0 collective-permute-done.61
  195.8 4.3 %collective-permute-done.63 = bf16[128,384]{0,1:T(8,128)(2,1)S(1)} collective-permute-done((bf16[128,384]{0,1:T(8,128)(2,1)S(1)}, bf16[128,384]{0,1:T(8,128)(2,1)S(1)}, u32[]{:S(2)}, u32[]{:S(2)}) %collective-permute-start.63) | collective-permute-done | bytes 98336 | tf_op jit(solution)/shard_map/cond/branch_1_fun/ppermute | solution.py:23
  200.1 3.2 %collective-permute-done.62 = bf16[128,384]{0,1:T(8,128)(2,1)S(1)} collective-permute-done((bf16[128,384]{0,1:T(8,128)(2,1)S(1)}, bf16[128,384]{0,1:T(8,128)(2,1)S(1)}, u32[]{:S(2)}, u32[]{:S(2)}) %collective-permute-start.62) | collective-permute-done | bytes 98336 | tf_op jit(solution)/shard_map/cond/branch_1_fun/ppermute | solution.py:23
  203.3 1.3 copy.100
  204.6 0.8 copy.96
  (105 shorter events, 2.9 us)
Async XLA Ops:
  6.4 25.0 %copy-start.1 = (bf16[32,2,128,128]{3,2,1,0:T(8,128)(2,1)S(1)}, bf16[32,2,128,128]{3,2,1,0:T(8,128)(2,1)}, u32[]{:S(2)}) copy-start(bf16[32,2,128,128]{3,2,1,0:T(8,128)(2,1)} %get-tuple-element.76.refs_4_) | copy-start | bytes 6291460
  31.4 5.7 %copy-start.7 = (bf16[128,1536]{1,0:T(8,128)(2,1)S(1)}, bf16[128,1536]{1,0:T(8,128)(2,1)}, u32[]{:S(2)}) copy-start(bf16[128,1536]{1,0:T(8,128)(2,1)} %get-tuple-element.158) | copy-start | bytes 1179652
  31.4 38.7 %collective-permute-start.35 = (bf16[768,1024]{1,0:T(8,128)(2,1)}, bf16[768,1024]{1,0:T(8,128)(2,1)}, u32[]{:S(2)}, u32[]{:S(2)}) collective-permute-start(bf16[768,1024]{1,0:T(8,128)(2,1)} %bitcast.37.own_ref), channel_id=1, source_target_pairs={{0,4},{4,0},{8,12},{12,8},{16,20},{20,16},{24,28},{28,24},{1,5},{5... | collective-permute-start | bytes 4718600 | tf_op jit(solution)/shard_map/cond/branch_1_fun/ppermute | solution.py:23
  32.6 5.8 %copy-start.32 = (s32[128,2]{0,1:T(2,128)S(1)}, s32[128,2]{0,1:T(2,128)}, u32[]{:S(2)}) copy-start(s32[128,2]{0,1:T(2,128)} %get-tuple-element.162) | copy-start | bytes 3076
  32.6 13.7 %collective-permute-start.38 = (f32[64,128]{1,0:T(8,128)}, f32[64,128]{1,0:T(8,128)}, u32[]{:S(2)}, u32[]{:S(2)}) collective-permute-start(f32[64,128]{1,0:T(8,128)} %bitcast.45), channel_id=1, source_target_pairs={{0,3},{1,2},{2,1},{3,0},{4,7},{5,6},{6,5},{7,4},{8,11},{9,10},{10,... | collective-permute-start | bytes 98312 | tf_op jit(solution)/shard_map/cond/branch_1_fun/ppermute | solution.py:23
  36.2 10.6 %collective-permute-start.37 = (f32[64,128]{1,0:T(8,128)}, f32[64,128]{1,0:T(8,128)}, u32[]{:S(2)}, u32[]{:S(2)}) collective-permute-start(f32[64,128]{1,0:T(8,128)} %bitcast.45), channel_id=1, source_target_pairs={{0,2},{1,3},{2,0},{3,1},{4,6},{5,7},{6,4},{7,5},{8,10},{9,11},{10,... | collective-permute-start | bytes 98312 | tf_op jit(solution)/shard_map/cond/branch_1_fun/ppermute | solution.py:23
  36.2 12.7 %collective-permute-start.36 = (f32[64,128]{1,0:T(8,128)}, f32[64,128]{1,0:T(8,128)}, u32[]{:S(2)}, u32[]{:S(2)}) collective-permute-start(f32[64,128]{1,0:T(8,128)} %bitcast.45), channel_id=1, source_target_pairs={{0,1},{1,0},{2,3},{3,2},{4,5},{5,4},{6,7},{7,6},{8,9},{9,8},{10,11... | collective-permute-start | bytes 98312 | tf_op jit(solution)/shard_map/cond/branch_1_fun/ppermute | solution.py:23
  37.5 15.2 %collective-permute-start.34 = (bf16[2,128,768]{2,1,0:T(8,128)(2,1)S(1)}, bf16[2,128,768]{2,1,0:T(8,128)(2,1)S(1)}, u32[]{:S(2)}, u32[]{:S(2)}) collective-permute-start(bf16[2,128,768]{2,1,0:T(8,128)(2,1)S(1)} %copy.82), channel_id=1, source_target_pairs={{0,8},{4,12},{8,0},{12,4},{16,24},{20,28},{24,16},{28,20},{1,9},{5... | collective-permute-start | bytes 1179656 | tf_op jit(solution)/shard_map/cond/branch_1_fun/ppermute | solution.py:23
  42.5 8.6 %copy-start.4 = (bf16[40,64,128]{2,1,0:T(8,128)(2,1)S(1)}, bf16[40,64,128]{2,1,0:T(8,128)(2,1)}, u32[]{:S(2)}) copy-start(bf16[40,64,128]{2,1,0:T(8,128)(2,1)} %get-tuple-element.74.refs_0_) | copy-start | bytes 1966084
  46.3 18.9 %collective-permute-start.33 = (bf16[2,128,768]{2,1,0:T(8,128)(2,1)S(1)}, bf16[2,128,768]{2,1,0:T(8,128)(2,1)S(1)}, u32[]{:S(2)}, u32[]{:S(2)}) collective-permute-start(bf16[2,128,768]{2,1,0:T(8,128)(2,1)S(1)} %copy.82), channel_id=1, source_target_pairs={{0,16},{4,20},{8,24},{12,28},{16,0},{20,4},{24,8},{28,12},{1,17},{... | collective-permute-start | bytes 1179656 | tf_op jit(solution)/shard_map/cond/branch_1_fun/ppermute | solution.py:23
  46.9 21.9 %collective-permute-start.32 = (bf16[2,128,768]{2,1,0:T(8,128)(2,1)S(1)}, bf16[2,128,768]{2,1,0:T(8,128)(2,1)S(1)}, u32[]{:S(2)}, u32[]{:S(2)}) collective-permute-start(bf16[2,128,768]{2,1,0:T(8,128)(2,1)S(1)} %copy.82), channel_id=1, source_target_pairs={{0,24},{4,28},{8,16},{12,20},{16,8},{20,12},{24,0},{28,4},{1,25},{... | collective-permute-start | bytes 1179656 | tf_op jit(solution)/shard_map/cond/branch_1_fun/ppermute | solution.py:23
  48.9 39.4 %collective-permute-start.45 = (bf16[32,64,128]{2,1,0:T(8,128)(2,1)}, bf16[32,64,128]{2,1,0:T(8,128)(2,1)}, u32[]{:S(2)}, u32[]{:S(2)}) collective-permute-start(bf16[32,64,128]{2,1,0:T(8,128)(2,1)} %get-tuple-element.81), channel_id=1, source_target_pairs={{0,1},{1,0},{2,3},{3,2},{4,5},{5,4},{6,7},{7,6},{8,9},{9,8},{10,11... | collective-permute-start | bytes 1572872 | tf_op jit(solution)/shard_map/cond/branch_1_fun/ppermute | solution.py:23
  52.6 25.3 %collective-permute-start.46 = (bf16[22,64,128]{2,1,0:T(8,128)(2,1)}, bf16[22,64,128]{2,1,0:T(8,128)(2,1)S(1)}, u32[]{:S(2)}, u32[]{:S(2)}) collective-permute-start(bf16[22,64,128]{2,1,0:T(8,128)(2,1)} %get-tuple-element.82), channel_id=1, source_target_pairs={{0,2},{1,3},{2,0},{3,1},{4,6},{5,7},{6,4},{7,5},{8,10},{9,11},{10,... | collective-permute-start | bytes 1081352 | tf_op jit(solution)/shard_map/cond/branch_1_fun/ppermute | solution.py:23
  65.2 16.2 %collective-permute-start.47 = (bf16[22,64,128]{2,1,0:T(8,128)(2,1)}, bf16[22,64,128]{2,1,0:T(8,128)(2,1)}, u32[]{:S(2)}, u32[]{:S(2)}) collective-permute-start(bf16[22,64,128]{2,1,0:T(8,128)(2,1)} %get-tuple-element.83), channel_id=1, source_target_pairs={{0,3},{1,2},{2,1},{3,0},{4,7},{5,6},{6,5},{7,4},{8,11},{9,10},{10,... | collective-permute-start | bytes 1081352 | tf_op jit(solution)/shard_map/cond/branch_1_fun/ppermute | solution.py:23
  77.1 16.6 %collective-permute-start.41 = (f32[9,128]{1,0:T(8,128)S(1)}, f32[9,128]{1,0:T(8,128)S(1)}, u32[]{:S(2)}, u32[]{:S(2)}) collective-permute-start(f32[9,128]{1,0:T(8,128)S(1)} %pad_maximum_fusion.4), channel_id=1, source_target_pairs={{0,3},{1,2},{2,1},{3,0},{4,7},{5,6},{6,5},{7,4},{8,11},{9,10},{10,... | collective-permute-start | bytes 13832 | tf_op jit(solution)/shard_map/cond/branch_1_fun/ppermute | solution.py:23
  77.3 16.4 %collective-permute-start.40 = (f32[9,128]{1,0:T(8,128)S(1)}, f32[9,128]{1,0:T(8,128)S(1)}, u32[]{:S(2)}, u32[]{:S(2)}) collective-permute-start(f32[9,128]{1,0:T(8,128)S(1)} %pad_maximum_fusion.4), channel_id=1, source_target_pairs={{0,2},{1,3},{2,0},{3,1},{4,6},{5,7},{6,4},{7,5},{8,10},{9,11},{10,... | collective-permute-start | bytes 13832 | tf_op jit(solution)/shard_map/cond/branch_1_fun/ppermute | solution.py:23
  77.9 12.4 %copy-start.15 = (bf16[22,64,128]{2,1,0:T(8,128)(2,1)}, bf16[22,64,128]{2,1,0:T(8,128)(2,1)S(1)}, u32[]{:S(2)}) copy-start(bf16[22,64,128]{2,1,0:T(8,128)(2,1)S(1)} %collective-permute-done.46.refs_2_) | copy-start | bytes 1081348
  77.9 16.8 %collective-permute-start.39 = (f32[9,128]{1,0:T(8,128)S(1)}, f32[9,128]{1,0:T(8,128)S(1)}, u32[]{:S(2)}, u32[]{:S(2)}) collective-permute-start(f32[9,128]{1,0:T(8,128)S(1)} %pad_maximum_fusion.4), channel_id=1, source_target_pairs={{0,1},{1,0},{2,3},{3,2},{4,5},{5,4},{6,7},{7,6},{8,9},{9,8},{10,11... | collective-permute-start | bytes 13832 | tf_op jit(solution)/shard_map/cond/branch_1_fun/ppermute | solution.py:23
  81.5 31.8 %collective-permute-start.52 = (bf16[22,64,128]{2,1,0:T(8,128)(2,1)}, bf16[22,64,128]{2,1,0:T(8,128)(2,1)S(1)}, u32[]{:S(2)}, u32[]{:S(2)}) collective-permute-start(bf16[22,64,128]{2,1,0:T(8,128)(2,1)} %get-tuple-element.89), channel_id=1, source_target_pairs={{0,2},{1,3},{2,0},{3,1},{4,6},{5,7},{6,4},{7,5},{8,10},{9,11},{10,... | collective-permute-start | bytes 1081352 | tf_op jit(solution)/shard_map/cond/branch_1_fun/ppermute | solution.py:23
  88.3 6.4 %copy-start.28 = (f32[2,4,128]{2,1,0:T(4,128)S(1)}, f32[2,4,128]{2,1,0:T(4,128)}, u32[]{:S(2)}) copy-start(f32[2,4,128]{2,1,0:T(4,128)} %get-tuple-element.71.own_ref) | copy-start | bytes 12292
  88.3 6.5 %copy-start.40 = (f32[128]{0:T(128)S(1)}, f32[128]{0:T(128)}, u32[]{:S(2)}) copy-start(f32[128]{0:T(128)} %get-tuple-element.78) | copy-start | bytes 1540
  88.3 25.9 %collective-permute-start.53 = (bf16[22,64,128]{2,1,0:T(8,128)(2,1)}, bf16[22,64,128]{2,1,0:T(8,128)(2,1)S(1)}, u32[]{:S(2)}, u32[]{:S(2)}) collective-permute-start(bf16[22,64,128]{2,1,0:T(8,128)(2,1)} %get-tuple-element.90), channel_id=1, source_target_pairs={{0,3},{1,2},{2,1},{3,0},{4,7},{5,6},{6,5},{7,4},{8,11},{9,10},{10,... | collective-permute-start | bytes 1081352 | tf_op jit(solution)/shard_map/cond/branch_1_fun/ppermute | solution.py:23
  93.6 26.9 %collective-permute-start.51 = (bf16[32,64,128]{2,1,0:T(8,128)(2,1)}, bf16[32,64,128]{2,1,0:T(8,128)(2,1)S(1)}, u32[]{:S(2)}, u32[]{:S(2)}) collective-permute-start(bf16[32,64,128]{2,1,0:T(8,128)(2,1)} %get-tuple-element.88), channel_id=1, source_target_pairs={{0,1},{1,0},{2,3},{3,2},{4,5},{5,4},{6,7},{7,6},{8,9},{9,8},{10,11... | collective-permute-start | bytes 1572872 | tf_op jit(solution)/shard_map/cond/branch_1_fun/ppermute | solution.py:23
  93.7 31.1 %collective-permute-start.48 = (bf16[64,1024]{1,0:T(8,128)(2,1)}, bf16[64,1024]{1,0:T(8,128)(2,1)S(1)}, u32[]{:S(2)}, u32[]{:S(2)}) collective-permute-start(bf16[64,1024]{1,0:T(8,128)(2,1)} %get-tuple-element.84), channel_id=1, source_target_pairs={{0,24},{4,28},{8,16},{12,20},{16,8},{20,12},{24,0},{28,4},{1,25},{... | collective-permute-start | bytes 393224 | tf_op jit(solution)/shard_map/cond/branch_1_fun/ppermute | solution.py:23
  94.8 34.4 %copy-start.30 = (f32[10,128]{1,0:T(8,128)}, f32[10,128]{1,0:T(8,128)S(1)}, u32[]{:S(2)}) copy-start(f32[10,128]{1,0:T(8,128)S(1)} %pad_maximum_fusion.5.refs_0_) | copy-start | bytes 15364
  94.8 30.9 %collective-permute-start.44 = (f32[10,128]{1,0:T(8,128)S(1)}, f32[10,128]{1,0:T(8,128)S(1)}, u32[]{:S(2)}, u32[]{:S(2)}) collective-permute-start(f32[10,128]{1,0:T(8,128)S(1)} %pad_maximum_fusion.5.refs_0_), channel_id=1, source_target_pairs={{0,24},{4,28},{8,16},{12,20},{16,8},{20,12},{24,0},{28,4},{1,25},{... | collective-permute-start | bytes 15368 | tf_op jit(solution)/shard_map/cond/branch_1_fun/ppermute | solution.py:23
  113.2 8.3 %copy-start.13 = (bf16[22,64,128]{2,1,0:T(8,128)(2,1)}, bf16[22,64,128]{2,1,0:T(8,128)(2,1)S(1)}, u32[]{:S(2)}) copy-start(bf16[22,64,128]{2,1,0:T(8,128)(2,1)S(1)} %collective-permute-done.52.refs_2_) | copy-start | bytes 1081348
  113.2 14.3 %collective-permute-start.43 = (f32[10,128]{1,0:T(8,128)S(1)}, f32[10,128]{1,0:T(8,128)S(1)}, u32[]{:S(2)}, u32[]{:S(2)}) collective-permute-start(f32[10,128]{1,0:T(8,128)S(1)} %pad_maximum_fusion.5.refs_0_), channel_id=1, source_target_pairs={{0,16},{4,20},{8,24},{12,28},{16,0},{20,4},{24,8},{28,12},{1,17},{... | collective-permute-start | bytes 15368 | tf_op jit(solution)/shard_map/cond/branch_1_fun/ppermute | solution.py:23
  114.2 7.3 %copy-start.14 = (bf16[22,64,128]{2,1,0:T(8,128)(2,1)}, bf16[22,64,128]{2,1,0:T(8,128)(2,1)S(1)}, u32[]{:S(2)}) copy-start(bf16[22,64,128]{2,1,0:T(8,128)(2,1)S(1)} %collective-permute-done.53.refs_3_) | copy-start | bytes 1081348
  114.2 14.3 %collective-permute-start.42 = (f32[10,128]{1,0:T(8,128)S(1)}, f32[10,128]{1,0:T(8,128)S(1)}, u32[]{:S(2)}, u32[]{:S(2)}) collective-permute-start(f32[10,128]{1,0:T(8,128)S(1)} %pad_maximum_fusion.5.refs_0_), channel_id=1, source_target_pairs={{0,8},{4,12},{8,0},{12,4},{16,24},{20,28},{24,16},{28,20},{1,9},{5... | collective-permute-start | bytes 15368 | tf_op jit(solution)/shard_map/cond/branch_1_fun/ppermute | solution.py:23
  120.6 0.9 copy-start.10
  120.6 10.4 %collective-permute-start.49 = (bf16[64,1024]{1,0:T(8,128)(2,1)}, bf16[64,1024]{1,0:T(8,128)(2,1)}, u32[]{:S(2)}, u32[]{:S(2)}) collective-permute-start(bf16[64,1024]{1,0:T(8,128)(2,1)} %get-tuple-element.85), channel_id=1, source_target_pairs={{0,16},{4,20},{8,24},{12,28},{16,0},{20,4},{24,8},{28,12},{1,17},{... | collective-permute-start | bytes 393224 | tf_op jit(solution)/shard_map/cond/branch_1_fun/ppermute | solution.py:23
  124.8 9.7 %copy-start.17 = (bf16[64,1024]{1,0:T(8,128)(2,1)}, bf16[64,1024]{1,0:T(8,128)(2,1)S(1)}, u32[]{:S(2)}) copy-start(bf16[64,1024]{1,0:T(8,128)(2,1)S(1)} %collective-permute-done.48.refs_0_) | copy-start | bytes 393220
  124.9 6.6 %collective-permute-start.50 = (bf16[64,1024]{1,0:T(8,128)(2,1)}, bf16[64,1024]{1,0:T(8,128)(2,1)S(1)}, u32[]{:S(2)}, u32[]{:S(2)}) collective-permute-start(bf16[64,1024]{1,0:T(8,128)(2,1)} %get-tuple-element.86), channel_id=1, source_target_pairs={{0,8},{4,12},{8,0},{12,4},{16,24},{20,28},{24,16},{28,20},{1,9},{5... | collective-permute-start | bytes 393224 | tf_op jit(solution)/shard_map/cond/branch_1_fun/ppermute | solution.py:23
  125.7 3.5 %copy-start.34 = (f32[10,128]{1,0:T(8,128)}, f32[10,128]{1,0:T(8,128)S(1)}, u32[]{:S(2)}) copy-start(f32[10,128]{1,0:T(8,128)S(1)} %collective-permute-done.44.refs_3_) | copy-start | bytes 15364
  125.7 7.9 %collective-permute-start.54 = (bf16[64,1024]{1,0:T(8,128)(2,1)}, bf16[64,1024]{1,0:T(8,128)(2,1)S(1)}, u32[]{:S(2)}, u32[]{:S(2)}) collective-permute-start(bf16[64,1024]{1,0:T(8,128)(2,1)} %get-tuple-element.91), channel_id=1, source_target_pairs={{0,24},{4,28},{8,16},{12,20},{16,8},{20,12},{24,0},{28,4},{1,25},{... | collective-permute-start | bytes 393224 | tf_op jit(solution)/shard_map/cond/branch_1_fun/ppermute | solution.py:23
  127.5 1.7 copy-start.36
  127.5 6.6 %collective-permute-start.55 = (bf16[64,1024]{1,0:T(8,128)(2,1)}, bf16[64,1024]{1,0:T(8,128)(2,1)S(1)}, u32[]{:S(2)}, u32[]{:S(2)}) collective-permute-start(bf16[64,1024]{1,0:T(8,128)(2,1)} %get-tuple-element.92), channel_id=1, source_target_pairs={{0,16},{4,20},{8,24},{12,28},{16,0},{20,4},{24,8},{28,12},{1,17},{... | collective-permute-start | bytes 393224 | tf_op jit(solution)/shard_map/cond/branch_1_fun/ppermute | solution.py:23
  128.4 0.8 copy-start.38
  128.4 6.1 %collective-permute-start.56 = (bf16[64,1024]{1,0:T(8,128)(2,1)}, bf16[64,1024]{1,0:T(8,128)(2,1)S(1)}, u32[]{:S(2)}, u32[]{:S(2)}) collective-permute-start(bf16[64,1024]{1,0:T(8,128)(2,1)} %get-tuple-element.93), channel_id=1, source_target_pairs={{0,8},{4,12},{8,0},{12,4},{16,24},{20,28},{24,16},{28,20},{1,9},{5... | collective-permute-start | bytes 393224 | tf_op jit(solution)/shard_map/cond/branch_1_fun/ppermute | solution.py:23
  131.5 3.1 %copy-start.20 = (bf16[64,1024]{1,0:T(8,128)(2,1)}, bf16[64,1024]{1,0:T(8,128)(2,1)S(1)}, u32[]{:S(2)}) copy-start(bf16[64,1024]{1,0:T(8,128)(2,1)S(1)} %collective-permute-done.50.refs_2_) | copy-start | bytes 393220
  133.6 1.0 copy-start.22
  134.1 0.7 copy-start.24
  134.6 0.6 copy-start.26
  135.2 6.2 %copy-start.3 = (bf16[2,512,768]{2,1,0:T(8,128)(2,1)S(1)}, bf16[2,512,768]{2,1,0:T(8,128)(2,1)}, u32[]{:S(2)}) copy-start(bf16[2,512,768]{2,1,0:T(8,128)(2,1)} %pad_maximum_fusion.3.x_ref) | copy-start | bytes 4718596
  144.7 3.6 %collective-permute-start.57 = (bf16[768,1024]{1,0:T(8,128)(2,1)}, bf16[768,1024]{1,0:T(8,128)(2,1)S(1)}, u32[]{:S(2)}, u32[]{:S(2)}) collective-permute-start(bf16[768,1024]{1,0:T(8,128)(2,1)} %convolution_convert_fusion.2), channel_id=1, source_target_pairs={{0,4},{4,0},{8,12},{12,8},{16,20},{20,16},{24,28},{28,24},{1,5},{5... | collective-permute-start | bytes 4718600 | tf_op jit(solution)/shard_map/cond/branch_1_fun/ppermute | solution.py:23
  150.2 3.7 %copy-start.46 = (bf16[2,128,768]{2,1,0:T(8,128)(2,1)S(1)}, bf16[2,128,768]{2,1,0:T(8,128)(2,1)}, u32[]{:S(2)}) copy-start(bf16[2,128,768]{2,1,0:T(8,128)(2,1)} %get-tuple-element.97) | copy-start | bytes 1179652
  150.2 6.6 %copy-start.44 = (bf16[2,128,768]{2,1,0:T(8,128)(2,1)S(1)}, bf16[2,128,768]{2,1,0:T(8,128)(2,1)}, u32[]{:S(2)}) copy-start(bf16[2,128,768]{2,1,0:T(8,128)(2,1)} %get-tuple-element.98) | copy-start | bytes 1179652
  150.2 7.2 %copy-start.42 = (bf16[2,128,768]{2,1,0:T(8,128)(2,1)S(1)}, bf16[2,128,768]{2,1,0:T(8,128)(2,1)}, u32[]{:S(2)}) copy-start(bf16[2,128,768]{2,1,0:T(8,128)(2,1)} %get-tuple-element.99) | copy-start | bytes 1179652
  150.2 40.4 %copy-start.12 = (bf16[2,128,768]{2,1,0:T(8,128)(2,1)S(1)}, bf16[2,128,768]{2,1,0:T(8,128)(2,1)}, u32[]{:S(2)}) copy-start(bf16[2,128,768]{2,1,0:T(8,128)(2,1)} %get-tuple-element.96) | copy-start | bytes 1179652
  150.2 53.1 %all-to-all-start.3 = ((bf16[4,192,1024]{2,1,0:T(8,128)(2,1)}), bf16[4,192,1024]{2,1,0:T(8,128)(2,1)S(1)}, u32[]{:S(2)}, u32[]{:S(2)}) async-start(bf16[4,192,1024]{2,1,0:T(8,128)(2,1)} %bitcast.53), calls=%async_computation.3 | async-start | bytes 3145728 | tf_op jit(solution)/shard_map/cond/branch_1_fun/all_to_all | solution.py:323
  153.9 30.0 %collective-permute-start.58 = (bf16[2,128,768]{2,1,0:T(8,128)(2,1)S(1)}, bf16[2,128,768]{2,1,0:T(8,128)(2,1)S(1)}, u32[]{:S(2)}, u32[]{:S(2)}) collective-permute-start(bf16[2,128,768]{2,1,0:T(8,128)(2,1)S(1)} %copy-done.46), channel_id=1, source_target_pairs={{0,24},{4,28},{8,16},{12,20},{16,8},{20,12},{24,0},{28,4},{1,25},{... | collective-permute-start | bytes 1179656 | tf_op jit(solution)/shard_map/cond/branch_1_fun/ppermute | solution.py:23
  156.8 33.7 %collective-permute-start.59 = (bf16[2,128,768]{2,1,0:T(8,128)(2,1)S(1)}, bf16[2,128,768]{2,1,0:T(8,128)(2,1)S(1)}, u32[]{:S(2)}, u32[]{:S(2)}) collective-permute-start(bf16[2,128,768]{2,1,0:T(8,128)(2,1)S(1)} %copy-done.44), channel_id=1, source_target_pairs={{0,16},{4,20},{8,24},{12,28},{16,0},{20,4},{24,8},{28,12},{1,17},{... | collective-permute-start | bytes 1179656 | tf_op jit(solution)/shard_map/cond/branch_1_fun/ppermute | solution.py:23
  157.4 33.2 %collective-permute-start.60 = (bf16[2,128,768]{2,1,0:T(8,128)(2,1)S(1)}, bf16[2,128,768]{2,1,0:T(8,128)(2,1)S(1)}, u32[]{:S(2)}, u32[]{:S(2)}) collective-permute-start(bf16[2,128,768]{2,1,0:T(8,128)(2,1)S(1)} %copy-done.42), channel_id=1, source_target_pairs={{0,8},{4,12},{8,0},{12,4},{16,24},{20,28},{24,16},{28,20},{1,9},{5... | collective-permute-start | bytes 1179656 | tf_op jit(solution)/shard_map/cond/branch_1_fun/ppermute | solution.py:23
  191.1 4.7 %collective-permute-start.61 = (bf16[128,384]{0,1:T(8,128)(2,1)S(1)}, bf16[128,384]{0,1:T(8,128)(2,1)S(1)}, u32[]{:S(2)}, u32[]{:S(2)}) collective-permute-start(bf16[128,384]{0,1:T(8,128)(2,1)S(1)} %get-tuple-element.182), channel_id=1, source_target_pairs={{0,1},{1,0},{2,3},{3,2},{4,5},{5,4},{6,7},{7,6},{8,9},{9,8},{10,11... | collective-permute-start | bytes 294920 | tf_op jit(solution)/shard_map/cond/branch_1_fun/ppermute | solution.py:23
  192.5 7.6 %collective-permute-start.63 = (bf16[128,384]{0,1:T(8,128)(2,1)S(1)}, bf16[128,384]{0,1:T(8,128)(2,1)S(1)}, u32[]{:S(2)}, u32[]{:S(2)}) collective-permute-start(bf16[128,384]{0,1:T(8,128)(2,1)S(1)} %get-tuple-element.183), channel_id=1, source_target_pairs={{0,3},{1,2},{2,1},{3,0},{4,7},{5,6},{6,5},{7,4},{8,11},{9,10},{10,... | collective-permute-start | bytes 294920 | tf_op jit(solution)/shard_map/cond/branch_1_fun/ppermute | solution.py:23
  194.8 8.4 %collective-permute-start.62 = (bf16[128,384]{0,1:T(8,128)(2,1)S(1)}, bf16[128,384]{0,1:T(8,128)(2,1)S(1)}, u32[]{:S(2)}, u32[]{:S(2)}) collective-permute-start(bf16[128,384]{0,1:T(8,128)(2,1)S(1)} %get-tuple-element.184), channel_id=1, source_target_pairs={{0,2},{1,3},{2,0},{3,1},{4,6},{5,7},{6,4},{7,5},{8,10},{9,11},{10,... | collective-permute-start | bytes 294920 | tf_op jit(solution)/shard_map/cond/branch_1_fun/ppermute | solution.py:23

commit v4 on v3

--- a/solution.py
+++ b/solution.py
@@ -194,6 +194,13 @@
     )(core, e, a, b, own, other, *mapped)
 
 
+def sum_kernel(*refs):
+    total = refs[0][...].astype(F32)
+    for ref in refs[1:-1]:
+        total += ref[...].astype(F32)
+    refs[-1][...] = total.astype(BF16)
+
+
 def plan(align_index, pairs, count, chip):
     vocab = lax.axis_size("vocab")
     v = lax.axis_index("vocab")
@@ -307,9 +314,14 @@
     rows_sum = rows_sum.astype(BF16).reshape(2, tokens, chips, features // dp).transpose(1, 2, 0, 3)
     pieces = rows_sum.reshape(tokens, vocab, features // vocab).transpose(1, 0, 2)
     piece = lambda t: lax.dynamic_index_in_dim(pieces, v ^ t, 0, keepdims=False)
-    hidden_grad = piece(0).astype(F32)
     others = [swap(piece(t), "vocab", t) for t in range(1, vocab)]
-    hidden_grad = sum([x.astype(F32) for x in others], hidden_grad).astype(BF16)
+    hidden_grad = pl.pallas_call(
+        sum_kernel,
+        in_specs=[VMEM] * vocab,
+        out_specs=VMEM,
+        out_shape=jax.ShapeDtypeStruct(others[0].shape, BF16),
+        name="hidden_sum",
+    )(piece(0), *others)
     dl = dl.reshape(chips * tokens, -1)
 
     def head_half(half):

time: 206 us -> 207 us (level)
  waiting for transfers between devices: 78.3 us -> 75.9 us
    ppermute x32, waiting for transfers between devices: 78.3 us -> 75.9 us  [swap(): lax.ppermute(x, axis, [(i, i ^ bits) for i in range(lax.axis_size(axis))])]
  transfers between devices with their start and end apart: 33 -> 33, of which waited for: 14 -> 13; matrix products, arithmetic and copies ran while one was open for 5% -> 5% of each run, Pallas kernels for 11% -> 12%
where the time goes in v4:
time: 207 us
  waiting for transfers between devices  75.9 us (37%)
  starting transfers between devices  50.5 us (24%)
  Pallas kernels  30.1 us (15%)
  blocking collectives  25 us (12%)
  other arithmetic  8.98 us (4%)
  local copies, waits for them, and re-layouts  7.52 us (4%)
  matrix products  6.63 us (3%)
    ppermute x32, waiting for transfers between devices, swap(): lax.ppermute(x, axis, [(i, i ^ bits) for i in range(lax.axis_size(axis))])  75.9 us
    ppermute x32, starting transfers between devices, swap(): lax.ppermute(x, axis, [(i, i ^ bits) for i in range(lax.axis_size(axis))])  46.8 us
    all_to_all x1, blocking collectives, step(): lax.all_to_all(head_weight, 'dp', split_axis=1, concat_axis=0, axis_index...  25 us
    pallas_call x2, Pallas kernels, teacher_lists(): pl.pallas_call(probs_kernel, grid_spec=pltpu.PrefetchScalarGridSpec(num_s...  7.5 us
    pallas_call x2, Pallas kernels, mapped_parts(): pl.pallas_call(functools.partial(mapped_kernel, pieces), grid_spec=pltpu....  6.69 us
    pallas_call x1, Pallas kernels, logits_parts(): pl.pallas_call(logits_kernel, grid_spec=pltpu.PrefetchScalarGridSpec(num_...  6.29 us
    pallas_call x1, Pallas kernels, grads(): pl.pallas_call(grads_kernel, grid_spec=pltpu.PrefetchScalarGridSpec(num_s...  6.17 us
    dot_general x2, matrix products, head_half(): lax.dot_general(x, dl, (((0,), (0,)), ((), ())), preferred_element_type=F32)  5.61 us
  transfers between devices with their start and end apart: 33, of which 13 were waited for; matrix products, arithmetic and copies ran while one was open for 5% of the time, Pallas kernels for 12%

profile of v4, /device:TPU:0, one launch (start us, length us, event | category | flops | bytes accessed | tf_op | source)
XLA Modules:
  0.0 206.5 jit_solution(2833446258887217768)
XLA Ops:
  0.8 0.8 copy.126
  2.6 1.3 fusion.58
  4.6 201.9 %conditional.1 = (bf16[128,384]{1,0:T(8,128)(2,1)}, bf16[192,4096]{1,0:T(8,128)(2,1)}) conditional(s32[]{:T(128)} %convert_element_type.87, (bf16[128,1536]{1,0:T(8,128)(2,1)}, bf16[192,4096]{1,0:T(8,128)(2,1)}, s32[6,64]{1,0:T(8,128)S(1)}, f32[128,5120]{1,0:T(8,128)}, s32[128,2]{0,1:T(2,128)}, /*index=5*/bf16[32,2,128,128]{3,2,1,0:T(8,128)(2,1)}, ...), branch_computations={%region_4.8_spmd, %region_8.12_spmd} | conditional | flops 1643101440 | bytes 113335072 | solution.py:245
  4.8 1.5 copy.139
  6.4 25.0 %all_to_all.61 = bf16[192,4,1024]{2,0,1:T(8,128)(2,1)} all-to-all(bf16[192,4,1024]{2,0,1:T(8,128)(2,1)S(1)} %bitcast.133), channel_id=1, replica_groups={{0,8,16,24},{4,12,20,28},{1,9,17,25},{5,13,21,29},{2,10,18,26},{6,14,22..., dimensions={1} | all-to-all | bytes 3145728 | tf_op jit(solution)/shard_map/cond/branch_1_fun/all_to_all | solution.py:271
  31.4 1.3 convert_reduce_fusion.1
  32.6 3.6 %collective-permute-start.38 = (f32[64,128]{1,0:T(8,128)}, f32[64,128]{1,0:T(8,128)}, u32[]{:S(2)}, u32[]{:S(2)}) collective-permute-start(f32[64,128]{1,0:T(8,128)} %bitcast.44), channel_id=1, source_target_pairs={{0,3},{1,2},{2,1},{3,0},{4,7},{5,6},{6,5},{7,4},{8,11},{9,10},{10,... | collective-permute-start | bytes 98312 | tf_op jit(solution)/shard_map/cond/branch_1_fun/ppermute | solution.py:23
  36.2 0.8 collective-permute-start.36
  37.5 1.0 collective-permute-start.34
  38.8 3.7 %probs.7 = (bf16[40,64,128]{2,1,0:T(8,128)(2,1)}, bf16[32,64,128]{2,1,0:T(8,128)(2,1)}, bf16[22,64,128]{2,1,0:T(8,128)(2,1)}, bf16[22,64,128]{2,1,0:T(8,128)(2,1)}) custom-call(s32[6,64]{1,0:T(8,128)S(1)} %get-tuple-element.64.tab_ref, f32[128,5120]{1,0:T(8,128)} %get-tuple-element.111.x_ref), custom_call_target="tpu_custom_call" | custom-call | tf_op jit(solution)/shard_map/cond/branch_1_fun/probs/pallas_call | solution.py:52
  42.5 3.8 %probs.6 = (bf16[40,64,128]{2,1,0:T(8,128)(2,1)}, bf16[32,64,128]{2,1,0:T(8,128)(2,1)}, bf16[22,64,128]{2,1,0:T(8,128)(2,1)}, bf16[22,64,128]{2,1,0:T(8,128)(2,1)}) custom-call(s32[6,64]{1,0:T(8,128)S(1)} %get-tuple-element.64.tab_ref, f32[128,5120]{1,0:T(8,128)} %get-tuple-element.111.x_ref), custom_call_target="tpu_custom_call" | custom-call | tf_op jit(solution)/shard_map/cond/branch_1_fun/probs/pallas_call | solution.py:52
  46.3 0.6 collective-permute-start.33
  46.9 2.0 collective-permute-start.32
  48.9 1.2 collective-permute-start.51
  50.1 1.0 fusion.32
  51.2 1.5 multiply_reduce_fusion.3
  52.6 3.0 %collective-permute-start.52 = (bf16[22,64,128]{2,1,0:T(8,128)(2,1)}, bf16[22,64,128]{2,1,0:T(8,128)(2,1)S(1)}, u32[]{:S(2)}, u32[]{:S(2)}) collective-permute-start(bf16[22,64,128]{2,1,0:T(8,128)(2,1)} %get-tuple-element.81), channel_id=1, source_target_pairs={{0,2},{1,3},{2,0},{3,1},{4,6},{5,7},{6,4},{7,5},{8,10},{9,11},{10,... | collective-permute-start | bytes 1081352 | tf_op jit(solution)/shard_map/cond/branch_1_fun/ppermute | solution.py:23
  55.6 9.6 %collective-permute-done.33 = bf16[2,128,768]{2,1,0:T(8,128)(2,1)S(1)} collective-permute-done((bf16[2,128,768]{2,1,0:T(8,128)(2,1)S(1)}, bf16[2,128,768]{2,1,0:T(8,128)(2,1)S(1)}, u32[]{:S(2)}, u32[]{:S(2)}) %collective-permute-start.33) | collective-permute-done | bytes 393248 | tf_op jit(solution)/shard_map/cond/branch_1_fun/ppermute | solution.py:23
  65.2 3.5 %collective-permute-start.53 = (bf16[22,64,128]{2,1,0:T(8,128)(2,1)}, bf16[22,64,128]{2,1,0:T(8,128)(2,1)}, u32[]{:S(2)}, u32[]{:S(2)}) collective-permute-start(bf16[22,64,128]{2,1,0:T(8,128)(2,1)} %get-tuple-element.82), channel_id=1, source_target_pairs={{0,3},{1,2},{2,1},{3,0},{4,7},{5,6},{6,5},{7,4},{8,11},{9,10},{10,... | collective-permute-start | bytes 1081352 | tf_op jit(solution)/shard_map/cond/branch_1_fun/ppermute | solution.py:23
  68.8 1.2 pad_maximum_fusion.3.x_ref
  70.1 6.3 %logits.3 = (f32[4,128,1024]{2,1,0:T(8,128)}, f32[2,4,128]{2,1,0:T(4,128)}) custom-call(s32[1]{0:T(128)} %bitcast.31.core_ref, bf16[2,512,768]{2,1,0:T(8,128)(2,1)} %pad_maximum_fusion.3.x_ref, bf16[768,1024]{1,0:T(8,128)(2,1)} %bitcast.36.own_ref, bf16[768,1024]{1,0:T(8,128)(2,1)} %collective-permute-done.35.other_ref), custom_call_target="tpu_custom_call" | custom-call | tf_op jit(solution)/shard_map/cond/branch_1_fun/logits/pallas_call | solution.py:131
  76.4 0.7 pad_maximum_fusion.4
  77.3 0.6 collective-permute-start.40
  77.9 3.5 %collective-permute-start.39 = (f32[9,128]{1,0:T(8,128)S(1)}, f32[9,128]{1,0:T(8,128)S(1)}, u32[]{:S(2)}, u32[]{:S(2)}) collective-permute-start(f32[9,128]{1,0:T(8,128)S(1)} %pad_maximum_fusion.4), channel_id=1, source_target_pairs={{0,1},{1,0},{2,3},{3,2},{4,5},{5,4},{6,7},{7,6},{8,9},{9,8},{10,11... | collective-permute-start | bytes 13832 | tf_op jit(solution)/shard_map/cond/branch_1_fun/ppermute | solution.py:23
  81.4 6.8 %collective-permute-start.46 = (bf16[22,64,128]{2,1,0:T(8,128)(2,1)}, bf16[22,64,128]{2,1,0:T(8,128)(2,1)S(1)}, u32[]{:S(2)}, u32[]{:S(2)}) collective-permute-start(bf16[22,64,128]{2,1,0:T(8,128)(2,1)} %get-tuple-element.74), channel_id=1, source_target_pairs={{0,2},{1,3},{2,0},{3,1},{4,6},{5,7},{6,4},{7,5},{8,10},{9,11},{10,... | collective-permute-start | bytes 1081352 | tf_op jit(solution)/shard_map/cond/branch_1_fun/ppermute | solution.py:23
  88.3 2.0 collective-permute-start.47
  90.3 3.3 %mapped.7 = (bf16[64,1024]{1,0:T(8,128)(2,1)}, bf16[64,1024]{1,0:T(8,128)(2,1)}, bf16[64,1024]{1,0:T(8,128)(2,1)}, bf16[64,1024]{1,0:T(8,128)(2,1)}) custom-call(s32[6,64]{1,0:T(8,128)S(1)} %get-tuple-element.64.tab_ref, bf16[40,64,128]{2,1,0:T(8,128)(2,1)} %get-tuple-element.69.refs_0_, bf16[32,64,128]{2,1,0:T(8,128)(2,1)} %collective-permute-done.51.refs_1_, ...), custom_call_target="tpu_custom_call" | custom-call | tf_op jit(solution)/shard_map/cond/branch_1_fun/mapped/pallas_call | solution.py:96
  93.7 1.0 collective-permute-start.54
  94.8 2.1 %collective-permute-start.44 = (f32[10,128]{1,0:T(8,128)S(1)}, f32[10,128]{1,0:T(8,128)S(1)}, u32[]{:S(2)}, u32[]{:S(2)}) collective-permute-start(f32[10,128]{1,0:T(8,128)S(1)} %pad_maximum_fusion.5.refs_0_), channel_id=1, source_target_pairs={{0,24},{4,28},{8,16},{12,20},{16,8},{20,12},{24,0},{28,4},{1,25},{... | collective-permute-start | bytes 15368 | tf_op jit(solution)/shard_map/cond/branch_1_fun/ppermute | solution.py:23
  96.9 16.3 %collective-permute-done.46.refs_2_ = bf16[22,64,128]{2,1,0:T(8,128)(2,1)S(1)} collective-permute-done((bf16[22,64,128]{2,1,0:T(8,128)(2,1)}, bf16[22,64,128]{2,1,0:T(8,128)(2,1)S(1)}, u32[]{:S(2)}, u32[]{:S(2)}) %collective-permute-start.46) | collective-permute-done | bytes 360480 | tf_op jit(solution)/shard_map/cond/branch_1_fun/ppermute | solution.py:23
  113.2 0.9 collective-permute-start.43
  114.1 0.6 collective-permute-start.42
  114.7 5.9 %collective-permute-done.45.refs_1_ = bf16[32,64,128]{2,1,0:T(8,128)(2,1)S(1)} collective-permute-done((bf16[32,64,128]{2,1,0:T(8,128)(2,1)}, bf16[32,64,128]{2,1,0:T(8,128)(2,1)S(1)}, u32[]{:S(2)}, u32[]{:S(2)}) %collective-permute-start.45) | collective-permute-done | bytes 524320 | tf_op jit(solution)/shard_map/cond/branch_1_fun/ppermute | solution.py:23
  120.6 0.9 collective-permute-start.55
  121.5 3.4 %mapped.6 = (bf16[64,1024]{1,0:T(8,128)(2,1)}, bf16[64,1024]{1,0:T(8,128)(2,1)}, bf16[64,1024]{1,0:T(8,128)(2,1)}, bf16[64,1024]{1,0:T(8,128)(2,1)}) custom-call(s32[6,64]{1,0:T(8,128)S(1)} %get-tuple-element.64.tab_ref, bf16[40,64,128]{2,1,0:T(8,128)(2,1)} %get-tuple-element.66.refs_0_, bf16[32,64,128]{2,1,0:T(8,128)(2,1)} %copy-done.10, ...), custom_call_target="tpu_custom_call" | custom-call | tf_op jit(solution)/shard_map/cond/branch_1_fun/mapped/pallas_call | solution.py:96
  124.9 0.9 collective-permute-start.56
  125.7 1.8 collective-permute-start.48
  127.5 0.9 collective-permute-start.49
  128.4 0.8 collective-permute-start.50
  129.3 1.8 stats.3
  131.0 0.5 collective-permute-done.56.refs_6_
  131.5 2.1 %collective-permute-done.48.refs_0_ = bf16[64,1024]{1,0:T(8,128)(2,1)S(1)} collective-permute-done((bf16[64,1024]{1,0:T(8,128)(2,1)}, bf16[64,1024]{1,0:T(8,128)(2,1)S(1)}, u32[]{:S(2)}, u32[]{:S(2)}) %collective-permute-start.48) | collective-permute-done | bytes 131104 | tf_op jit(solution)/shard_map/cond/branch_1_fun/ppermute | solution.py:23
  133.6 0.5 collective-permute-done.49.refs_1_
  134.1 0.5 collective-permute-done.50.refs_2_
  134.8 0.5 copy-done.26
  135.3 6.2 %grads.3 = (bf16[4,128,1024]{2,1,0:T(8,128)(2,1)}, bf16[2,128,768]{2,1,0:T(8,128)(2,1)}, bf16[2,128,768]{2,1,0:T(8,128)(2,1)}, bf16[2,128,768]{2,1,0:T(8,128)(2,1)}, bf16[2,128,768]{2,1,0:T(8,128)(2,1)}) custom-call(s32[1]{0:T(128)} %bitcast.31.core_ref, f32[4,128,1024]{2,1,0:T(8,128)} %get-tuple-element.62.e_ref, f32[4,128,1]{2,1,0:T(8,128)} %get-tuple-element.71.a_ref, ...), custom_call_target="tpu_custom_call" | custom-call | tf_op jit(solution)/shard_map/cond/branch_1_fun/grads/pallas_call | solution.py:183
  141.4 3.4 %convolution_convert_fusion.2 = bf16[768,1024]{1,0:T(8,128)(2,1)} fusion(bf16[512,1024]{1,0:T(8,128)(2,1)} %bitcast.162, bf16[2,512,768]{2,1,0:T(8,128)(2,1)S(1)} %copy-done.3, s32[]{:T(128)S(6)} %select_n.91), kind=kOutput, calls=%fused_computation.61 | convolution fusion | flops 806092800 | bytes 3407876 | tf_op jit(solution)/shard_map/cond/branch_1_fun/dot_general | solution.py:329
  144.8 2.2 %convolution_convert_fusion.3 = bf16[768,1024]{1,0:T(8,128)(2,1)S(1)} fusion(bf16[512,1024]{1,0:T(8,128)(2,1)} %bitcast.163, bf16[2,512,768]{2,1,0:T(8,128)(2,1)S(1)} %copy-done.3, s32[]{:T(128)S(6)} %select_n.90), kind=kOutput, calls=%fused_computation.62 | convolution fusion | flops 806092800 | bytes 3407876 | tf_op jit(solution)/shard_map/cond/branch_1_fun/dot_general | solution.py:329
  147.0 1.4 collective-permute-done.63
  148.4 1.8 add_convert_fusion.2
  150.3 3.7 %all-to-all-start.3 = ((bf16[4,192,1024]{2,1,0:T(8,128)(2,1)}), bf16[4,192,1024]{2,1,0:T(8,128)(2,1)S(1)}, u32[]{:S(2)}, u32[]{:S(2)}) async-start(bf16[4,192,1024]{2,1,0:T(8,128)(2,1)} %bitcast.60), calls=%async_computation.3 | async-start | bytes 3145728 | tf_op jit(solution)/shard_map/cond/branch_1_fun/all_to_all | solution.py:335
  154.0 2.9 %collective-permute-start.57 = (bf16[2,128,768]{2,1,0:T(8,128)(2,1)S(1)}, bf16[2,128,768]{2,1,0:T(8,128)(2,1)S(1)}, u32[]{:S(2)}, u32[]{:S(2)}) collective-permute-start(bf16[2,128,768]{2,1,0:T(8,128)(2,1)S(1)} %copy-done.52), channel_id=1, source_target_pairs={{0,24},{4,28},{8,16},{12,20},{16,8},{20,12},{24,0},{28,4},{1,25},{... | collective-permute-start | bytes 1179656 | tf_op jit(solution)/shard_map/cond/branch_1_fun/ppermute | solution.py:23
  156.9 0.6 collective-permute-start.58
  157.6 26.4 %collective-permute-done.57 = bf16[2,128,768]{2,1,0:T(8,128)(2,1)S(1)} collective-permute-done((bf16[2,128,768]{2,1,0:T(8,128)(2,1)S(1)}, bf16[2,128,768]{2,1,0:T(8,128)(2,1)S(1)}, u32[]{:S(2)}, u32[]{:S(2)}) %collective-permute-start.57) | collective-permute-done | bytes 393248 | tf_op jit(solution)/shard_map/cond/branch_1_fun/ppermute | solution.py:23
  184.0 6.6 %collective-permute-done.58 = bf16[2,128,768]{2,1,0:T(8,128)(2,1)S(1)} collective-permute-done((bf16[2,128,768]{2,1,0:T(8,128)(2,1)S(1)}, bf16[2,128,768]{2,1,0:T(8,128)(2,1)S(1)}, u32[]{:S(2)}, u32[]{:S(2)}) %collective-permute-start.58) | collective-permute-done | bytes 393248 | tf_op jit(solution)/shard_map/cond/branch_1_fun/ppermute | solution.py:23
  191.6 1.3 collective-permute-start.60
  192.9 1.3 collective-permute-start.61
  194.2 1.8 collective-permute-start.62
  196.0 0.8 copy.121
  196.8 0.4 collective-permute-done.60.refs_1_
  197.2 5.6 %collective-permute-done.61.refs_2_ = bf16[128,384]{1,0:T(8,128)(2,1)S(1)} collective-permute-done((bf16[128,384]{1,0:T(8,128)(2,1)S(1)}, bf16[128,384]{1,0:T(8,128)(2,1)S(1)}, u32[]{:S(2)}, u32[]{:S(2)}) %collective-permute-start.61) | collective-permute-done | bytes 98336 | tf_op jit(solution)/shard_map/cond/branch_1_fun/ppermute | solution.py:23
  202.8 0.6 copy-done.30
  203.5 1.7 hidden_sum.3
  205.2 1.3 copy.135
  (114 shorter events, 3.7 us)
Async XLA Ops:
  6.4 25.0 %copy-start.1 = (bf16[32,2,128,128]{3,2,1,0:T(8,128)(2,1)S(1)}, bf16[32,2,128,128]{3,2,1,0:T(8,128)(2,1)}, u32[]{:S(2)}) copy-start(bf16[32,2,128,128]{3,2,1,0:T(8,128)(2,1)} %get-tuple-element.113.refs_4_) | copy-start | bytes 6291460 | tf_op jit(solution)/shard_map/cond
  31.4 5.7 %copy-start.7 = (bf16[128,1536]{1,0:T(8,128)(2,1)S(1)}, bf16[128,1536]{1,0:T(8,128)(2,1)}, u32[]{:S(2)}) copy-start(bf16[128,1536]{1,0:T(8,128)(2,1)} %get-tuple-element.165) | copy-start | bytes 1179652 | tf_op jit(solution)/shard_map/cond
  31.4 38.7 %collective-permute-start.35 = (bf16[768,1024]{1,0:T(8,128)(2,1)}, bf16[768,1024]{1,0:T(8,128)(2,1)}, u32[]{:S(2)}, u32[]{:S(2)}) collective-permute-start(bf16[768,1024]{1,0:T(8,128)(2,1)} %bitcast.36.own_ref), channel_id=1, source_target_pairs={{0,4},{4,0},{8,12},{12,8},{16,20},{20,16},{24,28},{28,24},{1,5},{5... | collective-permute-start | bytes 4718600 | tf_op jit(solution)/shard_map/cond/branch_1_fun/ppermute | solution.py:23
  32.6 5.8 %copy-start.38 = (s32[128,2]{0,1:T(2,128)S(1)}, s32[128,2]{0,1:T(2,128)}, u32[]{:S(2)}) copy-start(s32[128,2]{0,1:T(2,128)} %get-tuple-element.169) | copy-start | bytes 3076 | tf_op jit(solution)/shard_map/cond
  32.6 13.7 %collective-permute-start.38 = (f32[64,128]{1,0:T(8,128)}, f32[64,128]{1,0:T(8,128)}, u32[]{:S(2)}, u32[]{:S(2)}) collective-permute-start(f32[64,128]{1,0:T(8,128)} %bitcast.44), channel_id=1, source_target_pairs={{0,3},{1,2},{2,1},{3,0},{4,7},{5,6},{6,5},{7,4},{8,11},{9,10},{10,... | collective-permute-start | bytes 98312 | tf_op jit(solution)/shard_map/cond/branch_1_fun/ppermute | solution.py:23
  36.2 10.6 %collective-permute-start.37 = (f32[64,128]{1,0:T(8,128)}, f32[64,128]{1,0:T(8,128)}, u32[]{:S(2)}, u32[]{:S(2)}) collective-permute-start(f32[64,128]{1,0:T(8,128)} %bitcast.44), channel_id=1, source_target_pairs={{0,2},{1,3},{2,0},{3,1},{4,6},{5,7},{6,4},{7,5},{8,10},{9,11},{10,... | collective-permute-start | bytes 98312 | tf_op jit(solution)/shard_map/cond/branch_1_fun/ppermute | solution.py:23
  36.2 12.6 %collective-permute-start.36 = (f32[64,128]{1,0:T(8,128)}, f32[64,128]{1,0:T(8,128)}, u32[]{:S(2)}, u32[]{:S(2)}) collective-permute-start(f32[64,128]{1,0:T(8,128)} %bitcast.44), channel_id=1, source_target_pairs={{0,1},{1,0},{2,3},{3,2},{4,5},{5,4},{6,7},{7,6},{8,9},{9,8},{10,11... | collective-permute-start | bytes 98312 | tf_op jit(solution)/shard_map/cond/branch_1_fun/ppermute | solution.py:23
  37.5 15.1 %collective-permute-start.34 = (bf16[2,128,768]{2,1,0:T(8,128)(2,1)S(1)}, bf16[2,128,768]{2,1,0:T(8,128)(2,1)S(1)}, u32[]{:S(2)}, u32[]{:S(2)}) collective-permute-start(bf16[2,128,768]{2,1,0:T(8,128)(2,1)S(1)} %copy.114), channel_id=1, source_target_pairs={{0,8},{4,12},{8,0},{12,4},{16,24},{20,28},{24,16},{28,20},{1,9},{5... | collective-permute-start | bytes 1179656 | tf_op jit(solution)/shard_map/cond/branch_1_fun/ppermute | solution.py:23
  42.5 8.6 %copy-start.4 = (bf16[40,64,128]{2,1,0:T(8,128)(2,1)S(1)}, bf16[40,64,128]{2,1,0:T(8,128)(2,1)}, u32[]{:S(2)}) copy-start(bf16[40,64,128]{2,1,0:T(8,128)(2,1)} %get-tuple-element.69.refs_0_) | copy-start | bytes 1966084 | tf_op jit(solution)/shard_map/cond
  46.3 18.9 %collective-permute-start.33 = (bf16[2,128,768]{2,1,0:T(8,128)(2,1)S(1)}, bf16[2,128,768]{2,1,0:T(8,128)(2,1)S(1)}, u32[]{:S(2)}, u32[]{:S(2)}) collective-permute-start(bf16[2,128,768]{2,1,0:T(8,128)(2,1)S(1)} %copy.114), channel_id=1, source_target_pairs={{0,16},{4,20},{8,24},{12,28},{16,0},{20,4},{24,8},{28,12},{1,17},{... | collective-permute-start | bytes 1179656 | tf_op jit(solution)/shard_map/cond/branch_1_fun/ppermute | solution.py:23
  46.9 21.9 %collective-permute-start.32 = (bf16[2,128,768]{2,1,0:T(8,128)(2,1)S(1)}, bf16[2,128,768]{2,1,0:T(8,128)(2,1)S(1)}, u32[]{:S(2)}, u32[]{:S(2)}) collective-permute-start(bf16[2,128,768]{2,1,0:T(8,128)(2,1)S(1)} %copy.114), channel_id=1, source_target_pairs={{0,24},{4,28},{8,16},{12,20},{16,8},{20,12},{24,0},{28,4},{1,25},{... | collective-permute-start | bytes 1179656 | tf_op jit(solution)/shard_map/cond/branch_1_fun/ppermute | solution.py:23
  48.9 39.4 %collective-permute-start.51 = (bf16[32,64,128]{2,1,0:T(8,128)(2,1)}, bf16[32,64,128]{2,1,0:T(8,128)(2,1)}, u32[]{:S(2)}, u32[]{:S(2)}) collective-permute-start(bf16[32,64,128]{2,1,0:T(8,128)(2,1)} %get-tuple-element.80), channel_id=1, source_target_pairs={{0,1},{1,0},{2,3},{3,2},{4,5},{5,4},{6,7},{7,6},{8,9},{9,8},{10,11... | collective-permute-start | bytes 1572872 | tf_op jit(solution)/shard_map/cond/branch_1_fun/ppermute | solution.py:23
  52.6 25.3 %collective-permute-start.52 = (bf16[22,64,128]{2,1,0:T(8,128)(2,1)}, bf16[22,64,128]{2,1,0:T(8,128)(2,1)S(1)}, u32[]{:S(2)}, u32[]{:S(2)}) collective-permute-start(bf16[22,64,128]{2,1,0:T(8,128)(2,1)} %get-tuple-element.81), channel_id=1, source_target_pairs={{0,2},{1,3},{2,0},{3,1},{4,6},{5,7},{6,4},{7,5},{8,10},{9,11},{10,... | collective-permute-start | bytes 1081352 | tf_op jit(solution)/shard_map/cond/branch_1_fun/ppermute | solution.py:23
  65.2 16.2 %collective-permute-start.53 = (bf16[22,64,128]{2,1,0:T(8,128)(2,1)}, bf16[22,64,128]{2,1,0:T(8,128)(2,1)}, u32[]{:S(2)}, u32[]{:S(2)}) collective-permute-start(bf16[22,64,128]{2,1,0:T(8,128)(2,1)} %get-tuple-element.82), channel_id=1, source_target_pairs={{0,3},{1,2},{2,1},{3,0},{4,7},{5,6},{6,5},{7,4},{8,11},{9,10},{10,... | collective-permute-start | bytes 1081352 | tf_op jit(solution)/shard_map/cond/branch_1_fun/ppermute | solution.py:23
  77.0 16.6 %collective-permute-start.41 = (f32[9,128]{1,0:T(8,128)S(1)}, f32[9,128]{1,0:T(8,128)S(1)}, u32[]{:S(2)}, u32[]{:S(2)}) collective-permute-start(f32[9,128]{1,0:T(8,128)S(1)} %pad_maximum_fusion.4), channel_id=1, source_target_pairs={{0,3},{1,2},{2,1},{3,0},{4,7},{5,6},{6,5},{7,4},{8,11},{9,10},{10,... | collective-permute-start | bytes 13832 | tf_op jit(solution)/shard_map/cond/branch_1_fun/ppermute | solution.py:23
  77.3 16.4 %collective-permute-start.40 = (f32[9,128]{1,0:T(8,128)S(1)}, f32[9,128]{1,0:T(8,128)S(1)}, u32[]{:S(2)}, u32[]{:S(2)}) collective-permute-start(f32[9,128]{1,0:T(8,128)S(1)} %pad_maximum_fusion.4), channel_id=1, source_target_pairs={{0,2},{1,3},{2,0},{3,1},{4,6},{5,7},{6,4},{7,5},{8,10},{9,11},{10,... | collective-permute-start | bytes 13832 | tf_op jit(solution)/shard_map/cond/branch_1_fun/ppermute | solution.py:23
  77.9 12.4 %copy-start.15 = (bf16[22,64,128]{2,1,0:T(8,128)(2,1)}, bf16[22,64,128]{2,1,0:T(8,128)(2,1)S(1)}, u32[]{:S(2)}) copy-start(bf16[22,64,128]{2,1,0:T(8,128)(2,1)S(1)} %collective-permute-done.52.refs_2_) | copy-start | bytes 1081348 | tf_op jit(solution)/shard_map/cond
  77.9 16.8 %collective-permute-start.39 = (f32[9,128]{1,0:T(8,128)S(1)}, f32[9,128]{1,0:T(8,128)S(1)}, u32[]{:S(2)}, u32[]{:S(2)}) collective-permute-start(f32[9,128]{1,0:T(8,128)S(1)} %pad_maximum_fusion.4), channel_id=1, source_target_pairs={{0,1},{1,0},{2,3},{3,2},{4,5},{5,4},{6,7},{7,6},{8,9},{9,8},{10,11... | collective-permute-start | bytes 13832 | tf_op jit(solution)/shard_map/cond/branch_1_fun/ppermute | solution.py:23
  81.4 31.8 %collective-permute-start.46 = (bf16[22,64,128]{2,1,0:T(8,128)(2,1)}, bf16[22,64,128]{2,1,0:T(8,128)(2,1)S(1)}, u32[]{:S(2)}, u32[]{:S(2)}) collective-permute-start(bf16[22,64,128]{2,1,0:T(8,128)(2,1)} %get-tuple-element.74), channel_id=1, source_target_pairs={{0,2},{1,3},{2,0},{3,1},{4,6},{5,7},{6,4},{7,5},{8,10},{9,11},{10,... | collective-permute-start | bytes 1081352 | tf_op jit(solution)/shard_map/cond/branch_1_fun/ppermute | solution.py:23
  88.3 6.4 %copy-start.34 = (f32[2,4,128]{2,1,0:T(4,128)S(1)}, f32[2,4,128]{2,1,0:T(4,128)}, u32[]{:S(2)}) copy-start(f32[2,4,128]{2,1,0:T(4,128)} %get-tuple-element.63.own_ref) | copy-start | bytes 12292 | tf_op jit(solution)/shard_map/cond
  88.3 6.5 %copy-start.46 = (f32[128]{0:T(128)S(1)}, f32[128]{0:T(128)}, u32[]{:S(2)}) copy-start(f32[128]{0:T(128)} %get-tuple-element.115) | copy-start | bytes 1540 | tf_op jit(solution)/shard_map/cond
  88.3 25.9 %collective-permute-start.47 = (bf16[22,64,128]{2,1,0:T(8,128)(2,1)}, bf16[22,64,128]{2,1,0:T(8,128)(2,1)S(1)}, u32[]{:S(2)}, u32[]{:S(2)}) collective-permute-start(bf16[22,64,128]{2,1,0:T(8,128)(2,1)} %get-tuple-element.75), channel_id=1, source_target_pairs={{0,3},{1,2},{2,1},{3,0},{4,7},{5,6},{6,5},{7,4},{8,11},{9,10},{10,... | collective-permute-start | bytes 1081352 | tf_op jit(solution)/shard_map/cond/branch_1_fun/ppermute | solution.py:23
  93.6 26.9 %collective-permute-start.45 = (bf16[32,64,128]{2,1,0:T(8,128)(2,1)}, bf16[32,64,128]{2,1,0:T(8,128)(2,1)S(1)}, u32[]{:S(2)}, u32[]{:S(2)}) collective-permute-start(bf16[32,64,128]{2,1,0:T(8,128)(2,1)} %get-tuple-element.73), channel_id=1, source_target_pairs={{0,1},{1,0},{2,3},{3,2},{4,5},{5,4},{6,7},{7,6},{8,9},{9,8},{10,11... | collective-permute-start | bytes 1572872 | tf_op jit(solution)/shard_map/cond/branch_1_fun/ppermute | solution.py:23
  93.7 31.1 %collective-permute-start.54 = (bf16[64,1024]{1,0:T(8,128)(2,1)}, bf16[64,1024]{1,0:T(8,128)(2,1)S(1)}, u32[]{:S(2)}, u32[]{:S(2)}) collective-permute-start(bf16[64,1024]{1,0:T(8,128)(2,1)} %get-tuple-element.83), channel_id=1, source_target_pairs={{0,24},{4,28},{8,16},{12,20},{16,8},{20,12},{24,0},{28,4},{1,25},{... | collective-permute-start | bytes 393224 | tf_op jit(solution)/shard_map/cond/branch_1_fun/ppermute | solution.py:23
  94.8 34.4 %copy-start.36 = (f32[10,128]{1,0:T(8,128)}, f32[10,128]{1,0:T(8,128)S(1)}, u32[]{:S(2)}) copy-start(f32[10,128]{1,0:T(8,128)S(1)} %pad_maximum_fusion.5.refs_0_) | copy-start | bytes 15364 | tf_op jit(solution)/shard_map/cond
  94.8 30.9 %collective-permute-start.44 = (f32[10,128]{1,0:T(8,128)S(1)}, f32[10,128]{1,0:T(8,128)S(1)}, u32[]{:S(2)}, u32[]{:S(2)}) collective-permute-start(f32[10,128]{1,0:T(8,128)S(1)} %pad_maximum_fusion.5.refs_0_), channel_id=1, source_target_pairs={{0,24},{4,28},{8,16},{12,20},{16,8},{20,12},{24,0},{28,4},{1,25},{... | collective-permute-start | bytes 15368 | tf_op jit(solution)/shard_map/cond/branch_1_fun/ppermute | solution.py:23
  113.2 8.3 %copy-start.13 = (bf16[22,64,128]{2,1,0:T(8,128)(2,1)}, bf16[22,64,128]{2,1,0:T(8,128)(2,1)S(1)}, u32[]{:S(2)}) copy-start(bf16[22,64,128]{2,1,0:T(8,128)(2,1)S(1)} %collective-permute-done.46.refs_2_) | copy-start | bytes 1081348 | tf_op jit(solution)/shard_map/cond
  113.2 14.3 %collective-permute-start.43 = (f32[10,128]{1,0:T(8,128)S(1)}, f32[10,128]{1,0:T(8,128)S(1)}, u32[]{:S(2)}, u32[]{:S(2)}) collective-permute-start(f32[10,128]{1,0:T(8,128)S(1)} %pad_maximum_fusion.5.refs_0_), channel_id=1, source_target_pairs={{0,16},{4,20},{8,24},{12,28},{16,0},{20,4},{24,8},{28,12},{1,17},{... | collective-permute-start | bytes 15368 | tf_op jit(solution)/shard_map/cond/branch_1_fun/ppermute | solution.py:23
  114.1 7.3 %copy-start.14 = (bf16[22,64,128]{2,1,0:T(8,128)(2,1)}, bf16[22,64,128]{2,1,0:T(8,128)(2,1)S(1)}, u32[]{:S(2)}) copy-start(bf16[22,64,128]{2,1,0:T(8,128)(2,1)S(1)} %collective-permute-done.47.refs_3_) | copy-start | bytes 1081348 | tf_op jit(solution)/shard_map/cond
  114.1 14.3 %collective-permute-start.42 = (f32[10,128]{1,0:T(8,128)S(1)}, f32[10,128]{1,0:T(8,128)S(1)}, u32[]{:S(2)}, u32[]{:S(2)}) collective-permute-start(f32[10,128]{1,0:T(8,128)S(1)} %pad_maximum_fusion.5.refs_0_), channel_id=1, source_target_pairs={{0,8},{4,12},{8,0},{12,4},{16,24},{20,28},{24,16},{28,20},{1,9},{5... | collective-permute-start | bytes 15368 | tf_op jit(solution)/shard_map/cond/branch_1_fun/ppermute | solution.py:23
  120.6 0.9 copy-start.10
  120.6 10.5 %collective-permute-start.55 = (bf16[64,1024]{1,0:T(8,128)(2,1)}, bf16[64,1024]{1,0:T(8,128)(2,1)}, u32[]{:S(2)}, u32[]{:S(2)}) collective-permute-start(bf16[64,1024]{1,0:T(8,128)(2,1)} %get-tuple-element.84), channel_id=1, source_target_pairs={{0,16},{4,20},{8,24},{12,28},{16,0},{20,4},{24,8},{28,12},{1,17},{... | collective-permute-start | bytes 393224 | tf_op jit(solution)/shard_map/cond/branch_1_fun/ppermute | solution.py:23
  124.9 9.8 %copy-start.17 = (bf16[64,1024]{1,0:T(8,128)(2,1)}, bf16[64,1024]{1,0:T(8,128)(2,1)S(1)}, u32[]{:S(2)}) copy-start(bf16[64,1024]{1,0:T(8,128)(2,1)S(1)} %collective-permute-done.54.refs_4_) | copy-start | bytes 393220 | tf_op jit(solution)/shard_map/cond
  124.9 6.6 %collective-permute-start.56 = (bf16[64,1024]{1,0:T(8,128)(2,1)}, bf16[64,1024]{1,0:T(8,128)(2,1)S(1)}, u32[]{:S(2)}, u32[]{:S(2)}) collective-permute-start(bf16[64,1024]{1,0:T(8,128)(2,1)} %get-tuple-element.85), channel_id=1, source_target_pairs={{0,8},{4,12},{8,0},{12,4},{16,24},{20,28},{24,16},{28,20},{1,9},{5... | collective-permute-start | bytes 393224 | tf_op jit(solution)/shard_map/cond/branch_1_fun/ppermute | solution.py:23
  125.7 3.5 %copy-start.40 = (f32[10,128]{1,0:T(8,128)}, f32[10,128]{1,0:T(8,128)S(1)}, u32[]{:S(2)}) copy-start(f32[10,128]{1,0:T(8,128)S(1)} %collective-permute-done.44.refs_3_) | copy-start | bytes 15364 | tf_op jit(solution)/shard_map/cond
  125.7 7.9 %collective-permute-start.48 = (bf16[64,1024]{1,0:T(8,128)(2,1)}, bf16[64,1024]{1,0:T(8,128)(2,1)S(1)}, u32[]{:S(2)}, u32[]{:S(2)}) collective-permute-start(bf16[64,1024]{1,0:T(8,128)(2,1)} %get-tuple-element.76), channel_id=1, source_target_pairs={{0,24},{4,28},{8,16},{12,20},{16,8},{20,12},{24,0},{28,4},{1,25},{... | collective-permute-start | bytes 393224 | tf_op jit(solution)/shard_map/cond/branch_1_fun/ppermute | solution.py:23
  127.5 1.7 copy-start.42
  127.5 6.6 %collective-permute-start.49 = (bf16[64,1024]{1,0:T(8,128)(2,1)}, bf16[64,1024]{1,0:T(8,128)(2,1)S(1)}, u32[]{:S(2)}, u32[]{:S(2)}) collective-permute-start(bf16[64,1024]{1,0:T(8,128)(2,1)} %get-tuple-element.77), channel_id=1, source_target_pairs={{0,16},{4,20},{8,24},{12,28},{16,0},{20,4},{24,8},{28,12},{1,17},{... | collective-permute-start | bytes 393224 | tf_op jit(solution)/shard_map/cond/branch_1_fun/ppermute | solution.py:23
  128.4 0.8 copy-start.44
  128.4 6.2 %collective-permute-start.50 = (bf16[64,1024]{1,0:T(8,128)(2,1)}, bf16[64,1024]{1,0:T(8,128)(2,1)S(1)}, u32[]{:S(2)}, u32[]{:S(2)}) collective-permute-start(bf16[64,1024]{1,0:T(8,128)(2,1)} %get-tuple-element.78), channel_id=1, source_target_pairs={{0,8},{4,12},{8,0},{12,4},{16,24},{20,28},{24,16},{28,20},{1,9},{5... | collective-permute-start | bytes 393224 | tf_op jit(solution)/shard_map/cond/branch_1_fun/ppermute | solution.py:23
  131.5 3.1 %copy-start.20 = (bf16[64,1024]{1,0:T(8,128)(2,1)}, bf16[64,1024]{1,0:T(8,128)(2,1)S(1)}, u32[]{:S(2)}) copy-start(bf16[64,1024]{1,0:T(8,128)(2,1)S(1)} %collective-permute-done.56.refs_6_) | copy-start | bytes 393220 | tf_op jit(solution)/shard_map/cond
  133.6 1.0 copy-start.22
  134.1 0.7 copy-start.24
  134.6 0.7 copy-start.26
  135.3 6.2 %copy-start.3 = (bf16[2,512,768]{2,1,0:T(8,128)(2,1)S(1)}, bf16[2,512,768]{2,1,0:T(8,128)(2,1)}, u32[]{:S(2)}) copy-start(bf16[2,512,768]{2,1,0:T(8,128)(2,1)} %pad_maximum_fusion.3.x_ref) | copy-start | bytes 4718596 | tf_op jit(solution)/shard_map/cond
  144.8 3.6 %collective-permute-start.63 = (bf16[768,1024]{1,0:T(8,128)(2,1)}, bf16[768,1024]{1,0:T(8,128)(2,1)S(1)}, u32[]{:S(2)}, u32[]{:S(2)}) collective-permute-start(bf16[768,1024]{1,0:T(8,128)(2,1)} %convolution_convert_fusion.2), channel_id=1, source_target_pairs={{0,4},{4,0},{8,12},{12,8},{16,20},{20,16},{24,28},{28,24},{1,5},{5... | collective-permute-start | bytes 4718600 | tf_op jit(solution)/shard_map/cond/branch_1_fun/ppermute | solution.py:23
  150.3 3.7 %copy-start.52 = (bf16[2,128,768]{2,1,0:T(8,128)(2,1)S(1)}, bf16[2,128,768]{2,1,0:T(8,128)(2,1)}, u32[]{:S(2)}) copy-start(bf16[2,128,768]{2,1,0:T(8,128)(2,1)} %get-tuple-element.88) | copy-start | bytes 1179652 | tf_op jit(solution)/shard_map/cond
  150.3 6.6 %copy-start.50 = (bf16[2,128,768]{2,1,0:T(8,128)(2,1)S(1)}, bf16[2,128,768]{2,1,0:T(8,128)(2,1)}, u32[]{:S(2)}) copy-start(bf16[2,128,768]{2,1,0:T(8,128)(2,1)} %get-tuple-element.89) | copy-start | bytes 1179652 | tf_op jit(solution)/shard_map/cond
  150.3 7.2 %copy-start.48 = (bf16[2,128,768]{2,1,0:T(8,128)(2,1)S(1)}, bf16[2,128,768]{2,1,0:T(8,128)(2,1)}, u32[]{:S(2)}) copy-start(bf16[2,128,768]{2,1,0:T(8,128)(2,1)} %get-tuple-element.90) | copy-start | bytes 1179652 | tf_op jit(solution)/shard_map/cond
  150.3 40.4 %copy-start.12 = (bf16[2,128,768]{2,1,0:T(8,128)(2,1)S(1)}, bf16[2,128,768]{2,1,0:T(8,128)(2,1)}, u32[]{:S(2)}) copy-start(bf16[2,128,768]{2,1,0:T(8,128)(2,1)} %get-tuple-element.87) | copy-start | bytes 1179652 | tf_op jit(solution)/shard_map/cond
  150.3 54.9 %all-to-all-start.3 = ((bf16[4,192,1024]{2,1,0:T(8,128)(2,1)}), bf16[4,192,1024]{2,1,0:T(8,128)(2,1)S(1)}, u32[]{:S(2)}, u32[]{:S(2)}) async-start(bf16[4,192,1024]{2,1,0:T(8,128)(2,1)} %bitcast.60), calls=%async_computation.3 | async-start | bytes 3145728 | tf_op jit(solution)/shard_map/cond/branch_1_fun/all_to_all | solution.py:335
  154.0 30.0 %collective-permute-start.57 = (bf16[2,128,768]{2,1,0:T(8,128)(2,1)S(1)}, bf16[2,128,768]{2,1,0:T(8,128)(2,1)S(1)}, u32[]{:S(2)}, u32[]{:S(2)}) collective-permute-start(bf16[2,128,768]{2,1,0:T(8,128)(2,1)S(1)} %copy-done.52), channel_id=1, source_target_pairs={{0,24},{4,28},{8,16},{12,20},{16,8},{20,12},{24,0},{28,4},{1,25},{... | collective-permute-start | bytes 1179656 | tf_op jit(solution)/shard_map/cond/branch_1_fun/ppermute | solution.py:23
  156.9 33.7 %collective-permute-start.58 = (bf16[2,128,768]{2,1,0:T(8,128)(2,1)S(1)}, bf16[2,128,768]{2,1,0:T(8,128)(2,1)S(1)}, u32[]{:S(2)}, u32[]{:S(2)}) collective-permute-start(bf16[2,128,768]{2,1,0:T(8,128)(2,1)S(1)} %copy-done.50), channel_id=1, source_target_pairs={{0,16},{4,20},{8,24},{12,28},{16,0},{20,4},{24,8},{28,12},{1,17},{... | collective-permute-start | bytes 1179656 | tf_op jit(solution)/shard_map/cond/branch_1_fun/ppermute | solution.py:23
  157.4 33.2 %collective-permute-start.59 = (bf16[2,128,768]{2,1,0:T(8,128)(2,1)S(1)}, bf16[2,128,768]{2,1,0:T(8,128)(2,1)S(1)}, u32[]{:S(2)}, u32[]{:S(2)}) collective-permute-start(bf16[2,128,768]{2,1,0:T(8,128)(2,1)S(1)} %copy-done.48), channel_id=1, source_target_pairs={{0,8},{4,12},{8,0},{12,4},{16,24},{20,28},{24,16},{28,20},{1,9},{5... | collective-permute-start | bytes 1179656 | tf_op jit(solution)/shard_map/cond/branch_1_fun/ppermute | solution.py:23
  191.6 5.6 %collective-permute-start.60 = (bf16[128,384]{1,0:T(8,128)(2,1)S(1)}, bf16[128,384]{1,0:T(8,128)(2,1)S(1)}, u32[]{:S(2)}, u32[]{:S(2)}) collective-permute-start(bf16[128,384]{1,0:T(8,128)(2,1)S(1)} %bitcast.151), channel_id=1, source_target_pairs={{0,1},{1,0},{2,3},{3,2},{4,5},{5,4},{6,7},{7,6},{8,9},{9,8},{10,11... | collective-permute-start | bytes 294920 | tf_op jit(solution)/shard_map/cond/branch_1_fun/ppermute | solution.py:23
  192.9 9.9 %collective-permute-start.61 = (bf16[128,384]{1,0:T(8,128)(2,1)S(1)}, bf16[128,384]{1,0:T(8,128)(2,1)S(1)}, u32[]{:S(2)}, u32[]{:S(2)}) collective-permute-start(bf16[128,384]{1,0:T(8,128)(2,1)S(1)} %bitcast.149), channel_id=1, source_target_pairs={{0,2},{1,3},{2,0},{3,1},{4,6},{5,7},{6,4},{7,5},{8,10},{9,11},{10,... | collective-permute-start | bytes 294920 | tf_op jit(solution)/shard_map/cond/branch_1_fun/ppermute | solution.py:23
  194.2 8.6 %collective-permute-start.62 = (bf16[128,384]{1,0:T(8,128)(2,1)S(1)}, bf16[128,384]{1,0:T(8,128)(2,1)S(1)}, u32[]{:S(2)}, u32[]{:S(2)}) collective-permute-start(bf16[128,384]{1,0:T(8,128)(2,1)S(1)} %bitcast.147), channel_id=1, source_target_pairs={{0,3},{1,2},{2,1},{3,0},{4,7},{5,6},{6,5},{7,4},{8,11},{9,10},{10,... | collective-permute-start | bytes 294920 | tf_op jit(solution)/shard_map/cond/branch_1_fun/ppermute | solution.py:23
  197.2 5.6 %copy-start.28 = (bf16[128,384]{1,0:T(8,128)(2,1)}, bf16[128,384]{1,0:T(8,128)(2,1)S(1)}, u32[]{:S(2)}) copy-start(bf16[128,384]{1,0:T(8,128)(2,1)S(1)} %collective-permute-done.60.refs_1_) | copy-start | bytes 294916 | tf_op jit(solution)/shard_map/cond
  202.8 0.6 copy-start.30
  202.8 0.7 copy-start.32
